TPU v7x, 32 devices: a whole 2x2x4 slice. The times are simulated.
32 devices in a mesh: seq: 2 (over y), row: 4 (over z), col: 4 (over x, core).
Axes of the slice: x: 2, y: 2, z: 4, core: 2. Of those that a mesh axis runs over, the one named last changes fastest.
Arguments:
- stream: bfloat16 [3072, 3072], P(('seq', 'row'), 'col'), may hold values from -6 to 6
- query_input: bfloat16 [3072, 3072], P(('seq', 'row'), 'col'), may hold values from -400 to 400
- key_input: bfloat16 [3072, 3072], P(('seq', 'row'), 'col'), may hold values from -400 to 400
- value_input: bfloat16 [3072, 3072], P(('seq', 'row'), 'col'), may hold values from -6 to 6
- q_gain: float32 [24, 128], P('col'), may hold values from 0.5 to 7
- k_gain: float32 [24, 128], P('col'), may hold values from 0.5 to 7
- out_weight: bfloat16 [3072, 3072], P('row', 'col'), may hold values from -0.109375 to 0.109375
- gate: float32 [3072], P('col'), may hold values from -4 to 4
Outputs:
- out: bfloat16 [3072, 3072], P(('seq', 'row'), 'col')
All inputs are finite; a program needn't handle non-finite values.
Results may differ from a plain program's by a relative error of at most 0.0057.
Values may be sent and summed in bfloat16 or wider, within the bound.
No kernel may reach another device: no remote copies, remote signals or barrier semaphores. Data moves between devices by JAX's collectives and lax.ppermute only.
A program may use at most 64 MiB of HBM per device.

v0:
```python
import math

import jax
import jax.numpy as jnp
from jax import lax
from jax.sharding import PartitionSpec as P

EPSILON = 1e-06
NEGATIVE_FLOOR = -1e30


def padded_2(block, sides, width):
    for axis, dim in sides:
        count = lax.axis_size(axis)
        forward = [(i, i + 1) for i in range(count - 1)]
        backward = [(target, source) for source, target in forward]
        low = lax.ppermute(
            lax.slice_in_dim(block, block.shape[dim] - width, None, axis=dim), axis, forward
        )
        high = lax.ppermute(lax.slice_in_dim(block, 0, width, axis=dim), axis, backward)
        block = jnp.concatenate([low, block, high], axis=dim)
    return block


def normalize(values, gain_table):
    token_count = values.shape[0]
    head_count, head_size = gain_table.shape
    split = values.astype(jnp.float32).reshape(token_count, head_count, head_size)
    mean_square = jnp.mean(split * split, axis=-1, keepdims=True)
    return (split * lax.rsqrt(mean_square + EPSILON) * gain_table).astype(jnp.bfloat16)


def layer_terms(queries, key_rows, value_rows, score_scale):
    scores = (
        jnp.einsum("qhd,khd->hqk", queries, key_rows, preferred_element_type=jnp.float32)
        * score_scale
    )
    layer_max = jnp.max(scores, axis=-1)
    unnormed = jnp.exp(scores - layer_max[..., None]).astype(jnp.bfloat16)
    layer_sum = jnp.sum(unnormed.astype(jnp.float32), axis=-1)
    weighted = jnp.einsum("hqk,khd->qhd", unnormed, value_rows, preferred_element_type=jnp.float32)
    return (layer_max, layer_sum, weighted)


def combine(maxima, layer_sums, weighted, presence):
    mask = presence[:, None, None]
    maxima = jnp.where(mask, maxima, NEGATIVE_FLOOR)
    layer_sums = jnp.where(mask, layer_sums, 0.0)
    overall = jnp.max(maxima, axis=0)
    factors = jnp.exp(maxima - overall)
    denominator = jnp.sum(factors * layer_sums, axis=0)
    numerator = jnp.sum(jnp.transpose(factors, (0, 2, 1))[..., None] * weighted, axis=0)
    return numerator / jnp.transpose(denominator)[..., None]


def body(stream, query_input, key_input, value_input, q_gain, k_gain, out_weight, gate):
    token_count, feature_count = query_input.shape
    head_count, head_size = q_gain.shape
    score_scale = 1.0 / math.sqrt(head_size)
    queries = normalize(query_input, q_gain)
    normed_keys = normalize(key_input, k_gain).reshape(token_count, feature_count)
    layered = jnp.stack([normed_keys, value_input], axis=0)[None, None]
    padded = padded_2(layered, (("seq", 0), ("row", 1)), 1)
    padded = padded.reshape(9, 2, token_count, feature_count)
    key_stack = padded[:, 0].reshape(9, token_count, head_count, head_size)
    value_stack = padded[:, 1].reshape(9, token_count, head_count, head_size)
    time_index = lax.axis_index("seq")
    time_count = lax.axis_size("seq")
    height_index = lax.axis_index("row")
    height_count = lax.axis_size("row")
    time_present = [time_index > 0, time_index >= 0, time_index < time_count - 1]
    height_present = [height_index > 0, height_index >= 0, height_index < height_count - 1]
    presence = jnp.stack(
        [time_flag & height_flag for time_flag in time_present for height_flag in height_present]
    )
    result_set = [
        layer_terms(queries, key_stack[layer_index], value_stack[layer_index], score_scale)
        for layer_index in range(9)
    ]
    maxima = jnp.stack([entry[0] for entry in result_set])
    layer_sums = jnp.stack([entry[1] for entry in result_set])
    weighted = jnp.stack([entry[2] for entry in result_set])
    attention = (
        combine(maxima, layer_sums, weighted, presence)
        .reshape(token_count, feature_count)
        .astype(jnp.bfloat16)
    )
    all_heads = lax.all_gather(attention, "col", axis=1, tiled=True)
    projected = jnp.dot(
        all_heads,
        lax.all_gather(out_weight, "row", axis=0, tiled=True),
        preferred_element_type=jnp.float32,
    )
    return (stream.astype(jnp.float32) + gate * projected).astype(jnp.bfloat16)


def solution(mesh):
    placed = (
        P(("seq", "row"), "col"),
        P(("seq", "row"), "col"),
        P(("seq", "row"), "col"),
        P(("seq", "row"), "col"),
        P("col", None),
        P("col", None),
        P("row", "col"),
        P("col"),
    )
    return jax.shard_map(
        body, mesh=mesh, in_specs=placed, out_specs=P(("seq", "row"), "col"), check_vma=False
    )
```

profile of v0, /device:TPU:0, one launch (start us, length us, event | category | flops | bytes accessed | tf_op | source)
XLA Modules:
  0.0 273.7 jit_solution(16906114481541438225)
XLA Ops:
  6.5 1.4 copy.31
  7.9 1.4 copy.30
  9.5 0.2 fusion.12
  9.7 0.1 maximum_bitcast_fusion
  9.8 1.4 collective-permute-start.1
  11.3 5.0 %collective-permute-start = (bf16[1,1,2,384,768]{3,4,2,1,0:T(8,128)(2,1)S(1)}, bf16[1,1,2,384,768]{3,4,2,1,0:T(8,128)(2,1)S(1)}, u32[]{:S(2)}, u32[]{:S(2)}) collective-permute-start(bf16[1,1,2,384,768]{3,4,2,1,0:T(8,128)(2,1)S(1)} %maximum_bitcast_fusion), channel_id=1, source_target_pairs={{0,16},{1,17},{2,18},{3,19},{4,20},{5,21},{6,22},{7,23},{8,24},{9,... | collective-permute-start | bytes 3538952 | tf_op jit(solution)/shard_map/ppermute | solution.py:17
  16.3 23.9 %collective-permute-done.1 = bf16[1,1,2,384,768]{3,4,2,1,0:T(8,128)(2,1)S(1)} collective-permute-done((bf16[1,1,2,384,768]{3,4,2,1,0:T(8,128)(2,1)S(1)}, bf16[1,1,2,384,768]{3,4,2,1,0:T(8,128)(2,1)S(1)}, u32[]{:S(2)}, u32[]{:S(2)}) %collective-permute-start.1) | collective-permute-done | bytes 1179680 | tf_op jit(solution)/shard_map/ppermute | solution.py:20
  40.2 1.3 collective-permute-done
  41.4 2.2 pad_maximum_fusion.1
  43.7 1.3 collective-permute-start.3
  44.9 6.8 %collective-permute-start.2 = (bf16[3,1,2,384,768]{3,4,2,1,0:T(8,128)(2,1)}, bf16[3,1,2,384,768]{3,4,2,1,0:T(8,128)(2,1)}, u32[]{:S(2)}, u32[]{:S(2)}) collective-permute-start(bf16[3,1,2,384,768]{3,4,2,1,0:T(8,128)(2,1)} %pad_maximum_fusion.1), channel_id=1, source_target_pairs={{0,4},{4,8},{8,12},{1,5},{5,9},{9,13},{2,6},{6,10},{10,14},{3,7},{... | collective-permute-start | bytes 10616840 | tf_op jit(solution)/shard_map/ppermute | solution.py:17
  51.9 0.3 copy.29
  52.3 0.1 fusion.13
  52.4 147.0 %collective-permute-done.3 = bf16[3,1,2,384,768]{3,4,2,1,0:T(8,128)(2,1)} collective-permute-done((bf16[3,1,2,384,768]{3,4,2,1,0:T(8,128)(2,1)}, bf16[3,1,2,384,768]{3,4,2,1,0:T(8,128)(2,1)}, u32[]{:S(2)}, u32[]{:S(2)}) %collective-permute-start.3) | collective-permute-done | bytes 3538976 | tf_op jit(solution)/shard_map/ppermute | solution.py:20
  199.4 5.3 %pad_maximum_fusion = bf16[3,3,2,384,768]{3,4,2,1,0:T(8,128)(2,1)S(1)} fusion(bf16[3,1,2,384,768]{3,4,2,1,0:T(8,128)(2,1)} %collective-permute-done.3, bf16[1,1,2,384,768]{3,4,2,1,0:T(8,128)(2,1)S(1)} %collective-permute-done.1, bf16[1,1,2,384,768]{3,4,2,1,0:T(8,128)(2,1)S(1)} %maximum_bitcast_fusion, bf16[1,1,2,384,768]{3,4,2,1,0:T(8,128)(2,1)} %copy-done, ...), kind=kLoop, calls=%fused_computation | loop fusion | flops 21233664 | bytes 21233664 | tf_op jit(solution)/shard_map/concatenate | solution.py:21
  204.8 2.4 fusion.44
  207.2 0.7 multiply_reduce_fusion.9
  207.9 0.7 multiply_reduce_fusion.8
  208.7 0.7 multiply_reduce_fusion.7
  209.4 0.7 multiply_reduce_fusion.6
  210.2 0.7 multiply_reduce_fusion.5
  210.9 0.7 multiply_reduce_fusion.4
  211.6 0.7 multiply_reduce_fusion.3
  212.4 0.7 multiply_reduce_fusion.2
  213.1 0.6 convert_reduce_fusion.8
  213.8 0.6 convert_reduce_fusion.7
  214.4 0.6 convert_reduce_fusion.6
  215.0 0.6 convert_reduce_fusion.5
  215.6 0.6 convert_reduce_fusion.4
  216.3 0.6 convert_reduce_fusion.3
  216.9 0.6 convert_reduce_fusion.2
  217.5 0.6 convert_reduce_fusion.1
  218.1 0.7 multiply_reduce_fusion.1
  218.9 0.8 convert_reduce_fusion
  219.9 1.8 fusion.8
  221.7 0.7 fusion.7
  222.5 0.3 copy-done.2
  222.8 0.7 fusion.6
  223.6 0.7 fusion.5
  224.3 0.7 fusion.4
  225.1 0.8 fusion.3
  225.9 0.8 fusion.2
  226.6 0.8 fusion.1
  227.4 0.7 fusion
  228.1 1.3 multiply_reduce_fusion
  229.5 0.9 divide_convert_fusion
  230.4 30.4 %all-gather.3.cloned.1.call-done = bf16[384,3072]{0,1:T(8,128)(2,1)} async-done(((bf16[384,768]{0,1:T(8,128)(2,1)}), bf16[384,3072]{0,1:T(8,128)(2,1)}) %all-gather.3.cloned.1.call-update) | async-done | bytes 2359312 | tf_op jit(solution)/shard_map/all_gather | solution.py:88
  260.8 6.0 %fusion.10 = bf16[384,768]{1,0:T(8,128)(2,1)} fusion(bf16[384,3072]{0,1:T(8,128)(2,1)} %all-gather.3.cloned.1.call-done, bf16[3072,768]{1,0:T(8,128)(2,1)} %all-gather.5.cloned.1.call-done, bf16[384,768]{1,0:T(8,128)(2,1)} %param.8, f32[768]{0:T(1024)S(1)} %copy-done.7), kind=kOutput, calls=%fused_computation.54 | convolution fusion | flops 1813118976 | bytes 8260608 | tf_op jit(solution)/shard_map/dot_general | solution.py:89
  (45 shorter events, 0.7 us)
Async XLA Ops:
  6.5 2.9 %copy-start.6 = (f32[6,128]{1,0:T(8,128)S(1)}, f32[6,128]{1,0:T(8,128)}, u32[]{:S(2)}) copy-start(f32[6,128]{1,0:T(8,128)} %param.13) | copy-start | bytes 9220
  6.5 223.9 %all-gather.5.cloned.1.call-start = ((), (), s32[]{:S(2)}) async-start(), calls=%async_computation.1 | async-start | bytes 5898240 | tf_op jit(solution)/shard_map/all_gather | solution.py:91
  9.8 42.0 %copy-start.4 = (bf16[384,768]{1,0:T(8,128)(2,1)S(1)}, bf16[384,768]{1,0:T(8,128)(2,1)}, u32[]{:S(2)}) copy-start(bf16[384,768]{1,0:T(8,128)(2,1)} %param.9) | copy-start | bytes 1769476
  9.8 30.4 %collective-permute-start.1 = (bf16[1,1,2,384,768]{3,4,2,1,0:T(8,128)(2,1)S(1)}, bf16[1,1,2,384,768]{3,4,2,1,0:T(8,128)(2,1)S(1)}, u32[]{:S(2)}, u32[]{:S(2)}) collective-permute-start(bf16[1,1,2,384,768]{3,4,2,1,0:T(8,128)(2,1)S(1)} %maximum_bitcast_fusion), channel_id=1, source_target_pairs={{16,0},{17,1},{18,2},{19,3},{20,4},{21,5},{22,6},{23,7},{24,8},{25... | collective-permute-start | bytes 3538952 | tf_op jit(solution)/shard_map/ppermute | solution.py:20
  11.3 30.2 %collective-permute-start = (bf16[1,1,2,384,768]{3,4,2,1,0:T(8,128)(2,1)S(1)}, bf16[1,1,2,384,768]{3,4,2,1,0:T(8,128)(2,1)S(1)}, u32[]{:S(2)}, u32[]{:S(2)}) collective-permute-start(bf16[1,1,2,384,768]{3,4,2,1,0:T(8,128)(2,1)S(1)} %maximum_bitcast_fusion), channel_id=1, source_target_pairs={{0,16},{1,17},{2,18},{3,19},{4,20},{5,21},{6,22},{7,23},{8,24},{9,... | collective-permute-start | bytes 3538952 | tf_op jit(solution)/shard_map/ppermute | solution.py:17
  41.4 2.2 copy-start
  43.7 155.8 %collective-permute-start.3 = (bf16[3,1,2,384,768]{3,4,2,1,0:T(8,128)(2,1)}, bf16[3,1,2,384,768]{3,4,2,1,0:T(8,128)(2,1)}, u32[]{:S(2)}, u32[]{:S(2)}) collective-permute-start(bf16[3,1,2,384,768]{3,4,2,1,0:T(8,128)(2,1)} %pad_maximum_fusion.1), channel_id=1, source_target_pairs={{4,0},{8,4},{12,8},{5,1},{9,5},{13,9},{6,2},{10,6},{14,10},{7,3},{... | collective-permute-start | bytes 10616840 | tf_op jit(solution)/shard_map/ppermute | solution.py:20
  44.9 154.5 %collective-permute-start.2 = (bf16[3,1,2,384,768]{3,4,2,1,0:T(8,128)(2,1)}, bf16[3,1,2,384,768]{3,4,2,1,0:T(8,128)(2,1)}, u32[]{:S(2)}, u32[]{:S(2)}) collective-permute-start(bf16[3,1,2,384,768]{3,4,2,1,0:T(8,128)(2,1)} %pad_maximum_fusion.1), channel_id=1, source_target_pairs={{0,4},{4,8},{8,12},{1,5},{5,9},{9,13},{2,6},{6,10},{10,14},{3,7},{... | collective-permute-start | bytes 10616840 | tf_op jit(solution)/shard_map/ppermute | solution.py:17
  51.8 209.0 %all-gather.3.cloned.1.call-start = ((), (), s32[]{:S(2)}) async-start(), calls=%async_computation | async-start | bytes 2949120 | tf_op jit(solution)/shard_map/all_gather | solution.py:88
  204.8 2.4 copy-start.5
  219.7 2.1 copy-start.3
  221.7 1.1 copy-start.2
  222.5 1.1 copy-start.1
  228.1 32.7 %copy-start.7 = (f32[768]{0:T(1024)S(1)}, f32[768]{0:T(1024)}, u32[]{:S(2)}) copy-start(f32[768]{0:T(1024)} %param.15) | copy-start | bytes 9220
Sparse Core Ops, SparseCore 0:
  51.9 148.7 all-gather.4
  230.5 30.2 all-gather.2
where the time goes:
time: 274 us
  waiting for transfers between devices  203 us (74%)
  matrix products  20.4 us (7%)
  other arithmetic  16.1 us (6%)
  starting transfers between devices  14.6 us (5%)
  between operations  13.9 us (5%)
  local copies, waits for them, and re-layouts  6.02 us (2%)
    ppermute x2, waiting for transfers between devices, padded_2(): lax.ppermute(lax.slice_in_dim(block, 0, width, axis=dim), axis, backward)  171 us
    all_gather x1, waiting for transfers between devices, body(): all_heads = lax.all_gather(attention, 'col', axis=1, tiled=True)  30.4 us
    ppermute x2, starting transfers between devices, padded_2(): lax.ppermute(lax.slice_in_dim(block, block.shape[dim] - width, None, axis...  11.8 us
    dot_general x9, matrix products, layer_terms(): jnp.einsum('hqk,khd->qhd', unnormed, value_rows, preferred_element_type=j...  7.78 us
    concatenate x2, other arithmetic, padded_2(): block = jnp.concatenate([low, block, high], axis=dim)  7.52 us
    dot_general x9, matrix products, layer_terms(): jnp.einsum('qhd,khd->hqk', queries, key_rows, preferred_element_type=jnp....  6.62 us
    dot_general x1, matrix products, body(): jnp.dot(all_heads, lax.all_gather(out_weight, 'row', axis=0, tiled=True),...  6.01 us
    reduce_sum x9, other arithmetic, layer_terms(): layer_sum = jnp.sum(unnormed.astype(jnp.float32), axis=-1)  5.58 us
  transfers between devices with their start and end apart: 6, of which 4 were waited for; matrix products, arithmetic and copies ran while one was open for 11% of the time, Pallas kernels for 0%

commit v1 on v0

--- a/solution.py
+++ b/solution.py
@@ -1,8 +1,11 @@
+import functools
 import math
 
 import jax
 import jax.numpy as jnp
 from jax import lax
+from jax.experimental import pallas as pl
+from jax.experimental.pallas import tpu as pltpu
 from jax.sharding import PartitionSpec as P
 
 EPSILON = 1e-06
@@ -94,6 +97,249 @@
     return (stream.astype(jnp.float32) + gate * projected).astype(jnp.bfloat16)
 
 
+ABSENT = 1e30
+LOG2_E = 1.4426950408889634
+MIB = 1 << 20
+
+
+def prep_kernel(time_ref, q_ref, k_ref, v_ref, qg_ref, kg_ref, q_keep, q_send, kv_keep, k_send, v_send):
+    mine = time_ref[0]
+    half = q_keep.shape[1]
+    head_size = qg_ref.shape[1]
+    count = half // head_size
+
+    def normed(ref, gain_ref, part, index):
+        start = pl.multiple_of(part * half + index * head_size, head_size)
+        x = ref[:, pl.ds(start, head_size)].astype(jnp.float32)
+        mean_square = jnp.mean(x * x, axis=-1, keepdims=True)
+        gain = gain_ref[pl.ds(part * count + index, 1), :]
+        return (x * lax.rsqrt(mean_square + EPSILON) * gain).astype(jnp.bfloat16)
+
+    for part, k_out, v_out, q_out in (
+        (1 - mine, k_send, v_send, q_send),
+        (mine, kv_keep.at[0], kv_keep.at[1], q_keep),
+    ):
+        v_out[...] = v_ref[:, pl.ds(pl.multiple_of(part * half, half), half)]
+        for index in range(count):
+            columns = pl.ds(index * head_size, head_size)
+            k_out[:, columns] = normed(k_ref, kg_ref, part, index)
+            q_out[:, columns] = normed(q_ref, qg_ref, part, index)
+
+
+def whole_spec(ndim):
+    return pl.BlockSpec(memory_space=pltpu.VMEM)
+
+
+def prep(mine, q, k, v, q_gain, k_gain):
+    rows, width = q.shape
+    half = width // 2
+    one = jax.ShapeDtypeStruct((rows, half), jnp.bfloat16)
+    two = jax.ShapeDtypeStruct((2, rows, half), jnp.bfloat16)
+    return pl.pallas_call(
+        prep_kernel,
+        out_shape=[one, one, two, one, one],
+        in_specs=[pl.BlockSpec(memory_space=pltpu.SMEM)] + [pl.BlockSpec(memory_space=pltpu.VMEM)] * 5,
+        out_specs=[pl.BlockSpec(memory_space=pltpu.VMEM)] * 5,
+        compiler_params=pltpu.CompilerParams(vmem_limit_bytes=16 * MIB),
+        cost_estimate=pl.CostEstimate(flops=rows * width * 16, bytes_accessed=rows * width * 12, transcendentals=0),
+    )(mine, q, k, v, q_gain, k_gain)
+
+
+def attend_kernel(scale, first, last, *refs):
+    present, q_mine, q_peer, k0, k1, k2, v0, v1, v2 = refs[:9]
+    refs = refs[9:]
+    if not first:
+        m_in, acc_in = refs[:2]
+        refs = refs[2:]
+    flags = [None, present[0] > 0, present[1] > 0]
+    keys = [k0[...], k1[...], k2[...]]
+    size = keys[0].shape[1]
+    ones = jnp.ones(keys[0].shape, jnp.bfloat16)
+    values = [jnp.concatenate([v[...], ones], axis=1) for v in (v0, v1, v2)]
+    factor = scale * LOG2_E
+    for which, q_ref in enumerate((q_mine, q_peer)):
+        q = q_ref[...]
+        scores = [
+            lax.dot_general(q, key, (((1,), (1,)), ((), ())), preferred_element_type=jnp.float32)
+            for key in keys
+        ]
+        top = None
+        for flag, score in zip(flags, scores):
+            part = score[:, :size]
+            for start in range(size, score.shape[1], size):
+                part = jnp.maximum(part, score[:, start : start + size])
+            if flag is not None:
+                part = jnp.where(flag, part, NEGATIVE_FLOOR)
+            top = part if top is None else jnp.maximum(top, part)
+        top = jnp.max(top, axis=1, keepdims=True)
+        if first:
+            total = None
+        else:
+            before = m_in[which]
+            top = jnp.maximum(before[:, :1], top)
+            total = acc_in[which] * jnp.exp2((before[:, :1] - top) * factor)
+        for flag, score, value in zip(flags, scores, values):
+            shift = top if flag is None else jnp.where(flag, top, ABSENT)
+            weights = jnp.exp2((score - shift) * factor).astype(jnp.bfloat16)
+            term = jnp.dot(weights, value, preferred_element_type=jnp.float32)
+            total = term if total is None else total + term
+        if last:
+            (out,) = refs
+            out[which] = (total[:, :size] / total[:, size:]).astype(jnp.bfloat16)
+        else:
+            m_out, acc_out = refs
+            m_out[which] = jnp.broadcast_to(top, (top.shape[0], size))
+            acc_out[which] = total
+
+
+def attend(present, q_mine, q_peer, keys, values, head_size, carry=None):
+    rows, width = q_mine.shape
+    heads = width // head_size
+    column = pl.BlockSpec((rows, head_size), lambda h: (0, h))
+
+    def spec(pair):
+        array, part = pair
+        if part is None:
+            return column
+        return pl.BlockSpec((None, rows, head_size), lambda h, part=part: (part, 0, h))
+
+    m_spec = pl.BlockSpec((None, 2, rows, head_size), lambda h: (h, 0, 0, 0))
+    acc_spec = pl.BlockSpec((None, 2, rows, 2 * head_size), lambda h: (h, 0, 0, 0))
+    operands = list(keys) + list(values)
+    in_specs = [pl.BlockSpec(memory_space=pltpu.SMEM), column, column] + [spec(pair) for pair in operands]
+    arguments = [present, q_mine, q_peer] + [pair[0] for pair in operands]
+    first, last = carry is None, carry is not None
+    if first:
+        out_shape = [
+            jax.ShapeDtypeStruct((heads, 2, rows, head_size), jnp.float32),
+            jax.ShapeDtypeStruct((heads, 2, rows, 2 * head_size), jnp.float32),
+        ]
+        out_specs = [m_spec, acc_spec]
+    else:
+        in_specs += [m_spec, acc_spec]
+        arguments += list(carry)
+        out_shape = jax.ShapeDtypeStruct((2, rows, width), jnp.bfloat16)
+        out_specs = pl.BlockSpec((2, rows, head_size), lambda h: (0, 0, h))
+    return pl.pallas_call(
+        functools.partial(attend_kernel, 1.0 / math.sqrt(head_size), first, last),
+        grid=(heads,),
+        out_shape=out_shape,
+        in_specs=in_specs,
+        out_specs=out_specs,
+        compiler_params=pltpu.CompilerParams(vmem_limit_bytes=40 * MIB),
+        cost_estimate=pl.CostEstimate(
+            flops=heads * 2 * rows * 3 * rows * head_size * 8,
+            bytes_accessed=8 * MIB,
+            transcendentals=heads * 2 * rows * 3 * rows,
+        ),
+    )(*arguments)
+
+
+def project_kernel(shift_ref, a0, a1, w0, w1, w2, w3, w4, out):
+    shift = shift_ref[0]
+    for case in range(4):
+
+        @pl.when(shift == case)
+        def _(case=case):
+            weights = [w0[...], w1[...], w2[...], w3[...] + w4[...]]
+            pieces = [a0[0], a1[0], a0[1], a1[1]]
+            total = None
+            for index, piece in enumerate(pieces):
+                term = jnp.dot(piece, weights[index ^ case], preferred_element_type=jnp.float32)
+                total = term if total is None else total + term
+            out[...] = total.astype(out.dtype)
+
+
+def project(shift, pieces, weights, token_block, dtype):
+    rows, width = pieces[0].shape[2:]
+    columns = weights[0].shape[1]
+    piece = pl.BlockSpec((2, None, rows, width), lambda i: (0, token_block, 0, 0))
+    whole = pl.BlockSpec((width, columns), lambda i: (0, 0))
+    return pl.pallas_call(
+        project_kernel,
+        grid=(1,),
+        out_shape=jax.ShapeDtypeStruct((rows, columns), dtype),
+        in_specs=[pl.BlockSpec(memory_space=pltpu.SMEM), piece, piece] + [whole] * 5,
+        out_specs=pl.BlockSpec((rows, columns), lambda i: (0, 0)),
+        compiler_params=pltpu.CompilerParams(vmem_limit_bytes=24 * MIB),
+        cost_estimate=pl.CostEstimate(
+            flops=rows * width * columns * 8, bytes_accessed=5 * MIB, transcendentals=0
+        ),
+    )(shift, *pieces, *weights)
+
+
+def pair_body(stream, query_input, key_input, value_input, q_gain, k_gain, out_weight, gate):
+    head_size = q_gain.shape[1]
+    time = lax.axis_index("seq")
+    height = lax.axis_index("row")
+    column = lax.axis_index("col")
+    rows = lax.axis_size("row")
+
+    def swap(x):
+        return lax.ppermute(x, "seq", [(0, 1), (1, 0)])
+
+    def up(x):
+        return lax.ppermute(x, "row", [(i, i + 1) for i in range(rows - 1)])
+
+    def down(x):
+        return lax.ppermute(x, "row", [(i + 1, i) for i in range(rows - 1)])
+
+    def along(x, axis, mask):
+        return lax.ppermute(x, axis, [(i, i ^ mask) for i in range(4)])
+
+    one = lambda value: jnp.reshape(value, (1,)).astype(jnp.int32)
+    q_keep, q_send, kv_keep, k_send, v_send = prep(
+        one(time), query_input, key_input, value_input, q_gain, k_gain
+    )
+    k_peer = swap(k_send)
+    v_peer = swap(v_send)
+    q_peer = swap(q_send)
+    kv_low, kv_high = up(kv_keep), down(kv_keep)
+    k_low, k_high = up(k_peer), down(k_peer)
+    v_low, v_high = up(v_peer), down(v_peer)
+
+    present = jnp.stack([height > 0, height < rows - 1]).astype(jnp.int32)
+    carry = attend(
+        present, q_keep, q_peer,
+        [(kv_keep, 0), (kv_low, 0), (kv_high, 0)], [(kv_keep, 1), (kv_low, 1), (kv_high, 1)],
+        head_size,
+    )
+    attention = attend(
+        present, q_keep, q_peer,
+        [(k_peer, None), (k_low, None), (k_high, None)], [(v_peer, None), (v_low, None), (v_high, None)],
+        head_size, carry,
+    )
+
+    depth = out_weight.shape[0] // 2
+    mine = lax.dynamic_slice_in_dim(out_weight, time * depth, depth, axis=0)
+    parts = 2
+    width = out_weight.shape[1] // parts
+    weights = []
+    for part in range(parts):
+        w0 = mine[:, part * width : (part + 1) * width]
+        w1 = along(w0, "row", 1)
+        w2 = along(w0, "row", 2)
+        w3 = lax.ppermute(w0, "row", [(1, 2), (2, 1)])
+        w4 = lax.ppermute(w2, "row", [(1, 0), (2, 3)])
+        weights.append((w0, w1, w2, w3, w4))
+
+    across = along(attention, "col", 2)
+    near = jnp.stack([attention, across])
+    far = along(near, "col", 1)
+    shift = one(height ^ column)
+    outs = []
+    for part in range(parts):
+        sent = project(shift, (near, far), weights[part], 1, jnp.bfloat16)
+        outs.append(swap(sent))
+    result = []
+    for part in range(parts):
+        own = project(shift, (near, far), weights[part], 0, jnp.float32)
+        span = slice(part * width, (part + 1) * width)
+        total = own + outs[part].astype(jnp.float32)
+        result.append((stream[:, span].astype(jnp.float32) + gate[span] * total).astype(jnp.bfloat16))
+    return jnp.concatenate(result, axis=1)
+
+
 def solution(mesh):
     placed = (
         P(("seq", "row"), "col"),
@@ -105,6 +351,8 @@
         P("row", "col"),
         P("col"),
     )
+    shape = mesh.shape
+    paired = shape["seq"] == 2 and shape["row"] == 4 and shape["col"] == 4
     return jax.shard_map(
-        body, mesh=mesh, in_specs=placed, out_specs=P(("seq", "row"), "col"), check_vma=False
-    )
+        pair_body if paired else body, mesh=mesh, in_specs=placed, out_specs=P(("seq", "row"), "col"), check_vma=False
+    )

time: 274 us -> 126 us (0.46)
  waiting for transfers between devices: 203 us -> 52.2 us
  starting transfers between devices: 14.6 us -> 41.9 us
  Pallas kernels: 0 us -> 22.1 us
  matrix products: 20.4 us -> 0 us
  other arithmetic: 16.1 us -> 0.48 us
  between operations: 13.9 us -> 0.29 us
    ppermute x4 -> x21, waiting for transfers between devices: 172 us -> 52.2 us  [the longest x6 31.8 us: along(): return lax.ppermute(x, axis, [(i, i ^ mask) for i in range(4)])]
    all_gather x2 -> x0, waiting for transfers between devices: 30.4 us -> none  [the longest x1 30.4 us: body(): all_heads = lax.all_gather(attention, 'col', axis=1, tiled=True)]
    ppermute x4 -> x21, starting transfers between devices: 14.5 us -> 41.9 us  [the longest x3 13.8 us: up(): return lax.ppermute(x, 'row', [(i, i + 1) for i in range(rows - 1)])]
    pallas_call x0 -> x7, Pallas kernels: none -> 22.1 us  [the longest x2 12.3 us: attend(): pl.pallas_call(functools.partial(attend_kernel, 1.0 / math.sqrt(head_size...]
    dot_general x19 -> x0, matrix products: 20.4 us -> none  [the longest x9 7.78 us: layer_terms(): jnp.einsum('hqk,khd->qhd', unnormed, value_rows, preferred_element_type=j...]
    concatenate x2 -> x0, other arithmetic: 7.52 us -> none  [padded_2(): block = jnp.concatenate([low, block, high], axis=dim)]
    reduce_sum x13 -> x0, other arithmetic: 7.19 us -> none  [the longest x9 5.58 us: layer_terms(): layer_sum = jnp.sum(unnormed.astype(jnp.float32), axis=-1)]
    unnamed x35 -> x24, local copies, waits for them, and re-layouts: 3.5 us -> 7.09 us
  transfers between devices with their start and end apart: 6 -> 21, of which waited for: 4 -> 9; matrix products, arithmetic and copies ran while one was open for 11% -> 1% of each run, Pallas kernels for 0% -> 12%
where the time goes in v1:
time: 126 us; the launch traced here: 125 us
  waiting for transfers between devices  52.2 us (41%)
  starting transfers between devices  41.9 us (33%)
  Pallas kernels  22.1 us (18%)
  local copies, waits for them, and re-layouts  8.22 us (7%)
    ppermute x6, waiting for transfers between devices, along(): return lax.ppermute(x, axis, [(i, i ^ mask) for i in range(4)])  31.8 us
    ppermute x5, waiting for transfers between devices, swap(): return lax.ppermute(x, 'seq', [(0, 1), (1, 0)])  14 us
    ppermute x3, starting transfers between devices, up(): return lax.ppermute(x, 'row', [(i, i + 1) for i in range(rows - 1)])  13.8 us
    ppermute x6, starting transfers between devices, along(): return lax.ppermute(x, axis, [(i, i ^ mask) for i in range(4)])  12.9 us
    pallas_call x2, Pallas kernels, attend(): pl.pallas_call(functools.partial(attend_kernel, 1.0 / math.sqrt(head_size...  12.3 us
    pallas_call x4, Pallas kernels, project(): pl.pallas_call(project_kernel, grid=(1,), out_shape=jax.ShapeDtypeStruct(...  8.48 us
    unnamed x24, local copies, waits for them, and re-layouts  7.09 us
    ppermute x5, starting transfers between devices, swap(): return lax.ppermute(x, 'seq', [(0, 1), (1, 0)])  6.8 us
  transfers between devices with their start and end apart: 21, of which 9 were waited for; matrix products, arithmetic and copies ran while one was open for 1% of the time, Pallas kernels for 12%

profile of v1, /device:TPU:0, one launch (start us, length us, event | category | flops | bytes accessed | tf_op | source)
XLA Modules:
  0.0 125.2 jit_solution(15804435542741895267)
XLA Ops:
  0.0 1.1 copy-done.3
  1.1 1.1 copy-done.4
  2.1 1.1 copy-done.5
  3.2 0.7 copy-done.6
  3.9 0.7 copy-done.7
  4.6 1.3 %shard_map.82 = (bf16[384,384]{1,0:T(8,128)(2,1)S(1)}, bf16[384,384]{1,0:T(8,128)(2,1)S(1)}, bf16[2,384,384]{2,1,0:T(8,128)(2,1)S(1)}, bf16[384,384]{1,0:T(8,128)(2,1)}, bf16[384,384]{1,0:T(8,128)(2,1)S(1)}) custom-call(s32[1]{0:T(128)} %bitcast.3.time_ref, bf16[384,768]{1,0:T(8,128)(2,1)S(1)} %copy-done.3, bf16[384,768]{1,0:T(8,128)(2,1)S(1)} %copy-done.4, ...), custom_call_target="tpu_custom_call" | custom-call | flops 4718592 | bytes 3538944 | tf_op jit(solution)/shard_map/pallas_call | solution.py:138
  5.8 5.0 %collective-permute-start.7 = (bf16[2,384,384]{2,1,0:T(8,128)(2,1)S(1)}, bf16[2,384,384]{2,1,0:T(8,128)(2,1)S(1)}, u32[]{:S(2)}, u32[]{:S(2)}) collective-permute-start(bf16[2,384,384]{2,1,0:T(8,128)(2,1)S(1)} %get-tuple-element.16.refs_3_.refs_6_), channel_id=1, source_target_pairs={{0,4},{4,8},{8,12},{1,5},{5,9},{9,13},{2,6},{6,10},{10,14},{3,7},{... | collective-permute-start | bytes 1769480 | tf_op jit(solution)/shard_map/ppermute | solution.py:282
  10.8 1.3 %collective-permute-start.8 = (bf16[2,384,384]{2,1,0:T(8,128)(2,1)S(1)}, bf16[2,384,384]{2,1,0:T(8,128)(2,1)S(1)}, u32[]{:S(2)}, u32[]{:S(2)}) collective-permute-start(bf16[2,384,384]{2,1,0:T(8,128)(2,1)S(1)} %get-tuple-element.16.refs_3_.refs_6_), channel_id=1, source_target_pairs={{4,0},{8,4},{12,8},{5,1},{9,5},{13,9},{6,2},{10,6},{14,10},{7,3},{... | collective-permute-start | bytes 1769480 | tf_op jit(solution)/shard_map/ppermute | solution.py:285
  12.1 1.6 %collective-permute-start.1 = (bf16[384,384]{1,0:T(8,128)(2,1)}, bf16[384,384]{1,0:T(8,128)(2,1)S(1)}, u32[]{:S(2)}, u32[]{:S(2)}) collective-permute-start(bf16[384,384]{1,0:T(8,128)(2,1)} %get-tuple-element.14), channel_id=1, source_target_pairs={{0,16},{16,0},{1,17},{17,1},{2,18},{18,2},{3,19},{19,3},{4,20},{20... | collective-permute-start | bytes 884744 | tf_op jit(solution)/shard_map/ppermute | solution.py:279
  13.7 0.5 collective-permute-start
  14.2 1.5 %collective-permute-start.4 = (bf16[384,384]{1,0:T(8,128)(2,1)S(1)}, bf16[384,384]{1,0:T(8,128)(2,1)S(1)}, u32[]{:S(2)}, u32[]{:S(2)}) collective-permute-start(bf16[384,384]{1,0:T(8,128)(2,1)S(1)} %get-tuple-element.15), channel_id=1, source_target_pairs={{0,16},{16,0},{1,17},{17,1},{2,18},{18,2},{3,19},{19,3},{4,20},{20... | collective-permute-start | bytes 884744 | tf_op jit(solution)/shard_map/ppermute | solution.py:279
  15.7 6.6 %collective-permute-done.1.refs_3_ = bf16[384,384]{1,0:T(8,128)(2,1)S(1)} collective-permute-done((bf16[384,384]{1,0:T(8,128)(2,1)}, bf16[384,384]{1,0:T(8,128)(2,1)S(1)}, u32[]{:S(2)}, u32[]{:S(2)}) %collective-permute-start.1) | collective-permute-done | bytes 294944 | tf_op jit(solution)/shard_map/ppermute | solution.py:279
  22.3 4.6 %collective-permute-start.2 = (bf16[384,384]{1,0:T(8,128)(2,1)S(1)}, bf16[384,384]{1,0:T(8,128)(2,1)S(1)}, u32[]{:S(2)}, u32[]{:S(2)}) collective-permute-start(bf16[384,384]{1,0:T(8,128)(2,1)S(1)} %collective-permute-done.1.refs_3_), channel_id=1, source_target_pairs={{0,4},{4,8},{8,12},{1,5},{5,9},{9,13},{2,6},{6,10},{10,14},{3,7},{... | collective-permute-start | bytes 884744 | tf_op jit(solution)/shard_map/ppermute | solution.py:282
  26.9 1.7 %collective-permute-done.refs_2_ = bf16[384,384]{1,0:T(8,128)(2,1)S(1)} collective-permute-done((bf16[384,384]{1,0:T(8,128)(2,1)S(1)}, bf16[384,384]{1,0:T(8,128)(2,1)S(1)}, u32[]{:S(2)}, u32[]{:S(2)}) %collective-permute-start) | collective-permute-done | bytes 294944 | tf_op jit(solution)/shard_map/ppermute | solution.py:279
  28.6 1.3 %collective-permute-start.3 = (bf16[384,384]{1,0:T(8,128)(2,1)S(1)}, bf16[384,384]{1,0:T(8,128)(2,1)S(1)}, u32[]{:S(2)}, u32[]{:S(2)}) collective-permute-start(bf16[384,384]{1,0:T(8,128)(2,1)S(1)} %collective-permute-done.1.refs_3_), channel_id=1, source_target_pairs={{4,0},{8,4},{12,8},{5,1},{9,5},{13,9},{6,2},{10,6},{14,10},{7,3},{... | collective-permute-start | bytes 884744 | tf_op jit(solution)/shard_map/ppermute | solution.py:285
  29.9 3.6 %collective-permute-done.4.refs_6_ = bf16[384,384]{1,0:T(8,128)(2,1)S(1)} collective-permute-done((bf16[384,384]{1,0:T(8,128)(2,1)S(1)}, bf16[384,384]{1,0:T(8,128)(2,1)S(1)}, u32[]{:S(2)}, u32[]{:S(2)}) %collective-permute-start.4) | collective-permute-done | bytes 294944 | tf_op jit(solution)/shard_map/ppermute | solution.py:279
  33.5 4.3 %collective-permute-start.5 = (bf16[384,384]{1,0:T(8,128)(2,1)S(1)}, bf16[384,384]{1,0:T(8,128)(2,1)S(1)}, u32[]{:S(2)}, u32[]{:S(2)}) collective-permute-start(bf16[384,384]{1,0:T(8,128)(2,1)S(1)} %collective-permute-done.4.refs_6_), channel_id=1, source_target_pairs={{0,4},{4,8},{8,12},{1,5},{5,9},{9,13},{2,6},{6,10},{10,14},{3,7},{... | collective-permute-start | bytes 884744 | tf_op jit(solution)/shard_map/ppermute | solution.py:282
  37.8 1.3 %collective-permute-start.6 = (bf16[384,384]{1,0:T(8,128)(2,1)S(1)}, bf16[384,384]{1,0:T(8,128)(2,1)S(1)}, u32[]{:S(2)}, u32[]{:S(2)}) collective-permute-start(bf16[384,384]{1,0:T(8,128)(2,1)S(1)} %collective-permute-done.4.refs_6_), channel_id=1, source_target_pairs={{4,0},{8,4},{12,8},{5,1},{9,5},{13,9},{6,2},{10,6},{14,10},{7,3},{... | collective-permute-start | bytes 884744 | tf_op jit(solution)/shard_map/ppermute | solution.py:285
  39.1 0.1 add_convert_fusion.2.refs_0_
  39.1 6.2 %shard_map.83 = (f32[3,2,384,128]{3,2,1,0:T(8,128)S(1)}, f32[3,2,384,256]{3,2,1,0:T(8,128)S(1)}) custom-call(s32[2]{0:T(128)S(1)} %add_convert_fusion.2.refs_0_, bf16[384,384]{1,0:T(8,128)(2,1)S(1)} %get-tuple-element.12.refs_1_, bf16[384,384]{1,0:T(8,128)(2,1)S(1)} %collective-permute-done.refs_2_, ...), custom_call_target="tpu_custom_call" | custom-call | flops 2717908992 | bytes 8388608 | tf_op jit(solution)/shard_map/pallas_call | solution.py:223
  45.4 1.3 collective-permute-done.6.refs_8_
  46.6 6.1 %shard_map.84 = bf16[2,384,384]{2,1,0:T(8,128)(2,1)S(1)} custom-call(s32[2]{0:T(128)S(1)} %add_convert_fusion.2.refs_0_, bf16[384,384]{1,0:T(8,128)(2,1)S(1)} %get-tuple-element.12.refs_1_, bf16[384,384]{1,0:T(8,128)(2,1)S(1)} %collective-permute-done.refs_2_, bf16[384,384]{1,0:T(8,128)(2,1)S(1)} %collective-permute-done.1.refs_3_, ...), custom_call_target="tpu_custom_call" | custom-call | flops 2717908992 | bytes 8388608 | tf_op jit(solution)/shard_map/pallas_call | solution.py:223
  52.8 1.6 %collective-permute-start.9 = (bf16[2,384,384]{2,1,0:T(8,128)(2,1)S(1)}, bf16[2,384,384]{2,1,0:T(8,128)(2,1)S(1)}, u32[]{:S(2)}, u32[]{:S(2)}) collective-permute-start(bf16[2,384,384]{2,1,0:T(8,128)(2,1)S(1)} %shard_map.84), channel_id=1, source_target_pairs={{0,2},{1,3},{2,0},{3,1},{4,6},{5,7},{6,4},{7,5},{8,10},{9,11},{10,... | collective-permute-start | bytes 1769480 | tf_op jit(solution)/shard_map/ppermute | solution.py:288
  54.3 10.9 %collective-permute-done.9 = bf16[2,384,384]{2,1,0:T(8,128)(2,1)S(1)} collective-permute-done((bf16[2,384,384]{2,1,0:T(8,128)(2,1)S(1)}, bf16[2,384,384]{2,1,0:T(8,128)(2,1)S(1)}, u32[]{:S(2)}, u32[]{:S(2)}) %collective-permute-start.9) | collective-permute-done | bytes 589856 | tf_op jit(solution)/shard_map/ppermute | solution.py:288
  65.2 0.1 pad_maximum_fusion.a0
  65.5 1.1 constant_dynamic-slice_fusion
  66.6 3.1 %collective-permute-start.17 = (bf16[384,384]{1,0:T(8,128)(2,1)S(1)}, bf16[384,384]{1,0:T(8,128)(2,1)S(1)}, u32[]{:S(2)}, u32[]{:S(2)}) collective-permute-start(bf16[384,384]{1,0:T(8,128)(2,1)S(1)} %get-tuple-element.20.w0), channel_id=1, source_target_pairs={{0,8},{4,12},{8,0},{12,4},{1,9},{5,13},{9,1},{13,5},{2,10},{6,14},... | collective-permute-start | bytes 884744 | tf_op jit(solution)/shard_map/ppermute | solution.py:288
  69.7 1.6 %collective-permute-start.16 = (bf16[384,384]{1,0:T(8,128)(2,1)S(1)}, bf16[384,384]{1,0:T(8,128)(2,1)S(1)}, u32[]{:S(2)}, u32[]{:S(2)}) collective-permute-start(bf16[384,384]{1,0:T(8,128)(2,1)S(1)} %get-tuple-element.20.w0), channel_id=1, source_target_pairs={{0,4},{4,0},{8,12},{12,8},{1,5},{5,1},{9,13},{13,9},{2,6},{6,2},{1... | collective-permute-start | bytes 884744 | tf_op jit(solution)/shard_map/ppermute | solution.py:288
  71.3 0.7 collective-permute-start.18
  72.0 3.2 %collective-permute-start.12 = (bf16[384,384]{1,0:T(8,128)(2,1)S(1)}, bf16[384,384]{1,0:T(8,128)(2,1)}, u32[]{:S(2)}, u32[]{:S(2)}) collective-permute-start(bf16[384,384]{1,0:T(8,128)(2,1)S(1)} %get-tuple-element.19.w0), channel_id=1, source_target_pairs={{0,8},{4,12},{8,0},{12,4},{1,9},{5,13},{9,1},{13,5},{2,10},{6,14},... | collective-permute-start | bytes 884744 | tf_op jit(solution)/shard_map/ppermute | solution.py:288
  75.1 8.8 %collective-permute-done.17.w2 = bf16[384,384]{1,0:T(8,128)(2,1)S(1)} collective-permute-done((bf16[384,384]{1,0:T(8,128)(2,1)S(1)}, bf16[384,384]{1,0:T(8,128)(2,1)S(1)}, u32[]{:S(2)}, u32[]{:S(2)}) %collective-permute-start.17) | collective-permute-done | bytes 294944 | tf_op jit(solution)/shard_map/ppermute | solution.py:288
  83.9 1.3 %collective-permute-start.19 = (bf16[384,384]{1,0:T(8,128)(2,1)S(1)}, bf16[384,384]{1,0:T(8,128)(2,1)}, u32[]{:S(2)}, u32[]{:S(2)}) collective-permute-start(bf16[384,384]{1,0:T(8,128)(2,1)S(1)} %collective-permute-done.17.w2), channel_id=1, source_target_pairs={{4,0},{8,12},{5,1},{9,13},{6,2},{10,14},{7,3},{11,15},{20,16},{24,... | collective-permute-start | bytes 884744 | tf_op jit(solution)/shard_map/ppermute | solution.py:323
  85.2 3.4 %collective-permute-start.11 = (bf16[384,384]{1,0:T(8,128)(2,1)S(1)}, bf16[384,384]{1,0:T(8,128)(2,1)}, u32[]{:S(2)}, u32[]{:S(2)}) collective-permute-start(bf16[384,384]{1,0:T(8,128)(2,1)S(1)} %get-tuple-element.19.w0), channel_id=1, source_target_pairs={{0,4},{4,0},{8,12},{12,8},{1,5},{5,1},{9,13},{13,9},{2,6},{6,2},{1... | collective-permute-start | bytes 884744 | tf_op jit(solution)/shard_map/ppermute | solution.py:288
  88.6 0.7 copy-done
  89.3 1.4 %collective-permute-start.13 = (bf16[384,384]{1,0:T(8,128)(2,1)S(1)}, bf16[384,384]{1,0:T(8,128)(2,1)}, u32[]{:S(2)}, u32[]{:S(2)}) collective-permute-start(bf16[384,384]{1,0:T(8,128)(2,1)S(1)} %get-tuple-element.19.w0), channel_id=1, source_target_pairs={{4,8},{8,4},{5,9},{9,5},{6,10},{10,6},{7,11},{11,7},{20,24},{24,20... | collective-permute-start | bytes 884744 | tf_op jit(solution)/shard_map/ppermute | solution.py:322
  90.7 12.2 %collective-permute-done.12.w2 = bf16[384,384]{1,0:T(8,128)(2,1)} collective-permute-done((bf16[384,384]{1,0:T(8,128)(2,1)S(1)}, bf16[384,384]{1,0:T(8,128)(2,1)}, u32[]{:S(2)}, u32[]{:S(2)}) %collective-permute-start.12) | collective-permute-done | bytes 294944 | tf_op jit(solution)/shard_map/ppermute | solution.py:288
  102.9 1.3 %collective-permute-start.14 = (bf16[384,384]{1,0:T(8,128)(2,1)}, bf16[384,384]{1,0:T(8,128)(2,1)}, u32[]{:S(2)}, u32[]{:S(2)}) collective-permute-start(bf16[384,384]{1,0:T(8,128)(2,1)} %collective-permute-done.12.w2), channel_id=1, source_target_pairs={{4,0},{8,12},{5,1},{9,13},{6,2},{10,14},{7,3},{11,15},{20,16},{24,... | collective-permute-start | bytes 884744 | tf_op jit(solution)/shard_map/ppermute | solution.py:323
  104.2 1.0 copy-done.1
  105.1 2.0 %shard_map.88 = bf16[384,384]{1,0:T(8,128)(2,1)S(1)} custom-call(s32[1]{0:T(128)} %bitcast.shift_ref, bf16[2,2,384,384]{3,2,1,0:T(8,128)(2,1)S(1)} %pad_maximum_fusion.a0, bf16[2,2,384,384]{3,2,1,0:T(8,128)(2,1)S(1)} %collective-permute-done.10.a1, bf16[384,384]{1,0:T(8,128)(2,1)S(1)} %get-tuple-element.20.w0, ...), custom_call_target="tpu_custom_call" | custom-call | flops 452984832 | bytes 5242880 | tf_op jit(solution)/shard_map/pallas_call | solution.py:258
  107.1 1.6 %collective-permute-start.20 = (bf16[384,384]{1,0:T(8,128)(2,1)S(1)}, bf16[384,384]{1,0:T(8,128)(2,1)S(1)}, u32[]{:S(2)}, u32[]{:S(2)}) collective-permute-start(bf16[384,384]{1,0:T(8,128)(2,1)S(1)} %shard_map.88), channel_id=1, source_target_pairs={{0,16},{16,0},{1,17},{17,1},{2,18},{18,2},{3,19},{19,3},{4,20},{20... | collective-permute-start | bytes 884744 | tf_op jit(solution)/shard_map/ppermute | solution.py:279
  108.7 5.1 %collective-permute-done.14.w4 = bf16[384,384]{1,0:T(8,128)(2,1)} collective-permute-done((bf16[384,384]{1,0:T(8,128)(2,1)}, bf16[384,384]{1,0:T(8,128)(2,1)}, u32[]{:S(2)}, u32[]{:S(2)}) %collective-permute-start.14) | collective-permute-done | bytes 294944 | tf_op jit(solution)/shard_map/ppermute | solution.py:323
  113.8 2.3 %shard_map.86 = bf16[384,384]{1,0:T(8,128)(2,1)S(1)} custom-call(s32[1]{0:T(128)} %bitcast.shift_ref, bf16[2,2,384,384]{3,2,1,0:T(8,128)(2,1)S(1)} %pad_maximum_fusion.a0, bf16[2,2,384,384]{3,2,1,0:T(8,128)(2,1)S(1)} %collective-permute-done.10.a1, bf16[384,384]{1,0:T(8,128)(2,1)S(1)} %get-tuple-element.19.w0, bf16[384,384]{1,0:T(8,128)(2,1)} %collective-permute-done.11.w1, ...), custom_call_target="tpu_custom_call" | custom-call | flops 452984832 | bytes 5242880 | tf_op jit(solution)/shard_map/pallas_call | solution.py:258
  116.2 1.6 %collective-permute-start.15 = (bf16[384,384]{1,0:T(8,128)(2,1)S(1)}, bf16[384,384]{1,0:T(8,128)(2,1)S(1)}, u32[]{:S(2)}, u32[]{:S(2)}) collective-permute-start(bf16[384,384]{1,0:T(8,128)(2,1)S(1)} %shard_map.86), channel_id=1, source_target_pairs={{0,16},{16,0},{1,17},{17,1},{2,18},{18,2},{3,19},{19,3},{4,20},{20... | collective-permute-start | bytes 884744 | tf_op jit(solution)/shard_map/ppermute | solution.py:279
  117.8 2.0 %shard_map.87 = f32[384,384]{1,0:T(8,128)S(1)} custom-call(s32[1]{0:T(128)} %bitcast.shift_ref, bf16[2,2,384,384]{3,2,1,0:T(8,128)(2,1)S(1)} %pad_maximum_fusion.a0, bf16[2,2,384,384]{3,2,1,0:T(8,128)(2,1)S(1)} %collective-permute-done.10.a1, bf16[384,384]{1,0:T(8,128)(2,1)S(1)} %get-tuple-element.20.w0, bf16[384,384]{1,0:T(8,128)(2,1)S(1)} %collective-permute-done.16.w1, ...), custom_call_target="tpu_custom_call" | custom-call | flops 452984832 | bytes 5242880 | tf_op jit(solution)/shard_map/pallas_call | solution.py:258
  119.8 2.2 %shard_map.85 = f32[384,384]{1,0:T(8,128)S(1)} custom-call(s32[1]{0:T(128)} %bitcast.shift_ref, bf16[2,2,384,384]{3,2,1,0:T(8,128)(2,1)S(1)} %pad_maximum_fusion.a0, bf16[2,2,384,384]{3,2,1,0:T(8,128)(2,1)S(1)} %collective-permute-done.10.a1, bf16[384,384]{1,0:T(8,128)(2,1)S(1)} %get-tuple-element.19.w0, bf16[384,384]{1,0:T(8,128)(2,1)} %collective-permute-done.11.w1, ...), custom_call_target="tpu_custom_call" | custom-call | flops 452984832 | bytes 5242880 | tf_op jit(solution)/shard_map/pallas_call | solution.py:258
  122.0 2.1 %collective-permute-done.15 = bf16[384,384]{1,0:T(8,128)(2,1)S(1)} collective-permute-done((bf16[384,384]{1,0:T(8,128)(2,1)S(1)}, bf16[384,384]{1,0:T(8,128)(2,1)S(1)}, u32[]{:S(2)}, u32[]{:S(2)}) %collective-permute-start.15) | collective-permute-done | bytes 294944 | tf_op jit(solution)/shard_map/ppermute | solution.py:279
  124.1 0.3 add_convert_fusion.1
  124.4 0.8 copy-done.11
  (31 shorter events, 0.1 us)
Async XLA Ops:
  0.0 1.1 copy-start.3
  1.1 1.1 copy-start.4
  2.1 1.1 copy-start.5
  3.2 0.7 copy-start.6
  3.9 0.7 copy-start.7
  5.8 31.9 %collective-permute-start.7 = (bf16[2,384,384]{2,1,0:T(8,128)(2,1)S(1)}, bf16[2,384,384]{2,1,0:T(8,128)(2,1)S(1)}, u32[]{:S(2)}, u32[]{:S(2)}) collective-permute-start(bf16[2,384,384]{2,1,0:T(8,128)(2,1)S(1)} %get-tuple-element.16.refs_3_.refs_6_), channel_id=1, source_target_pairs={{0,4},{4,8},{8,12},{1,5},{5,9},{9,13},{2,6},{6,10},{10,14},{3,7},{... | collective-permute-start | bytes 1769480 | tf_op jit(solution)/shard_map/ppermute | solution.py:282
  10.8 28.4 %collective-permute-start.8 = (bf16[2,384,384]{2,1,0:T(8,128)(2,1)S(1)}, bf16[2,384,384]{2,1,0:T(8,128)(2,1)S(1)}, u32[]{:S(2)}, u32[]{:S(2)}) collective-permute-start(bf16[2,384,384]{2,1,0:T(8,128)(2,1)S(1)} %get-tuple-element.16.refs_3_.refs_6_), channel_id=1, source_target_pairs={{4,0},{8,4},{12,8},{5,1},{9,5},{13,9},{6,2},{10,6},{14,10},{7,3},{... | collective-permute-start | bytes 1769480 | tf_op jit(solution)/shard_map/ppermute | solution.py:285
  12.1 10.2 %collective-permute-start.1 = (bf16[384,384]{1,0:T(8,128)(2,1)}, bf16[384,384]{1,0:T(8,128)(2,1)S(1)}, u32[]{:S(2)}, u32[]{:S(2)}) collective-permute-start(bf16[384,384]{1,0:T(8,128)(2,1)} %get-tuple-element.14), channel_id=1, source_target_pairs={{0,16},{16,0},{1,17},{17,1},{2,18},{18,2},{3,19},{19,3},{4,20},{20... | collective-permute-start | bytes 884744 | tf_op jit(solution)/shard_map/ppermute | solution.py:279
  13.7 14.9 %collective-permute-start = (bf16[384,384]{1,0:T(8,128)(2,1)S(1)}, bf16[384,384]{1,0:T(8,128)(2,1)S(1)}, u32[]{:S(2)}, u32[]{:S(2)}) collective-permute-start(bf16[384,384]{1,0:T(8,128)(2,1)S(1)} %get-tuple-element.13), channel_id=1, source_target_pairs={{0,16},{16,0},{1,17},{17,1},{2,18},{18,2},{3,19},{19,3},{4,20},{20... | collective-permute-start | bytes 884744 | tf_op jit(solution)/shard_map/ppermute | solution.py:279
  14.2 19.3 %collective-permute-start.4 = (bf16[384,384]{1,0:T(8,128)(2,1)S(1)}, bf16[384,384]{1,0:T(8,128)(2,1)S(1)}, u32[]{:S(2)}, u32[]{:S(2)}) collective-permute-start(bf16[384,384]{1,0:T(8,128)(2,1)S(1)} %get-tuple-element.15), channel_id=1, source_target_pairs={{0,16},{16,0},{1,17},{17,1},{2,18},{18,2},{3,19},{19,3},{4,20},{20... | collective-permute-start | bytes 884744 | tf_op jit(solution)/shard_map/ppermute | solution.py:279
  22.3 23.1 %collective-permute-start.2 = (bf16[384,384]{1,0:T(8,128)(2,1)S(1)}, bf16[384,384]{1,0:T(8,128)(2,1)S(1)}, u32[]{:S(2)}, u32[]{:S(2)}) collective-permute-start(bf16[384,384]{1,0:T(8,128)(2,1)S(1)} %collective-permute-done.1.refs_3_), channel_id=1, source_target_pairs={{0,4},{4,8},{8,12},{1,5},{5,9},{9,13},{2,6},{6,10},{10,14},{3,7},{... | collective-permute-start | bytes 884744 | tf_op jit(solution)/shard_map/ppermute | solution.py:282
  28.6 16.8 %collective-permute-start.3 = (bf16[384,384]{1,0:T(8,128)(2,1)S(1)}, bf16[384,384]{1,0:T(8,128)(2,1)S(1)}, u32[]{:S(2)}, u32[]{:S(2)}) collective-permute-start(bf16[384,384]{1,0:T(8,128)(2,1)S(1)} %collective-permute-done.1.refs_3_), channel_id=1, source_target_pairs={{4,0},{8,4},{12,8},{5,1},{9,5},{13,9},{6,2},{10,6},{14,10},{7,3},{... | collective-permute-start | bytes 884744 | tf_op jit(solution)/shard_map/ppermute | solution.py:285
  33.5 11.9 %collective-permute-start.5 = (bf16[384,384]{1,0:T(8,128)(2,1)S(1)}, bf16[384,384]{1,0:T(8,128)(2,1)S(1)}, u32[]{:S(2)}, u32[]{:S(2)}) collective-permute-start(bf16[384,384]{1,0:T(8,128)(2,1)S(1)} %collective-permute-done.4.refs_6_), channel_id=1, source_target_pairs={{0,4},{4,8},{8,12},{1,5},{5,9},{9,13},{2,6},{6,10},{10,14},{3,7},{... | collective-permute-start | bytes 884744 | tf_op jit(solution)/shard_map/ppermute | solution.py:282
  37.8 8.9 %collective-permute-start.6 = (bf16[384,384]{1,0:T(8,128)(2,1)S(1)}, bf16[384,384]{1,0:T(8,128)(2,1)S(1)}, u32[]{:S(2)}, u32[]{:S(2)}) collective-permute-start(bf16[384,384]{1,0:T(8,128)(2,1)S(1)} %collective-permute-done.4.refs_6_), channel_id=1, source_target_pairs={{4,0},{8,4},{12,8},{5,1},{9,5},{13,9},{6,2},{10,6},{14,10},{7,3},{... | collective-permute-start | bytes 884744 | tf_op jit(solution)/shard_map/ppermute | solution.py:285
  52.8 12.4 %collective-permute-start.9 = (bf16[2,384,384]{2,1,0:T(8,128)(2,1)S(1)}, bf16[2,384,384]{2,1,0:T(8,128)(2,1)S(1)}, u32[]{:S(2)}, u32[]{:S(2)}) collective-permute-start(bf16[2,384,384]{2,1,0:T(8,128)(2,1)S(1)} %shard_map.84), channel_id=1, source_target_pairs={{0,2},{1,3},{2,0},{3,1},{4,6},{5,7},{6,4},{7,5},{8,10},{9,11},{10,... | collective-permute-start | bytes 1769480 | tf_op jit(solution)/shard_map/ppermute | solution.py:288
  65.4 38.8 %collective-permute-start.10 = (bf16[2,2,384,384]{3,2,1,0:T(8,128)(2,1)S(1)}, bf16[2,2,384,384]{3,2,1,0:T(8,128)(2,1)S(1)}, u32[]{:S(2)}, u32[]{:S(2)}) collective-permute-start(bf16[2,2,384,384]{3,2,1,0:T(8,128)(2,1)S(1)} %pad_maximum_fusion.a0), channel_id=1, source_target_pairs={{0,1},{1,0},{2,3},{3,2},{4,5},{5,4},{6,7},{7,6},{8,9},{9,8},{10,11... | collective-permute-start | bytes 3538952 | tf_op jit(solution)/shard_map/ppermute | solution.py:288
  66.6 17.3 %collective-permute-start.17 = (bf16[384,384]{1,0:T(8,128)(2,1)S(1)}, bf16[384,384]{1,0:T(8,128)(2,1)S(1)}, u32[]{:S(2)}, u32[]{:S(2)}) collective-permute-start(bf16[384,384]{1,0:T(8,128)(2,1)S(1)} %get-tuple-element.20.w0), channel_id=1, source_target_pairs={{0,8},{4,12},{8,0},{12,4},{1,9},{5,13},{9,1},{13,5},{2,10},{6,14},... | collective-permute-start | bytes 884744 | tf_op jit(solution)/shard_map/ppermute | solution.py:288
  69.7 15.5 %collective-permute-start.16 = (bf16[384,384]{1,0:T(8,128)(2,1)S(1)}, bf16[384,384]{1,0:T(8,128)(2,1)S(1)}, u32[]{:S(2)}, u32[]{:S(2)}) collective-permute-start(bf16[384,384]{1,0:T(8,128)(2,1)S(1)} %get-tuple-element.20.w0), channel_id=1, source_target_pairs={{0,4},{4,0},{8,12},{12,8},{1,5},{5,1},{9,13},{13,9},{2,6},{6,2},{1... | collective-permute-start | bytes 884744 | tf_op jit(solution)/shard_map/ppermute | solution.py:288
  71.3 17.3 %collective-permute-start.18 = (bf16[384,384]{1,0:T(8,128)(2,1)S(1)}, bf16[384,384]{1,0:T(8,128)(2,1)S(1)}, u32[]{:S(2)}, u32[]{:S(2)}) collective-permute-start(bf16[384,384]{1,0:T(8,128)(2,1)S(1)} %get-tuple-element.20.w0), channel_id=1, source_target_pairs={{4,8},{8,4},{5,9},{9,5},{6,10},{10,6},{7,11},{11,7},{20,24},{24,20... | collective-permute-start | bytes 884744 | tf_op jit(solution)/shard_map/ppermute | solution.py:322
  72.0 30.9 %collective-permute-start.12 = (bf16[384,384]{1,0:T(8,128)(2,1)S(1)}, bf16[384,384]{1,0:T(8,128)(2,1)}, u32[]{:S(2)}, u32[]{:S(2)}) collective-permute-start(bf16[384,384]{1,0:T(8,128)(2,1)S(1)} %get-tuple-element.19.w0), channel_id=1, source_target_pairs={{0,8},{4,12},{8,0},{12,4},{1,9},{5,13},{9,1},{13,5},{2,10},{6,14},... | collective-permute-start | bytes 884744 | tf_op jit(solution)/shard_map/ppermute | solution.py:288
  83.9 20.3 %collective-permute-start.19 = (bf16[384,384]{1,0:T(8,128)(2,1)S(1)}, bf16[384,384]{1,0:T(8,128)(2,1)}, u32[]{:S(2)}, u32[]{:S(2)}) collective-permute-start(bf16[384,384]{1,0:T(8,128)(2,1)S(1)} %collective-permute-done.17.w2), channel_id=1, source_target_pairs={{4,0},{8,12},{5,1},{9,13},{6,2},{10,14},{7,3},{11,15},{20,16},{24,... | collective-permute-start | bytes 884744 | tf_op jit(solution)/shard_map/ppermute | solution.py:323
  85.2 23.5 %collective-permute-start.11 = (bf16[384,384]{1,0:T(8,128)(2,1)S(1)}, bf16[384,384]{1,0:T(8,128)(2,1)}, u32[]{:S(2)}, u32[]{:S(2)}) collective-permute-start(bf16[384,384]{1,0:T(8,128)(2,1)S(1)} %get-tuple-element.19.w0), channel_id=1, source_target_pairs={{0,4},{4,0},{8,12},{12,8},{1,5},{5,1},{9,13},{13,9},{2,6},{6,2},{1... | collective-permute-start | bytes 884744 | tf_op jit(solution)/shard_map/ppermute | solution.py:288
  88.5 0.7 copy-start
  89.3 19.4 %collective-permute-start.13 = (bf16[384,384]{1,0:T(8,128)(2,1)S(1)}, bf16[384,384]{1,0:T(8,128)(2,1)}, u32[]{:S(2)}, u32[]{:S(2)}) collective-permute-start(bf16[384,384]{1,0:T(8,128)(2,1)S(1)} %get-tuple-element.19.w0), channel_id=1, source_target_pairs={{4,8},{8,4},{5,9},{9,5},{6,10},{10,6},{7,11},{11,7},{20,24},{24,20... | collective-permute-start | bytes 884744 | tf_op jit(solution)/shard_map/ppermute | solution.py:322
  102.9 11.0 %collective-permute-start.14 = (bf16[384,384]{1,0:T(8,128)(2,1)}, bf16[384,384]{1,0:T(8,128)(2,1)}, u32[]{:S(2)}, u32[]{:S(2)}) collective-permute-start(bf16[384,384]{1,0:T(8,128)(2,1)} %collective-permute-done.12.w2), channel_id=1, source_target_pairs={{4,0},{8,12},{5,1},{9,13},{6,2},{10,14},{7,3},{11,15},{20,16},{24,... | collective-permute-start | bytes 884744 | tf_op jit(solution)/shard_map/ppermute | solution.py:323
  104.2 1.0 copy-start.1
  107.1 10.6 %copy-start.9 = (f32[768]{0:T(1024)S(1)}, f32[768]{0:T(1024)}, u32[]{:S(2)}) copy-start(f32[768]{0:T(1024)} %param.15) | copy-start | bytes 9220
  107.1 10.6 %copy-start.2 = (bf16[384,384]{1,0:T(8,128)(2,1)S(1)}, bf16[384,384]{1,0:T(8,128)(2,1)}, u32[]{:S(2)}) copy-start(bf16[384,384]{1,0:T(8,128)(2,1)} %copy-done) | copy-start | bytes 884740
  107.1 14.9 %collective-permute-start.20 = (bf16[384,384]{1,0:T(8,128)(2,1)S(1)}, bf16[384,384]{1,0:T(8,128)(2,1)S(1)}, u32[]{:S(2)}, u32[]{:S(2)}) collective-permute-start(bf16[384,384]{1,0:T(8,128)(2,1)S(1)} %shard_map.88), channel_id=1, source_target_pairs={{0,16},{16,0},{1,17},{17,1},{2,18},{18,2},{3,19},{19,3},{4,20},{20... | collective-permute-start | bytes 884744 | tf_op jit(solution)/shard_map/ppermute | solution.py:279
  116.2 7.9 %collective-permute-start.15 = (bf16[384,384]{1,0:T(8,128)(2,1)S(1)}, bf16[384,384]{1,0:T(8,128)(2,1)S(1)}, u32[]{:S(2)}, u32[]{:S(2)}) collective-permute-start(bf16[384,384]{1,0:T(8,128)(2,1)S(1)} %shard_map.86), channel_id=1, source_target_pairs={{0,16},{16,0},{1,17},{17,1},{2,18},{18,2},{3,19},{19,3},{4,20},{20... | collective-permute-start | bytes 884744 | tf_op jit(solution)/shard_map/ppermute | solution.py:279
  119.7 4.4 %copy-start.8 = (bf16[384,768]{1,0:T(8,128)(2,1)S(1)}, bf16[384,768]{1,0:T(8,128)(2,1)}, u32[]{:S(2)}) copy-start(bf16[384,768]{1,0:T(8,128)(2,1)} %param.8) | copy-start | bytes 1769476
  119.8 4.4 %copy-start.10 = (bf16[384,768]{1,0:T(8,128)(2,1)S(1)}, bf16[384,768]{1,0:T(8,128)(2,1)}, u32[]{:S(2)}) copy-start(bf16[384,768]{1,0:T(8,128)(2,1)} %custom-call) | copy-start | bytes 1769476
  124.4 0.8 copy-start.11

commit v2 on v0

--- a/solution.py
+++ b/solution.py
@@ -1,8 +1,11 @@
+import functools
 import math
 
 import jax
 import jax.numpy as jnp
 from jax import lax
+from jax.experimental import pallas as pl
+from jax.experimental.pallas import tpu as pltpu
 from jax.sharding import PartitionSpec as P
 
 EPSILON = 1e-06
@@ -94,6 +97,319 @@
     return (stream.astype(jnp.float32) + gate * projected).astype(jnp.bfloat16)
 
 
+ABSENT = 1e30
+LOG2_E = 1.4426950408889634
+MIB = 1 << 20
+CHUNKS = 2
+FIRST_VMEM = 60 * MIB
+LAST_VMEM = 16 * MIB
+
+
+def vmem_spec():
+    return pl.BlockSpec(memory_space=pltpu.VMEM)
+
+
+def hbm_spec():
+    return pl.BlockSpec(memory_space=pltpu.HBM)
+
+
+def prep_kernel(
+    q_hbm, k_hbm, v_hbm, qg_hbm, kg_hbm, w_hbm, kv_send, kvw_keep, q_send, q_keep, *rest
+):
+    q_ref, k_ref, v_ref, qg_ref, kg_ref, sems = rest
+    mine = lax.axis_index("seq")
+    half = q_keep.shape[1]
+    head_size = qg_ref.shape[1]
+    count = half // head_size
+    rows = pl.ds(pl.multiple_of(mine * half, half), half)
+    moved = [(kg_hbm, kg_ref), (k_hbm, k_ref), (v_hbm, v_ref), (qg_hbm, qg_ref), (q_hbm, q_ref)]
+    for index in range(2):
+        moved.append((w_hbm.at[rows, index * half : (index + 1) * half], kvw_keep.at[2 + index]))
+    copies = [
+        pltpu.make_async_copy(source, target, sems.at[index]) for index, (source, target) in enumerate(moved)
+    ]
+    for copy in copies:
+        copy.start()
+
+    def normed(ref, gain_ref, part, out):
+        for index in range(count):
+            start = pl.multiple_of(part * half + index * head_size, head_size)
+            x = ref[:, pl.ds(start, head_size)].astype(jnp.float32)
+            mean_square = jnp.mean(x * x, axis=-1, keepdims=True)
+            gain = gain_ref[pl.ds(part * count + index, 1), :]
+            scaled = x * lax.rsqrt(mean_square + EPSILON) * gain
+            out[:, index * head_size : (index + 1) * head_size] = scaled.astype(jnp.bfloat16)
+
+    halves = ((1 - mine, kv_send, q_send), (mine, kvw_keep, q_keep))
+    copies[0].wait()
+    copies[1].wait()
+    for part, kv_out, _ in halves:
+        normed(k_ref, kg_ref, part, kv_out.at[0])
+    copies[2].wait()
+    for part, kv_out, _ in halves:
+        kv_out[1] = v_ref[:, pl.ds(pl.multiple_of(part * half, half), half)]
+    copies[3].wait()
+    copies[4].wait()
+    for part, _, q_out in halves:
+        normed(q_ref, qg_ref, part, q_out)
+    for copy in copies[5:]:
+        copy.wait()
+
+
+def prep(q, k, v, q_gain, k_gain, out_weight):
+    rows, width = q.shape
+    half = width // 2
+    one = jax.ShapeDtypeStruct((rows, half), jnp.bfloat16)
+    two = jax.ShapeDtypeStruct((2, rows, half), jnp.bfloat16)
+    four = jax.ShapeDtypeStruct((4, rows, half), jnp.bfloat16)
+    block = pltpu.VMEM((rows, width), jnp.bfloat16)
+    gain = pltpu.VMEM(q_gain.shape, jnp.float32)
+    return pl.pallas_call(
+        prep_kernel,
+        out_shape=[two, four, one, one],
+        in_specs=[hbm_spec()] * 6,
+        out_specs=[vmem_spec()] * 4,
+        scratch_shapes=[block, block, block, gain, gain, pltpu.SemaphoreType.DMA((7,))],
+        compiler_params=pltpu.CompilerParams(vmem_limit_bytes=FIRST_VMEM),
+        cost_estimate=pl.CostEstimate(flops=rows * width * 16, bytes_accessed=rows * width * 12, transcendentals=0),
+    )(q, k, v, q_gain, k_gain, out_weight)
+
+
+def attend_kernel(scale, first, head_size, times, *refs):
+    queries, refs = refs[: len(times)], refs[len(times) :]
+    kv0, kv1, kv2 = refs[:3]
+    refs = refs[3:]
+    height = lax.axis_index("row")
+    flags = [None, None, (height > 0) & (height < lax.axis_size("row") - 1)]
+    rows = kv0.shape[1]
+    factor = scale * LOG2_E
+    ones = jnp.ones((rows, head_size), jnp.bfloat16)
+
+    def head(index, unused):
+        columns = pl.ds(pl.multiple_of(index * head_size, head_size), head_size)
+        keys = [kv[0, :, columns] for kv in (kv0, kv1, kv2)]
+        values = [jnp.concatenate([kv[1, :, columns], ones], axis=1) for kv in (kv0, kv1, kv2)]
+        for which, q_ref in zip(times, queries):
+            q = q_ref[:, columns]
+            scores = [
+                lax.dot_general(q, key, (((1,), (1,)), ((), ())), preferred_element_type=jnp.float32)
+                for key in keys
+            ]
+            top = None
+            for flag, score in zip(flags, scores):
+                part = score[:, :head_size]
+                for start in range(head_size, rows, head_size):
+                    part = jnp.maximum(part, score[:, start : start + head_size])
+                if flag is not None:
+                    part = jnp.where(flag, part, NEGATIVE_FLOOR)
+                top = part if top is None else jnp.maximum(top, part)
+            top = jnp.max(top, axis=1, keepdims=True)
+            total = None
+            if not first:
+                m_in, acc_in = refs[:2]
+                before = m_in[index, which][:, :1]
+                top = jnp.maximum(before, top)
+                total = acc_in[index, which] * jnp.exp2((before - top) * factor)
+            for flag, score, value in zip(flags, scores, values):
+                shift = top if flag is None else jnp.where(flag, top, ABSENT)
+                weights = jnp.exp2((score - shift) * factor).astype(jnp.bfloat16)
+                term = jnp.dot(weights, value, preferred_element_type=jnp.float32)
+                total = term if total is None else total + term
+            if first:
+                m_out, acc_out = refs
+                m_out[index, which] = jnp.broadcast_to(top, (rows, head_size))
+                acc_out[index, which] = total
+            else:
+                out = refs[2]
+                out[:, columns] = (total[:, :head_size] / total[:, head_size:]).astype(jnp.bfloat16)
+        return unused
+
+    lax.fori_loop(0, queries[0].shape[1] // head_size, head, 0)
+
+
+def attend(times, queries, layers, head_size, carry=None):
+    rows, width = queries[0].shape
+    heads = width // head_size
+    vmem = pl.BlockSpec(memory_space=pltpu.VMEM)
+    arguments = [*queries, *layers]
+    if carry is None:
+        out_shape = [
+            jax.ShapeDtypeStruct((heads, 2, rows, head_size), jnp.float32),
+            jax.ShapeDtypeStruct((heads, 2, rows, 2 * head_size), jnp.float32),
+        ]
+        out_specs = [vmem, vmem]
+    else:
+        arguments += list(carry)
+        out_shape = jax.ShapeDtypeStruct((rows, width), jnp.bfloat16)
+        out_specs = vmem
+    return pl.pallas_call(
+        functools.partial(attend_kernel, 1.0 / math.sqrt(head_size), carry is None, head_size, times),
+        out_shape=out_shape,
+        in_specs=[vmem] * len(arguments),
+        out_specs=out_specs,
+        compiler_params=pltpu.CompilerParams(vmem_limit_bytes=16 * MIB),
+        cost_estimate=pl.CostEstimate(
+            flops=heads * len(times) * rows * 3 * rows * head_size * 8,
+            bytes_accessed=8 * MIB,
+            transcendentals=heads * len(times) * rows * 3 * rows,
+        ),
+    )(*arguments)
+
+
+def plane_sum(pieces, weights, spans, write):
+    shift = lax.axis_index("row") ^ lax.axis_index("col")
+    for case in range(4):
+
+        @pl.when(shift == case)
+        def _(case=case):
+            for part, (low, high) in enumerate(spans):
+                total = None
+                for index, piece in enumerate(pieces):
+                    term = jnp.dot(piece, weights(index ^ case, part, low, high), preferred_element_type=jnp.float32)
+                    total = term if total is None else total + term
+                write(part, low, high, total)
+
+
+def weight_of(kvw, kvw_pair, kvw_mid, second, third, which, part):
+    if which == 2:
+        return second[part][0][...] + second[part][1][...]
+    if which == 3:
+        return kvw_mid[2 + part] + third[part][...]
+    return (kvw, kvw_pair)[which][2 + part]
+
+
+def peer_kernel(part, a0, a1, a2, a3, kvw, kvw_pair, kvw_mid, s0, s1, t0, out):
+    def write(unused, low, high, total):
+        out[...] = total.astype(out.dtype)
+
+    def weights(which, unused, low, high):
+        return weight_of(kvw, kvw_pair, kvw_mid, {part: (s0, s1)}, {part: t0}, which, part)
+
+    plane_sum([a[...] for a in (a0, a1, a2, a3)], weights, [(0, out.shape[1])], write)
+
+
+def own_kernel(spans, a0, a1, a2, a3, kvw, kvw_pair, kvw_mid, gate, stream_hbm, *rest):
+    second, third = (rest[0:2], rest[3:5]), (rest[2], rest[5])
+    out, stream, sem = rest[6:]
+    copy = pltpu.make_async_copy(stream_hbm, stream, sem)
+    copy.start()
+    copy.wait()
+
+    def write(part, low, high, total):
+        out[:, low:high] = stream[:, low:high].astype(jnp.float32) + gate[:, low:high] * total
+
+    def weights(which, part, low, high):
+        return weight_of(kvw, kvw_pair, kvw_mid, second, third, which, part)
+
+    plane_sum([a[...] for a in (a0, a1, a2, a3)], weights, spans, write)
+
+
+def final_kernel(spans, base, gate, *rest):
+    received, out_hbm, out, sems = rest[:-3], rest[-3], rest[-2], rest[-1]
+    copies = []
+    for part, (low, high) in enumerate(spans):
+        total = base[:, low:high] + gate[:, low:high] * received[part][...].astype(jnp.float32)
+        out[:, low:high] = total.astype(out.dtype)
+        copies.append(pltpu.make_async_copy(out.at[:, low:high], out_hbm.at[:, low:high], sems.at[part]))
+        copies[-1].start()
+    for copy in copies:
+        copy.wait()
+
+
+def pair_body(stream, query_input, key_input, value_input, q_gain, k_gain, out_weight, gate):
+    head_size = q_gain.shape[1]
+    tokens, width = stream.shape
+    rows = lax.axis_size("row")
+    spans = [(width * i // CHUNKS, width * (i + 1) // CHUNKS) for i in range(CHUNKS)]
+
+    def swap(x):
+        return lax.ppermute(x, "seq", [(0, 1), (1, 0)])
+
+    def pair(x):
+        return lax.ppermute(x, "row", [(i, i ^ 1) for i in range(4)])
+
+    def middle(x):
+        return lax.ppermute(x, "row", [(1, 2), (2, 1)])
+
+    def along(x, axis, mask):
+        return lax.ppermute(x, axis, [(i, i ^ mask) for i in range(4)])
+
+    def call(kernel, arguments, specs, out_shape, out_spec, scratch, flops):
+        return pl.pallas_call(
+            kernel,
+            out_shape=out_shape,
+            in_specs=specs,
+            out_specs=out_spec,
+            scratch_shapes=scratch,
+            compiler_params=pltpu.CompilerParams(vmem_limit_bytes=LAST_VMEM),
+            cost_estimate=pl.CostEstimate(flops=flops, bytes_accessed=2 * MIB, transcendentals=0),
+        )(*arguments)
+
+    def inward(x):
+        return lax.ppermute(x, "row", [(1, 0), (2, 3)])
+
+    barrier = lax.optimization_barrier
+    kv_send, kvw, q_send, q_keep = prep(query_input, key_input, value_input, q_gain, k_gain, out_weight)
+    kv_peer = swap(kv_send)
+    kvw_pair, kvw_mid = pair(kvw), middle(kvw)
+    q_peer = swap(q_send)
+    peer_pair, peer_mid = pair(kv_peer), middle(kv_peer)
+
+    carry = attend((0, 1), [q_keep, q_peer], [kvw, kvw_pair, kvw_mid], head_size)
+    first_pair, first_mid, carry = barrier((kvw_pair[2], kvw_mid[2], carry))
+    forward = [middle(first_pair)]
+    second = [inward(first_mid)]
+    layers = [kv_peer, peer_pair, peer_mid]
+    theirs = attend((1,), [q_peer], layers, head_size, carry)
+    theirs, forward[0] = barrier((theirs, forward[0]))
+    across_theirs, beside_theirs = along(theirs, "col", 2), along(theirs, "col", 1)
+    third = [inward(forward[0])]
+    next_pair, next_mid, carry = barrier((kvw_pair[3], kvw_mid[3], carry, theirs))[:3]
+    forward.append(middle(next_pair))
+    second.append(inward(next_mid))
+    third.append(inward(forward[1]))
+    mine = attend((0,), [q_keep], layers, head_size, carry)
+    across_mine, beside_mine = along(mine, "col", 2), along(mine, "col", 1)
+    weights = [[forward[part], second[part], third[part]] for part in range(2)]
+
+    gate = gate.reshape(1, width)
+    vmem, hbm = vmem_spec(), hbm_spec()
+    groups = [theirs, beside_theirs, across_theirs, along(across_theirs, "col", 1)]
+    received = []
+    for part, (low, high) in enumerate(spans):
+        sent = call(
+            functools.partial(peer_kernel, part),
+            [*groups, kvw, kvw_pair, kvw_mid, *weights[part]],
+            [vmem] * 10,
+            jax.ShapeDtypeStruct((tokens, high - low), jnp.bfloat16),
+            vmem,
+            [],
+            tokens * width * (high - low) * 4,
+        )
+        if part == 0:
+            sent, groups[0] = barrier((sent, groups[0]))
+        received.append(swap(sent))
+    groups = [mine, beside_mine, across_mine, along(across_mine, "col", 1)]
+    base = call(
+        functools.partial(own_kernel, spans),
+        [*groups, kvw, kvw_pair, kvw_mid, gate, stream, *weights[0], *weights[1]],
+        [vmem] * 8 + [hbm] + [vmem] * 6,
+        jax.ShapeDtypeStruct((tokens, width), jnp.float32),
+        vmem,
+        [pltpu.VMEM((tokens, width), stream.dtype), pltpu.SemaphoreType.DMA(())],
+        tokens * width * width * 4,
+    )
+    return call(
+        functools.partial(final_kernel, spans),
+        [base, gate, *received],
+        [vmem] * (2 + CHUNKS),
+        jax.ShapeDtypeStruct((tokens, width), jnp.bfloat16),
+        hbm,
+        [pltpu.VMEM((tokens, width), jnp.bfloat16), pltpu.SemaphoreType.DMA((CHUNKS,))],
+        tokens * width * 4,
+    )
+
+
 def solution(mesh):
     placed = (
         P(("seq", "row"), "col"),
@@ -105,6 +421,8 @@
         P("row", "col"),
         P("col"),
     )
+    shape = mesh.shape
+    paired = shape["seq"] == 2 and shape["row"] == 4 and shape["col"] == 4
     return jax.shard_map(
-        body, mesh=mesh, in_specs=placed, out_specs=P(("seq", "row"), "col"), check_vma=False
-    )
+        pair_body if paired else body, mesh=mesh, in_specs=placed, out_specs=P(("seq", "row"), "col"), check_vma=False
+    )

time: 274 us -> 95.6 us (0.35)
  waiting for transfers between devices: 203 us -> 49.8 us
  Pallas kernels: 0 us -> 21.6 us
  matrix products: 20.4 us -> 0 us
  other arithmetic: 16.1 us -> 0 us
  between operations: 13.9 us -> 0.41 us
  starting transfers between devices: 14.6 us -> 23.4 us
  local copies, waits for them, and re-layouts: 6.02 us -> 0.14 us
    ppermute x4 -> x20, waiting for transfers between devices: 172 us -> 49.8 us  [the longest x4 18.8 us: swap(): return lax.ppermute(x, 'seq', [(0, 1), (1, 0)])]
    all_gather x2 -> x0, waiting for transfers between devices: 30.4 us -> none  [the longest x1 30.4 us: body(): all_heads = lax.all_gather(attention, 'col', axis=1, tiled=True)]
    pallas_call x0 -> x8, Pallas kernels: none -> 21.6 us  [the longest x3 13.3 us: attend(): pl.pallas_call(functools.partial(attend_kernel, 1.0 / math.sqrt(head_size...]
    dot_general x19 -> x0, matrix products: 20.4 us -> none  [the longest x9 7.78 us: layer_terms(): jnp.einsum('hqk,khd->qhd', unnormed, value_rows, preferred_element_type=j...]
    ppermute x4 -> x20, starting transfers between devices: 14.5 us -> 23.4 us  [the longest x2 7.43 us: pair(): return lax.ppermute(x, 'row', [(i, i ^ 1) for i in range(4)])]
    concatenate x2 -> x0, other arithmetic: 7.52 us -> none  [padded_2(): block = jnp.concatenate([low, block, high], axis=dim)]
    reduce_sum x13 -> x0, other arithmetic: 7.19 us -> none  [the longest x9 5.58 us: layer_terms(): layer_sum = jnp.sum(unnormed.astype(jnp.float32), axis=-1)]
    unnamed x35 -> x8, local copies, waits for them, and re-layouts: 3.5 us -> 0.02 us
  transfers between devices with their start and end apart: 6 -> 20, of which waited for: 4 -> 9; matrix products, arithmetic and copies ran while one was open for 11% -> 0% of each run, Pallas kernels for 0% -> 18%
where the time goes in v2:
time: 95.6 us; the launch traced here: 95.3 us
  waiting for transfers between devices  49.8 us (52%)
  starting transfers between devices  23.4 us (24%)
  Pallas kernels  21.6 us (23%)
    ppermute x4, waiting for transfers between devices, swap(): return lax.ppermute(x, 'seq', [(0, 1), (1, 0)])  18.8 us
    ppermute x4, waiting for transfers between devices, inward(): return lax.ppermute(x, 'row', [(1, 0), (2, 3)])  15.4 us
    pallas_call x3, Pallas kernels, attend(): pl.pallas_call(functools.partial(attend_kernel, 1.0 / math.sqrt(head_size...  13.3 us
    ppermute x2, waiting for transfers between devices, pair(): return lax.ppermute(x, 'row', [(i, i ^ 1) for i in range(4)])  9.51 us
    ppermute x2, starting transfers between devices, pair(): return lax.ppermute(x, 'row', [(i, i ^ 1) for i in range(4)])  7.43 us
    ppermute x6, waiting for transfers between devices, along(): return lax.ppermute(x, axis, [(i, i ^ mask) for i in range(4)])  6.14 us
    ppermute x4, starting transfers between devices, swap(): return lax.ppermute(x, 'seq', [(0, 1), (1, 0)])  5.27 us
    ppermute x4, starting transfers between devices, inward(): return lax.ppermute(x, 'row', [(1, 0), (2, 3)])  5.16 us
  transfers between devices with their start and end apart: 20, of which 9 were waited for; matrix products, arithmetic and copies ran while one was open for 0% of the time, Pallas kernels for 18%

profile of v2, /device:TPU:0, one launch (start us, length us, event | category | flops | bytes accessed | tf_op | source)
XLA Modules:
  0.0 95.3 jit_solution(3938815111088926620)
XLA Ops:
  0.0 3.4 %shard_map.82 = (bf16[2,384,384]{2,1,0:T(8,128)(2,1)}, bf16[4,384,384]{2,1,0:T(8,128)(2,1)}, bf16[384,384]{1,0:T(8,128)(2,1)}, bf16[384,384]{1,0:T(8,128)(2,1)}) custom-call(bf16[384,768]{1,0:T(8,128)(2,1)} %q_hbm.1, bf16[384,768]{1,0:T(8,128)(2,1)} %k_hbm.1, bf16[384,768]{1,0:T(8,128)(2,1)} %v_hbm.1, f32[6,128]{1,0:T(8,128)} %qg_hbm.1, f32[6,128]{1,0:T(8,128)} %kg_hbm.1, ...), custom_call_target="tpu_custom_call" | custom-call | flops 4718592 | bytes 3538944 | tf_op jit(solution)/shard_map/pallas_call | solution.py:167
  3.4 3.1 %collective-permute-start.3 = (bf16[4,384,384]{2,1,0:T(8,128)(2,1)}, bf16[4,384,384]{2,1,0:T(8,128)(2,1)S(1)}, u32[]{:S(2)}, u32[]{:S(2)}) collective-permute-start(bf16[4,384,384]{2,1,0:T(8,128)(2,1)} %get-tuple-element.25.refs_2_.kvw), channel_id=1, source_target_pairs={{0,4},{4,0},{8,12},{12,8},{1,5},{5,1},{9,13},{13,9},{2,6},{6,2},{1... | collective-permute-start | bytes 3538952 | tf_op jit(solution)/shard_map/ppermute | solution.py:329
  6.5 0.7 collective-permute-start.4
  7.2 1.6 %collective-permute-start = (bf16[2,384,384]{2,1,0:T(8,128)(2,1)}, bf16[2,384,384]{2,1,0:T(8,128)(2,1)S(1)}, u32[]{:S(2)}, u32[]{:S(2)}) collective-permute-start(bf16[2,384,384]{2,1,0:T(8,128)(2,1)} %get-tuple-element.24), channel_id=1, source_target_pairs={{0,16},{16,0},{1,17},{17,1},{2,18},{18,2},{3,19},{19,3},{4,20},{20... | collective-permute-start | bytes 1769480 | tf_op jit(solution)/shard_map/ppermute | solution.py:326
  8.8 0.5 collective-permute-start.5
  9.3 14.4 %collective-permute-done.refs_1_ = bf16[2,384,384]{2,1,0:T(8,128)(2,1)S(1)} collective-permute-done((bf16[2,384,384]{2,1,0:T(8,128)(2,1)}, bf16[2,384,384]{2,1,0:T(8,128)(2,1)S(1)}, u32[]{:S(2)}, u32[]{:S(2)}) %collective-permute-start) | collective-permute-done | bytes 589856 | tf_op jit(solution)/shard_map/ppermute | solution.py:326
  23.7 4.3 %collective-permute-start.1 = (bf16[2,384,384]{2,1,0:T(8,128)(2,1)S(1)}, bf16[2,384,384]{2,1,0:T(8,128)(2,1)S(1)}, u32[]{:S(2)}, u32[]{:S(2)}) collective-permute-start(bf16[2,384,384]{2,1,0:T(8,128)(2,1)S(1)} %collective-permute-done.refs_1_), channel_id=1, source_target_pairs={{0,4},{4,0},{8,12},{12,8},{1,5},{5,1},{9,13},{13,9},{2,6},{6,2},{1... | collective-permute-start | bytes 1769480 | tf_op jit(solution)/shard_map/ppermute | solution.py:329
  28.1 0.7 collective-permute-start.2
  28.8 4.7 %collective-permute-done.3.refs_3_.kvw_pair = bf16[4,384,384]{2,1,0:T(8,128)(2,1)S(1)} collective-permute-done((bf16[4,384,384]{2,1,0:T(8,128)(2,1)}, bf16[4,384,384]{2,1,0:T(8,128)(2,1)S(1)}, u32[]{:S(2)}, u32[]{:S(2)}) %collective-permute-start.3) | collective-permute-done | bytes 1179680 | tf_op jit(solution)/shard_map/ppermute | solution.py:329
  33.5 0.1 slice_bitcast_fusion.1
  33.5 0.0 collective-permute-done.4.refs_4_.kvw_mid
  33.5 0.1 slice_bitcast_fusion
  33.6 4.8 %shard_map.83 = (f32[3,2,384,128]{3,2,1,0:T(8,128)S(1)}, f32[3,2,384,256]{3,2,1,0:T(8,128)S(1)}) custom-call(bf16[384,384]{1,0:T(8,128)(2,1)S(1)} %copy-done.2, bf16[384,384]{1,0:T(8,128)(2,1)S(1)} %collective-permute-done.5.refs_1_.refs_0_, bf16[4,384,384]{2,1,0:T(8,128)(2,1)S(1)} %copy-done, ...), custom_call_target="tpu_custom_call" | custom-call | flops 2717908992 | bytes 8388608 | tf_op jit(solution)/shard_map/pallas_call | solution.py:245
  38.5 0.7 collective-permute-start.6
  39.2 1.3 %collective-permute-start.10 = (bf16[384,384]{1,0:T(8,128)(2,1)S(1)}, bf16[384,384]{1,0:T(8,128)(2,1)S(1)}, u32[]{:S(2)}, u32[]{:S(2)}) collective-permute-start(bf16[384,384]{1,0:T(8,128)(2,1)S(1)} %get-tuple-element.36), channel_id=1, source_target_pairs={{4,0},{8,12},{5,1},{9,13},{6,2},{10,14},{7,3},{11,15},{20,16},{24,... | collective-permute-start | bytes 884744 | tf_op jit(solution)/shard_map/ppermute | solution.py:349
  40.5 4.8 %collective-permute-done.1.refs_2_ = bf16[2,384,384]{2,1,0:T(8,128)(2,1)S(1)} collective-permute-done((bf16[2,384,384]{2,1,0:T(8,128)(2,1)S(1)}, bf16[2,384,384]{2,1,0:T(8,128)(2,1)S(1)}, u32[]{:S(2)}, u32[]{:S(2)}) %collective-permute-start.1) | collective-permute-done | bytes 589856 | tf_op jit(solution)/shard_map/ppermute | solution.py:329
  45.3 0.0 collective-permute-done.2.refs_3_
  45.3 4.2 %shard_map.84.a0 = bf16[384,384]{1,0:T(8,128)(2,1)S(1)} custom-call(bf16[384,384]{1,0:T(8,128)(2,1)S(1)} %collective-permute-done.5.refs_1_.refs_0_, bf16[2,384,384]{2,1,0:T(8,128)(2,1)S(1)} %collective-permute-done.refs_1_, bf16[2,384,384]{2,1,0:T(8,128)(2,1)S(1)} %collective-permute-done.1.refs_2_, ...), custom_call_target="tpu_custom_call" | custom-call | flops 1358954496 | bytes 8388608 | tf_op jit(solution)/shard_map/pallas_call | solution.py:245
  49.5 1.7 %collective-permute-start.16 = (bf16[384,384]{1,0:T(8,128)(2,1)S(1)}, bf16[384,384]{1,0:T(8,128)(2,1)S(1)}, u32[]{:S(2)}, u32[]{:S(2)}) collective-permute-start(bf16[384,384]{1,0:T(8,128)(2,1)S(1)} %shard_map.84.a0), channel_id=1, source_target_pairs={{0,2},{1,3},{2,0},{3,1},{4,6},{5,7},{6,4},{7,5},{8,10},{9,11},{10,... | collective-permute-start | bytes 884744 | tf_op jit(solution)/shard_map/ppermute | solution.py:335
  51.2 4.2 %shard_map.85.a0 = bf16[384,384]{1,0:T(8,128)(2,1)S(1)} custom-call(bf16[384,384]{1,0:T(8,128)(2,1)S(1)} %copy-done.2, bf16[2,384,384]{2,1,0:T(8,128)(2,1)S(1)} %collective-permute-done.refs_1_, bf16[2,384,384]{2,1,0:T(8,128)(2,1)S(1)} %collective-permute-done.1.refs_2_, bf16[2,384,384]{2,1,0:T(8,128)(2,1)S(1)} %collective-permute-done.2.refs_3_, ...), custom_call_target="tpu_custom_call" | custom-call | flops 1358954496 | bytes 8388608 | tf_op jit(solution)/shard_map/pallas_call | solution.py:245
  55.5 0.4 collective-permute-start.8
  55.9 0.7 collective-permute-start.12
  56.6 1.3 %collective-permute-start.11 = (bf16[384,384]{1,0:T(8,128)(2,1)S(1)}, bf16[384,384]{1,0:T(8,128)(2,1)S(1)}, u32[]{:S(2)}, u32[]{:S(2)}) collective-permute-start(bf16[384,384]{1,0:T(8,128)(2,1)S(1)} %collective-permute-done.6.rest_0_.s0), channel_id=1, source_target_pairs={{4,0},{8,12},{5,1},{9,13},{6,2},{10,14},{7,3},{11,15},{20,16},{24,... | collective-permute-start | bytes 884744 | tf_op jit(solution)/shard_map/ppermute | solution.py:349
  57.9 0.0 collective-permute-done.10.rest_1_.s1
  57.9 0.1 collective-permute-start.15
  58.0 0.7 collective-permute-done.16.a2
  58.7 0.0 collective-permute-start.17
  58.7 5.4 %collective-permute-done.8.a2 = bf16[384,384]{1,0:T(8,128)(2,1)S(1)} collective-permute-done((bf16[384,384]{1,0:T(8,128)(2,1)S(1)}, bf16[384,384]{1,0:T(8,128)(2,1)S(1)}, u32[]{:S(2)}, u32[]{:S(2)}) %collective-permute-start.8) | collective-permute-done | bytes 294944 | tf_op jit(solution)/shard_map/ppermute | solution.py:335
  64.1 1.3 %collective-permute-start.13 = (bf16[384,384]{1,0:T(8,128)(2,1)S(1)}, bf16[384,384]{1,0:T(8,128)(2,1)S(1)}, u32[]{:S(2)}, u32[]{:S(2)}) collective-permute-start(bf16[384,384]{1,0:T(8,128)(2,1)S(1)} %get-tuple-element.38), channel_id=1, source_target_pairs={{4,0},{8,12},{5,1},{9,13},{6,2},{10,14},{7,3},{11,15},{20,16},{24,... | collective-permute-start | bytes 884744 | tf_op jit(solution)/shard_map/ppermute | solution.py:349
  65.4 1.3 %collective-permute-start.14 = (bf16[384,384]{1,0:T(8,128)(2,1)S(1)}, bf16[384,384]{1,0:T(8,128)(2,1)S(1)}, u32[]{:S(2)}, u32[]{:S(2)}) collective-permute-start(bf16[384,384]{1,0:T(8,128)(2,1)S(1)} %collective-permute-done.12.rest_3_.s0), channel_id=1, source_target_pairs={{4,0},{8,12},{5,1},{9,13},{6,2},{10,14},{7,3},{11,15},{20,16},{24,... | collective-permute-start | bytes 884744 | tf_op jit(solution)/shard_map/ppermute | solution.py:349
  66.7 7.1 %collective-permute-done.11.rest_2_.t0 = bf16[384,384]{1,0:T(8,128)(2,1)S(1)} collective-permute-done((bf16[384,384]{1,0:T(8,128)(2,1)S(1)}, bf16[384,384]{1,0:T(8,128)(2,1)S(1)}, u32[]{:S(2)}, u32[]{:S(2)}) %collective-permute-start.11) | collective-permute-done | bytes 294944 | tf_op jit(solution)/shard_map/ppermute | solution.py:349
  73.8 0.0 collective-permute-start.7
  73.8 0.0 collective-permute-done.15.a1
  73.8 0.5 collective-permute-start.9
  74.3 0.0 collective-permute-done.17.a3
  74.3 1.0 %shard_map.87 = bf16[384,384]{1,0:T(8,128)(2,1)S(1)} custom-call(bf16[384,384]{1,0:T(8,128)(2,1)S(1)} %shard_map.84.a0, bf16[384,384]{1,0:T(8,128)(2,1)S(1)} %collective-permute-done.15.a1, bf16[384,384]{1,0:T(8,128)(2,1)S(1)} %collective-permute-done.16.a2, bf16[384,384]{1,0:T(8,128)(2,1)S(1)} %collective-permute-done.17.a3, ...), custom_call_target="tpu_custom_call" | custom-call | flops 452984832 | bytes 2097152 | tf_op jit(solution)/shard_map/pallas_call | solution.py:338
  75.3 0.0 copy-start.3
  75.3 0.0 copy-start.1
  75.3 1.6 %collective-permute-start.18 = (bf16[384,384]{1,0:T(8,128)(2,1)S(1)}, bf16[384,384]{1,0:T(8,128)(2,1)S(1)}, u32[]{:S(2)}, u32[]{:S(2)}) collective-permute-start(bf16[384,384]{1,0:T(8,128)(2,1)S(1)} %shard_map.87), channel_id=1, source_target_pairs={{0,16},{16,0},{1,17},{17,1},{2,18},{18,2},{3,19},{19,3},{4,20},{20... | collective-permute-start | bytes 884744 | tf_op jit(solution)/shard_map/ppermute | solution.py:326
  76.9 3.2 %collective-permute-done.13.rest_4_.s1 = bf16[384,384]{1,0:T(8,128)(2,1)S(1)} collective-permute-done((bf16[384,384]{1,0:T(8,128)(2,1)S(1)}, bf16[384,384]{1,0:T(8,128)(2,1)S(1)}, u32[]{:S(2)}, u32[]{:S(2)}) %collective-permute-start.13) | collective-permute-done | bytes 294944 | tf_op jit(solution)/shard_map/ppermute | solution.py:349
  80.1 5.1 %collective-permute-done.14.rest_5_.t0 = bf16[384,384]{1,0:T(8,128)(2,1)S(1)} collective-permute-done((bf16[384,384]{1,0:T(8,128)(2,1)S(1)}, bf16[384,384]{1,0:T(8,128)(2,1)S(1)}, u32[]{:S(2)}, u32[]{:S(2)}) %collective-permute-start.14) | collective-permute-done | bytes 294944 | tf_op jit(solution)/shard_map/ppermute | solution.py:349
  85.2 1.2 %shard_map.88 = bf16[384,384]{1,0:T(8,128)(2,1)S(1)} custom-call(bf16[384,384]{1,0:T(8,128)(2,1)S(1)} %shard_map.84.a0, bf16[384,384]{1,0:T(8,128)(2,1)S(1)} %collective-permute-done.15.a1, bf16[384,384]{1,0:T(8,128)(2,1)S(1)} %collective-permute-done.16.a2, bf16[384,384]{1,0:T(8,128)(2,1)S(1)} %collective-permute-done.17.a3, ...), custom_call_target="tpu_custom_call" | custom-call | flops 452984832 | bytes 2097152 | tf_op jit(solution)/shard_map/pallas_call | solution.py:338
  86.4 1.6 %collective-permute-start.19 = (bf16[384,384]{1,0:T(8,128)(2,1)S(1)}, bf16[384,384]{1,0:T(8,128)(2,1)S(1)}, u32[]{:S(2)}, u32[]{:S(2)}) collective-permute-start(bf16[384,384]{1,0:T(8,128)(2,1)S(1)} %shard_map.88), channel_id=1, source_target_pairs={{0,16},{16,0},{1,17},{17,1},{2,18},{18,2},{3,19},{19,3},{4,20},{20... | collective-permute-start | bytes 884744 | tf_op jit(solution)/shard_map/ppermute | solution.py:326
  88.0 0.0 collective-permute-done.7.a1
  88.0 0.0 collective-permute-done.9.a3
  88.0 1.9 %shard_map.86.base = f32[384,768]{1,0:T(8,128)S(1)} custom-call(bf16[384,384]{1,0:T(8,128)(2,1)S(1)} %shard_map.85.a0, bf16[384,384]{1,0:T(8,128)(2,1)S(1)} %collective-permute-done.7.a1, bf16[384,384]{1,0:T(8,128)(2,1)S(1)} %collective-permute-done.8.a2, bf16[384,384]{1,0:T(8,128)(2,1)S(1)} %collective-permute-done.9.a3, bf16[4,384,384]{2,1,0:T(8,128)(2,1)S(1)} %copy-done, ...), custom_call_target="tpu_custom_call" | custom-call | flops 905969664 | bytes 2097152 | tf_op jit(solution)/shard_map/pallas_call | solution.py:338
  89.9 4.3 %collective-permute-done.19.rest_1_ = bf16[384,384]{1,0:T(8,128)(2,1)S(1)} collective-permute-done((bf16[384,384]{1,0:T(8,128)(2,1)S(1)}, bf16[384,384]{1,0:T(8,128)(2,1)S(1)}, u32[]{:S(2)}, u32[]{:S(2)}) %collective-permute-start.19) | collective-permute-done | bytes 294944 | tf_op jit(solution)/shard_map/ppermute | solution.py:326
  94.2 0.9 shard_map.89
  (11 shorter events, 0.0 us)
Async XLA Ops:
  3.4 30.1 %collective-permute-start.3 = (bf16[4,384,384]{2,1,0:T(8,128)(2,1)}, bf16[4,384,384]{2,1,0:T(8,128)(2,1)S(1)}, u32[]{:S(2)}, u32[]{:S(2)}) collective-permute-start(bf16[4,384,384]{2,1,0:T(8,128)(2,1)} %get-tuple-element.25.refs_2_.kvw), channel_id=1, source_target_pairs={{0,4},{4,0},{8,12},{12,8},{1,5},{5,1},{9,13},{13,9},{2,6},{6,2},{1... | collective-permute-start | bytes 3538952 | tf_op jit(solution)/shard_map/ppermute | solution.py:329
  6.5 27.1 %collective-permute-start.4 = (bf16[4,384,384]{2,1,0:T(8,128)(2,1)}, bf16[4,384,384]{2,1,0:T(8,128)(2,1)S(1)}, u32[]{:S(2)}, u32[]{:S(2)}) collective-permute-start(bf16[4,384,384]{2,1,0:T(8,128)(2,1)} %get-tuple-element.25.refs_2_.kvw), channel_id=1, source_target_pairs={{4,8},{8,4},{5,9},{9,5},{6,10},{10,6},{7,11},{11,7},{20,24},{24,20... | collective-permute-start | bytes 3538952 | tf_op jit(solution)/shard_map/ppermute | solution.py:332
  7.2 16.5 %collective-permute-start = (bf16[2,384,384]{2,1,0:T(8,128)(2,1)}, bf16[2,384,384]{2,1,0:T(8,128)(2,1)S(1)}, u32[]{:S(2)}, u32[]{:S(2)}) collective-permute-start(bf16[2,384,384]{2,1,0:T(8,128)(2,1)} %get-tuple-element.24), channel_id=1, source_target_pairs={{0,16},{16,0},{1,17},{17,1},{2,18},{18,2},{3,19},{19,3},{4,20},{20... | collective-permute-start | bytes 1769480 | tf_op jit(solution)/shard_map/ppermute | solution.py:326
  8.8 24.8 %copy-start = (bf16[4,384,384]{2,1,0:T(8,128)(2,1)S(1)}, bf16[4,384,384]{2,1,0:T(8,128)(2,1)}, u32[]{:S(2)}) copy-start(bf16[4,384,384]{2,1,0:T(8,128)(2,1)} %get-tuple-element.25.refs_2_.kvw) | copy-start | bytes 3538948
  8.8 24.8 %copy-start.2 = (bf16[384,384]{1,0:T(8,128)(2,1)S(1)}, bf16[384,384]{1,0:T(8,128)(2,1)}, u32[]{:S(2)}) copy-start(bf16[384,384]{1,0:T(8,128)(2,1)} %get-tuple-element.23.refs_0_) | copy-start | bytes 884740
  8.8 24.8 %collective-permute-start.5 = (bf16[384,384]{1,0:T(8,128)(2,1)}, bf16[384,384]{1,0:T(8,128)(2,1)S(1)}, u32[]{:S(2)}, u32[]{:S(2)}) collective-permute-start(bf16[384,384]{1,0:T(8,128)(2,1)} %get-tuple-element.26), channel_id=1, source_target_pairs={{0,16},{16,0},{1,17},{17,1},{2,18},{18,2},{3,19},{19,3},{4,20},{20... | collective-permute-start | bytes 884744 | tf_op jit(solution)/shard_map/ppermute | solution.py:326
  23.7 21.6 %collective-permute-start.1 = (bf16[2,384,384]{2,1,0:T(8,128)(2,1)S(1)}, bf16[2,384,384]{2,1,0:T(8,128)(2,1)S(1)}, u32[]{:S(2)}, u32[]{:S(2)}) collective-permute-start(bf16[2,384,384]{2,1,0:T(8,128)(2,1)S(1)} %collective-permute-done.refs_1_), channel_id=1, source_target_pairs={{0,4},{4,0},{8,12},{12,8},{1,5},{5,1},{9,13},{13,9},{2,6},{6,2},{1... | collective-permute-start | bytes 1769480 | tf_op jit(solution)/shard_map/ppermute | solution.py:329
  28.1 17.2 %collective-permute-start.2 = (bf16[2,384,384]{2,1,0:T(8,128)(2,1)S(1)}, bf16[2,384,384]{2,1,0:T(8,128)(2,1)S(1)}, u32[]{:S(2)}, u32[]{:S(2)}) collective-permute-start(bf16[2,384,384]{2,1,0:T(8,128)(2,1)S(1)} %collective-permute-done.refs_1_), channel_id=1, source_target_pairs={{4,8},{8,4},{5,9},{9,5},{6,10},{10,6},{7,11},{11,7},{20,24},{24,20... | collective-permute-start | bytes 1769480 | tf_op jit(solution)/shard_map/ppermute | solution.py:332
  38.5 11.0 %collective-permute-start.6 = (bf16[384,384]{1,0:T(8,128)(2,1)S(1)}, bf16[384,384]{1,0:T(8,128)(2,1)S(1)}, u32[]{:S(2)}, u32[]{:S(2)}) collective-permute-start(bf16[384,384]{1,0:T(8,128)(2,1)S(1)} %get-tuple-element.31), channel_id=1, source_target_pairs={{4,8},{8,4},{5,9},{9,5},{6,10},{10,6},{7,11},{11,7},{20,24},{24,20... | collective-permute-start | bytes 884744 | tf_op jit(solution)/shard_map/ppermute | solution.py:332
  39.2 18.7 %collective-permute-start.10 = (bf16[384,384]{1,0:T(8,128)(2,1)S(1)}, bf16[384,384]{1,0:T(8,128)(2,1)S(1)}, u32[]{:S(2)}, u32[]{:S(2)}) collective-permute-start(bf16[384,384]{1,0:T(8,128)(2,1)S(1)} %get-tuple-element.36), channel_id=1, source_target_pairs={{4,0},{8,12},{5,1},{9,13},{6,2},{10,14},{7,3},{11,15},{20,16},{24,... | collective-permute-start | bytes 884744 | tf_op jit(solution)/shard_map/ppermute | solution.py:349
  49.5 9.2 %collective-permute-start.16 = (bf16[384,384]{1,0:T(8,128)(2,1)S(1)}, bf16[384,384]{1,0:T(8,128)(2,1)S(1)}, u32[]{:S(2)}, u32[]{:S(2)}) collective-permute-start(bf16[384,384]{1,0:T(8,128)(2,1)S(1)} %shard_map.84.a0), channel_id=1, source_target_pairs={{0,2},{1,3},{2,0},{3,1},{4,6},{5,7},{6,4},{7,5},{8,10},{9,11},{10,... | collective-permute-start | bytes 884744 | tf_op jit(solution)/shard_map/ppermute | solution.py:335
  55.5 8.6 %collective-permute-start.8 = (bf16[384,384]{1,0:T(8,128)(2,1)S(1)}, bf16[384,384]{1,0:T(8,128)(2,1)S(1)}, u32[]{:S(2)}, u32[]{:S(2)}) collective-permute-start(bf16[384,384]{1,0:T(8,128)(2,1)S(1)} %shard_map.85.a0), channel_id=1, source_target_pairs={{0,2},{1,3},{2,0},{3,1},{4,6},{5,7},{6,4},{7,5},{8,10},{9,11},{10,... | collective-permute-start | bytes 884744 | tf_op jit(solution)/shard_map/ppermute | solution.py:335
  55.9 9.5 %collective-permute-start.12 = (bf16[384,384]{1,0:T(8,128)(2,1)S(1)}, bf16[384,384]{1,0:T(8,128)(2,1)S(1)}, u32[]{:S(2)}, u32[]{:S(2)}) collective-permute-start(bf16[384,384]{1,0:T(8,128)(2,1)S(1)} %get-tuple-element.37), channel_id=1, source_target_pairs={{4,8},{8,4},{5,9},{9,5},{6,10},{10,6},{7,11},{11,7},{20,24},{24,20... | collective-permute-start | bytes 884744 | tf_op jit(solution)/shard_map/ppermute | solution.py:332
  56.6 17.2 %collective-permute-start.11 = (bf16[384,384]{1,0:T(8,128)(2,1)S(1)}, bf16[384,384]{1,0:T(8,128)(2,1)S(1)}, u32[]{:S(2)}, u32[]{:S(2)}) collective-permute-start(bf16[384,384]{1,0:T(8,128)(2,1)S(1)} %collective-permute-done.6.rest_0_.s0), channel_id=1, source_target_pairs={{4,0},{8,12},{5,1},{9,13},{6,2},{10,14},{7,3},{11,15},{20,16},{24,... | collective-permute-start | bytes 884744 | tf_op jit(solution)/shard_map/ppermute | solution.py:349
  57.9 15.9 %collective-permute-start.15 = (bf16[384,384]{1,0:T(8,128)(2,1)S(1)}, bf16[384,384]{1,0:T(8,128)(2,1)S(1)}, u32[]{:S(2)}, u32[]{:S(2)}) collective-permute-start(bf16[384,384]{1,0:T(8,128)(2,1)S(1)} %shard_map.84.a0), channel_id=1, source_target_pairs={{0,1},{1,0},{2,3},{3,2},{4,5},{5,4},{6,7},{7,6},{8,9},{9,8},{10,11... | collective-permute-start | bytes 884744 | tf_op jit(solution)/shard_map/ppermute | solution.py:335
  58.7 15.6 %collective-permute-start.17 = (bf16[384,384]{1,0:T(8,128)(2,1)S(1)}, bf16[384,384]{1,0:T(8,128)(2,1)S(1)}, u32[]{:S(2)}, u32[]{:S(2)}) collective-permute-start(bf16[384,384]{1,0:T(8,128)(2,1)S(1)} %collective-permute-done.16.a2), channel_id=1, source_target_pairs={{0,1},{1,0},{2,3},{3,2},{4,5},{5,4},{6,7},{7,6},{8,9},{9,8},{10,11... | collective-permute-start | bytes 884744 | tf_op jit(solution)/shard_map/ppermute | solution.py:335
  64.1 16.0 %collective-permute-start.13 = (bf16[384,384]{1,0:T(8,128)(2,1)S(1)}, bf16[384,384]{1,0:T(8,128)(2,1)S(1)}, u32[]{:S(2)}, u32[]{:S(2)}) collective-permute-start(bf16[384,384]{1,0:T(8,128)(2,1)S(1)} %get-tuple-element.38), channel_id=1, source_target_pairs={{4,0},{8,12},{5,1},{9,13},{6,2},{10,14},{7,3},{11,15},{20,16},{24,... | collective-permute-start | bytes 884744 | tf_op jit(solution)/shard_map/ppermute | solution.py:349
  65.4 19.8 %collective-permute-start.14 = (bf16[384,384]{1,0:T(8,128)(2,1)S(1)}, bf16[384,384]{1,0:T(8,128)(2,1)S(1)}, u32[]{:S(2)}, u32[]{:S(2)}) collective-permute-start(bf16[384,384]{1,0:T(8,128)(2,1)S(1)} %collective-permute-done.12.rest_3_.s0), channel_id=1, source_target_pairs={{4,0},{8,12},{5,1},{9,13},{6,2},{10,14},{7,3},{11,15},{20,16},{24,... | collective-permute-start | bytes 884744 | tf_op jit(solution)/shard_map/ppermute | solution.py:349
  73.8 14.2 %collective-permute-start.7 = (bf16[384,384]{1,0:T(8,128)(2,1)S(1)}, bf16[384,384]{1,0:T(8,128)(2,1)S(1)}, u32[]{:S(2)}, u32[]{:S(2)}) collective-permute-start(bf16[384,384]{1,0:T(8,128)(2,1)S(1)} %shard_map.85.a0), channel_id=1, source_target_pairs={{0,1},{1,0},{2,3},{3,2},{4,5},{5,4},{6,7},{7,6},{8,9},{9,8},{10,11... | collective-permute-start | bytes 884744 | tf_op jit(solution)/shard_map/ppermute | solution.py:335
  73.8 14.2 %collective-permute-start.9 = (bf16[384,384]{1,0:T(8,128)(2,1)S(1)}, bf16[384,384]{1,0:T(8,128)(2,1)S(1)}, u32[]{:S(2)}, u32[]{:S(2)}) collective-permute-start(bf16[384,384]{1,0:T(8,128)(2,1)S(1)} %collective-permute-done.8.a2), channel_id=1, source_target_pairs={{0,1},{1,0},{2,3},{3,2},{4,5},{5,4},{6,7},{7,6},{8,9},{9,8},{10,11... | collective-permute-start | bytes 884744 | tf_op jit(solution)/shard_map/ppermute | solution.py:335
  75.3 12.7 %copy-start.3 = (f32[768]{0:T(1024)S(1)}, f32[768]{0:T(1024)}, u32[]{:S(2)}) copy-start(f32[768]{0:T(1024)} %param.15) | copy-start | bytes 9220
  75.3 12.7 %copy-start.1 = (bf16[384,768]{1,0:T(8,128)(2,1)S(1)}, bf16[384,768]{1,0:T(8,128)(2,1)}, u32[]{:S(2)}) copy-start(bf16[384,768]{1,0:T(8,128)(2,1)} %stream_hbm.1) | copy-start | bytes 1769476
  75.3 14.6 %collective-permute-start.18 = (bf16[384,384]{1,0:T(8,128)(2,1)S(1)}, bf16[384,384]{1,0:T(8,128)(2,1)S(1)}, u32[]{:S(2)}, u32[]{:S(2)}) collective-permute-start(bf16[384,384]{1,0:T(8,128)(2,1)S(1)} %shard_map.87), channel_id=1, source_target_pairs={{0,16},{16,0},{1,17},{17,1},{2,18},{18,2},{3,19},{19,3},{4,20},{20... | collective-permute-start | bytes 884744 | tf_op jit(solution)/shard_map/ppermute | solution.py:326
  86.4 7.9 %collective-permute-start.19 = (bf16[384,384]{1,0:T(8,128)(2,1)S(1)}, bf16[384,384]{1,0:T(8,128)(2,1)S(1)}, u32[]{:S(2)}, u32[]{:S(2)}) collective-permute-start(bf16[384,384]{1,0:T(8,128)(2,1)S(1)} %shard_map.88), channel_id=1, source_target_pairs={{0,16},{16,0},{1,17},{17,1},{2,18},{18,2},{3,19},{19,3},{4,20},{20... | collective-permute-start | bytes 884744 | tf_op jit(solution)/shard_map/ppermute | solution.py:326

commit v3 on v2

--- a/solution.py
+++ b/solution.py
@@ -116,13 +116,15 @@
 def prep_kernel(
     q_hbm, k_hbm, v_hbm, qg_hbm, kg_hbm, w_hbm, kv_send, kvw_keep, q_send, q_keep, *rest
 ):
-    q_ref, k_ref, v_ref, qg_ref, kg_ref, sems = rest
+    q_ref, k_ref, qg_ref, kg_ref, sems = rest
     mine = lax.axis_index("seq")
     half = q_keep.shape[1]
     head_size = qg_ref.shape[1]
     count = half // head_size
     rows = pl.ds(pl.multiple_of(mine * half, half), half)
-    moved = [(kg_hbm, kg_ref), (k_hbm, k_ref), (v_hbm, v_ref), (qg_hbm, qg_ref), (q_hbm, q_ref)]
+    moved = [(kg_hbm, kg_ref), (k_hbm, k_ref), (qg_hbm, qg_ref), (q_hbm, q_ref)]
+    for part, out in ((1 - mine, kv_send), (mine, kvw_keep)):
+        moved.append((v_hbm.at[:, pl.ds(pl.multiple_of(part * half, half), half)], out.at[1]))
     for index in range(2):
         moved.append((w_hbm.at[rows, index * half : (index + 1) * half], kvw_keep.at[2 + index]))
     copies = [
@@ -146,13 +148,10 @@
     for part, kv_out, _ in halves:
         normed(k_ref, kg_ref, part, kv_out.at[0])
     copies[2].wait()
-    for part, kv_out, _ in halves:
-        kv_out[1] = v_ref[:, pl.ds(pl.multiple_of(part * half, half), half)]
     copies[3].wait()
-    copies[4].wait()
     for part, _, q_out in halves:
         normed(q_ref, qg_ref, part, q_out)
-    for copy in copies[5:]:
+    for copy in copies[4:]:
         copy.wait()
 
 
@@ -169,7 +168,7 @@
         out_shape=[two, four, one, one],
         in_specs=[hbm_spec()] * 6,
         out_specs=[vmem_spec()] * 4,
-        scratch_shapes=[block, block, block, gain, gain, pltpu.SemaphoreType.DMA((7,))],
+        scratch_shapes=[block, block, gain, gain, pltpu.SemaphoreType.DMA((8,))],
         compiler_params=pltpu.CompilerParams(vmem_limit_bytes=FIRST_VMEM),
         cost_estimate=pl.CostEstimate(flops=rows * width * 16, bytes_accessed=rows * width * 12, transcendentals=0),
     )(q, k, v, q_gain, k_gain, out_weight)
@@ -185,8 +184,8 @@
     factor = scale * LOG2_E
     ones = jnp.ones((rows, head_size), jnp.bfloat16)
 
-    def head(index, unused):
-        columns = pl.ds(pl.multiple_of(index * head_size, head_size), head_size)
+    for index in range(queries[0].shape[1] // head_size):
+        columns = slice(index * head_size, (index + 1) * head_size)
         keys = [kv[0, :, columns] for kv in (kv0, kv1, kv2)]
         values = [jnp.concatenate([kv[1, :, columns], ones], axis=1) for kv in (kv0, kv1, kv2)]
         for which, q_ref in zip(times, queries):
@@ -222,9 +221,6 @@
             else:
                 out = refs[2]
                 out[:, columns] = (total[:, :head_size] / total[:, head_size:]).astype(jnp.bfloat16)
-        return unused
-
-    lax.fori_loop(0, queries[0].shape[1] // head_size, head, 0)
 
 
 def attend(times, queries, layers, head_size, carry=None):
@@ -270,27 +266,27 @@
                 write(part, low, high, total)
 
 
-def weight_of(kvw, kvw_pair, kvw_mid, second, third, which, part):
+def weight_of(kvw, kvw_pair, kvw_mid, inner, forward, outer, which, part):
     if which == 2:
-        return second[part][0][...] + second[part][1][...]
+        return inner[part] + forward(part)
     if which == 3:
-        return kvw_mid[2 + part] + third[part][...]
+        return kvw_mid[2 + part] + outer[part][...]
     return (kvw, kvw_pair)[which][2 + part]
 
 
-def peer_kernel(part, a0, a1, a2, a3, kvw, kvw_pair, kvw_mid, s0, s1, t0, out):
+def peer_kernel(part, a0, a1, a2, a3, kvw, kvw_pair, kvw_mid, inner, forward, outer, out):
     def write(unused, low, high, total):
         out[...] = total.astype(out.dtype)
 
     def weights(which, unused, low, high):
-        return weight_of(kvw, kvw_pair, kvw_mid, {part: (s0, s1)}, {part: t0}, which, part)
+        return weight_of(kvw, kvw_pair, kvw_mid, inner, lambda p: forward[...], {part: outer}, which, part)
 
     plane_sum([a[...] for a in (a0, a1, a2, a3)], weights, [(0, out.shape[1])], write)
 
 
-def own_kernel(spans, a0, a1, a2, a3, kvw, kvw_pair, kvw_mid, gate, stream_hbm, *rest):
-    second, third = (rest[0:2], rest[3:5]), (rest[2], rest[5])
-    out, stream, sem = rest[6:]
+def own_kernel(spans, a0, a1, a2, a3, kvw, kvw_pair, kvw_mid, inner, gate, stream_hbm, *rest):
+    forward, outer = rest[:2], rest[2 : 4]
+    out, stream, sem = rest[4 :]
     copy = pltpu.make_async_copy(stream_hbm, stream, sem)
     copy.start()
     copy.wait()
@@ -299,7 +295,7 @@
         out[:, low:high] = stream[:, low:high].astype(jnp.float32) + gate[:, low:high] * total
 
     def weights(which, part, low, high):
-        return weight_of(kvw, kvw_pair, kvw_mid, second, third, which, part)
+        return weight_of(kvw, kvw_pair, kvw_mid, inner, lambda p: forward[p][...], outer, which, part)
 
     plane_sum([a[...] for a in (a0, a1, a2, a3)], weights, spans, write)
 
@@ -356,30 +352,24 @@
     peer_pair, peer_mid = pair(kv_peer), middle(kv_peer)
 
     carry = attend((0, 1), [q_keep, q_peer], [kvw, kvw_pair, kvw_mid], head_size)
-    first_pair, first_mid, carry = barrier((kvw_pair[2], kvw_mid[2], carry))
-    forward = [middle(first_pair)]
-    second = [inward(first_mid)]
+    first_pair, early_mid, carry = barrier((kvw_pair[2], kvw_mid[2:], carry))
+    inner, forwards = inward(early_mid), [middle(first_pair)]
     layers = [kv_peer, peer_pair, peer_mid]
     theirs = attend((1,), [q_peer], layers, head_size, carry)
-    theirs, forward[0] = barrier((theirs, forward[0]))
+    theirs, forwards[0] = barrier((theirs, forwards[0]))
     across_theirs, beside_theirs = along(theirs, "col", 2), along(theirs, "col", 1)
-    third = [inward(forward[0])]
-    next_pair, next_mid, carry = barrier((kvw_pair[3], kvw_mid[3], carry, theirs))[:3]
-    forward.append(middle(next_pair))
-    second.append(inward(next_mid))
-    third.append(inward(forward[1]))
-    mine = attend((0,), [q_keep], layers, head_size, carry)
-    across_mine, beside_mine = along(mine, "col", 2), along(mine, "col", 1)
-    weights = [[forward[part], second[part], third[part]] for part in range(2)]
+    next_pair = barrier((kvw_pair[3], theirs))[0]
+    forwards.append(middle(next_pair))
+    outer = [inward(forwards[part]) for part in range(2)]
 
     gate = gate.reshape(1, width)
     vmem, hbm = vmem_spec(), hbm_spec()
     groups = [theirs, beside_theirs, across_theirs, along(across_theirs, "col", 1)]
-    received = []
+    sents = []
     for part, (low, high) in enumerate(spans):
         sent = call(
             functools.partial(peer_kernel, part),
-            [*groups, kvw, kvw_pair, kvw_mid, *weights[part]],
+            [*groups, kvw, kvw_pair, kvw_mid, inner, forwards[part], outer[part]],
             [vmem] * 10,
             jax.ShapeDtypeStruct((tokens, high - low), jnp.bfloat16),
             vmem,
@@ -388,12 +378,16 @@
         )
         if part == 0:
             sent, groups[0] = barrier((sent, groups[0]))
-        received.append(swap(sent))
+        sents.append(sent)
+    received = [swap(sent) for sent in sents]
+    carry, forwards[1] = barrier((carry, forwards[1]))
+    mine = attend((0,), [q_keep], layers, head_size, carry)
+    across_mine, beside_mine = along(mine, "col", 2), along(mine, "col", 1)
     groups = [mine, beside_mine, across_mine, along(across_mine, "col", 1)]
     base = call(
         functools.partial(own_kernel, spans),
-        [*groups, kvw, kvw_pair, kvw_mid, gate, stream, *weights[0], *weights[1]],
-        [vmem] * 8 + [hbm] + [vmem] * 6,
+        [*groups, kvw, kvw_pair, kvw_mid, inner, gate, stream, *forwards, *outer],
+        [vmem] * 9 + [hbm] + [vmem] * 4,
         jax.ShapeDtypeStruct((tokens, width), jnp.float32),
         vmem,
         [pltpu.VMEM((tokens, width), stream.dtype), pltpu.SemaphoreType.DMA(())],

time: 95.6 us -> 90 us (0.941)
  Pallas kernels: 21.6 us -> 18.5 us
  starting transfers between devices: 23.4 us -> 20.6 us
    ppermute x2, waiting for transfers between devices: 9.51 us -> 15.8 us  [pair(): return lax.ppermute(x, 'row', [(i, i ^ 1) for i in range(4)])]
    ppermute x6, waiting for transfers between devices: 6.14 us -> 1.13 us  [along(): return lax.ppermute(x, axis, [(i, i ^ mask) for i in range(4)])]
    pallas_call x3, Pallas kernels: 13.3 us -> 10.4 us  [attend(): pl.pallas_call(functools.partial(attend_kernel, 1.0 / math.sqrt(head_size...]
    ppermute x4 -> x3, waiting for transfers between devices: 15.4 us -> 13 us  [inward(): return lax.ppermute(x, 'row', [(1, 0), (2, 3)])]
    ppermute x2, starting transfers between devices: 7.43 us -> 5.9 us  [pair(): return lax.ppermute(x, 'row', [(i, i ^ 1) for i in range(4)])]
    ppermute x4 -> x3, starting transfers between devices: 5.16 us -> 4.03 us  [inward(): return lax.ppermute(x, 'row', [(1, 0), (2, 3)])]
  transfers between devices with their start and end apart: 20 -> 19, of which waited for: 9 -> 8; matrix products, arithmetic and copies ran while one was open for 0% -> 0% of each run, Pallas kernels for 18% -> 16%
where the time goes in v3:
time: 90 us; the launch traced here: 88.9 us
  waiting for transfers between devices  49.3 us (55%)
  starting transfers between devices  20.6 us (23%)
  Pallas kernels  18.5 us (21%)
    ppermute x4, waiting for transfers between devices, swap(): return lax.ppermute(x, 'seq', [(0, 1), (1, 0)])  19.4 us
    ppermute x2, waiting for transfers between devices, pair(): return lax.ppermute(x, 'row', [(i, i ^ 1) for i in range(4)])  15.8 us
    ppermute x3, waiting for transfers between devices, inward(): return lax.ppermute(x, 'row', [(1, 0), (2, 3)])  13 us
    pallas_call x3, Pallas kernels, attend(): pl.pallas_call(functools.partial(attend_kernel, 1.0 / math.sqrt(head_size...  10.4 us
    ppermute x2, starting transfers between devices, pair(): return lax.ppermute(x, 'row', [(i, i ^ 1) for i in range(4)])  5.9 us
    ppermute x4, starting transfers between devices, swap(): return lax.ppermute(x, 'seq', [(0, 1), (1, 0)])  5.2 us
    pallas_call x4, Pallas kernels, call(): pl.pallas_call(kernel, out_shape=out_shape, in_specs=specs, out_specs=out...  4.8 us
    ppermute x3, starting transfers between devices, inward(): return lax.ppermute(x, 'row', [(1, 0), (2, 3)])  4.03 us
  transfers between devices with their start and end apart: 19, of which 8 were waited for; matrix products, arithmetic and copies ran while one was open for 0% of the time, Pallas kernels for 16%

profile of v3, /device:TPU:0, one launch (start us, length us, event | category | flops | bytes accessed | tf_op | source)
XLA Modules:
  0.0 88.9 jit_solution(16802132485092618404)
XLA Ops:
  0.0 3.3 %shard_map.82 = (bf16[2,384,384]{2,1,0:T(8,128)(2,1)}, bf16[4,384,384]{2,1,0:T(8,128)(2,1)}, bf16[384,384]{1,0:T(8,128)(2,1)}, bf16[384,384]{1,0:T(8,128)(2,1)}) custom-call(bf16[384,768]{1,0:T(8,128)(2,1)} %q_hbm.1, bf16[384,768]{1,0:T(8,128)(2,1)} %k_hbm.1, bf16[384,768]{1,0:T(8,128)(2,1)} %v_hbm.1, f32[6,128]{1,0:T(8,128)} %qg_hbm.1, f32[6,128]{1,0:T(8,128)} %kg_hbm.1, ...), custom_call_target="tpu_custom_call" | custom-call | flops 4718592 | bytes 3538944 | tf_op jit(solution)/shard_map/pallas_call | solution.py:166
  3.3 0.7 collective-permute-start.4
  4.1 5.8 %collective-permute-start.3 = (bf16[4,384,384]{2,1,0:T(8,128)(2,1)}, bf16[4,384,384]{2,1,0:T(8,128)(2,1)S(1)}, u32[]{:S(2)}, u32[]{:S(2)}) collective-permute-start(bf16[4,384,384]{2,1,0:T(8,128)(2,1)} %get-tuple-element.25.refs_2_.kvw), channel_id=1, source_target_pairs={{0,4},{4,0},{8,12},{12,8},{1,5},{5,1},{9,13},{13,9},{2,6},{6,2},{1... | collective-permute-start | bytes 3538952 | tf_op jit(solution)/shard_map/ppermute | solution.py:325
  9.9 1.5 %collective-permute-start = (bf16[2,384,384]{2,1,0:T(8,128)(2,1)}, bf16[2,384,384]{2,1,0:T(8,128)(2,1)S(1)}, u32[]{:S(2)}, u32[]{:S(2)}) collective-permute-start(bf16[2,384,384]{2,1,0:T(8,128)(2,1)} %get-tuple-element.24), channel_id=1, source_target_pairs={{0,16},{16,0},{1,17},{17,1},{2,18},{18,2},{3,19},{19,3},{4,20},{20... | collective-permute-start | bytes 1769480 | tf_op jit(solution)/shard_map/ppermute | solution.py:322
  11.4 0.5 collective-permute-start.5
  11.9 14.4 %collective-permute-done.refs_1_ = bf16[2,384,384]{2,1,0:T(8,128)(2,1)S(1)} collective-permute-done((bf16[2,384,384]{2,1,0:T(8,128)(2,1)}, bf16[2,384,384]{2,1,0:T(8,128)(2,1)S(1)}, u32[]{:S(2)}, u32[]{:S(2)}) %collective-permute-start) | collective-permute-done | bytes 589856 | tf_op jit(solution)/shard_map/ppermute | solution.py:322
  26.4 0.1 collective-permute-start.1
  26.5 0.7 collective-permute-start.2
  27.2 0.0 collective-permute-done.4.refs_4_.kvw_mid
  27.2 0.1 slice.13
  27.2 9.7 %collective-permute-done.3.refs_3_.kvw_pair = bf16[4,384,384]{2,1,0:T(8,128)(2,1)S(1)} collective-permute-done((bf16[4,384,384]{2,1,0:T(8,128)(2,1)}, bf16[4,384,384]{2,1,0:T(8,128)(2,1)S(1)}, u32[]{:S(2)}, u32[]{:S(2)}) %collective-permute-start.3) | collective-permute-done | bytes 1179680 | tf_op jit(solution)/shard_map/ppermute | solution.py:325
  37.0 0.1 slice_bitcast_fusion
  37.0 0.0 collective-permute-done.5.refs_1_.refs_0_
  37.1 4.5 %shard_map.83 = (f32[3,2,384,128]{3,2,1,0:T(8,128)S(1)}, f32[3,2,384,256]{3,2,1,0:T(8,128)S(1)}) custom-call(bf16[384,384]{1,0:T(8,128)(2,1)S(1)} %copy-done.2, bf16[384,384]{1,0:T(8,128)(2,1)S(1)} %collective-permute-done.5.refs_1_.refs_0_, bf16[4,384,384]{2,1,0:T(8,128)(2,1)S(1)} %copy-done, ...), custom_call_target="tpu_custom_call" | custom-call | flops 2717908992 | bytes 8388608 | tf_op jit(solution)/shard_map/pallas_call | solution.py:241
  41.6 0.7 collective-permute-start.6
  42.2 1.3 %collective-permute-start.11 = (bf16[2,384,384]{2,1,0:T(8,128)(2,1)S(1)}, bf16[2,384,384]{2,1,0:T(8,128)(2,1)S(1)}, u32[]{:S(2)}, u32[]{:S(2)}) collective-permute-start(bf16[2,384,384]{2,1,0:T(8,128)(2,1)S(1)} %slice.13), channel_id=1, source_target_pairs={{4,0},{8,12},{5,1},{9,13},{6,2},{10,14},{7,3},{11,15},{20,16},{24,... | collective-permute-start | bytes 1769480 | tf_op jit(solution)/shard_map/ppermute | solution.py:345
  43.5 6.1 %collective-permute-done.1.refs_2_ = bf16[2,384,384]{2,1,0:T(8,128)(2,1)S(1)} collective-permute-done((bf16[2,384,384]{2,1,0:T(8,128)(2,1)S(1)}, bf16[2,384,384]{2,1,0:T(8,128)(2,1)S(1)}, u32[]{:S(2)}, u32[]{:S(2)}) %collective-permute-start.1) | collective-permute-done | bytes 589856 | tf_op jit(solution)/shard_map/ppermute | solution.py:325
  49.6 0.0 collective-permute-done.2.refs_3_
  49.6 2.9 %shard_map.84.a0 = bf16[384,384]{1,0:T(8,128)(2,1)S(1)} custom-call(bf16[384,384]{1,0:T(8,128)(2,1)S(1)} %collective-permute-done.5.refs_1_.refs_0_, bf16[2,384,384]{2,1,0:T(8,128)(2,1)S(1)} %collective-permute-done.refs_1_, bf16[2,384,384]{2,1,0:T(8,128)(2,1)S(1)} %collective-permute-done.1.refs_2_, ...), custom_call_target="tpu_custom_call" | custom-call | flops 1358954496 | bytes 8388608 | tf_op jit(solution)/shard_map/pallas_call | solution.py:241
  52.5 0.0 collective-permute-done.6.rest_0_.forward
  52.6 0.7 collective-permute-start.7
  53.2 1.6 %collective-permute-start.15 = (bf16[384,384]{1,0:T(8,128)(2,1)S(1)}, bf16[384,384]{1,0:T(8,128)(2,1)S(1)}, u32[]{:S(2)}, u32[]{:S(2)}) collective-permute-start(bf16[384,384]{1,0:T(8,128)(2,1)S(1)} %shard_map.84.a0), channel_id=1, source_target_pairs={{0,2},{1,3},{2,0},{3,1},{4,6},{5,7},{6,4},{7,5},{8,10},{9,11},{10,... | collective-permute-start | bytes 884744 | tf_op jit(solution)/shard_map/ppermute | solution.py:331
  54.8 1.3 %collective-permute-start.12 = (bf16[384,384]{1,0:T(8,128)(2,1)S(1)}, bf16[384,384]{1,0:T(8,128)(2,1)S(1)}, u32[]{:S(2)}, u32[]{:S(2)}) collective-permute-start(bf16[384,384]{1,0:T(8,128)(2,1)S(1)} %collective-permute-done.6.rest_0_.forward), channel_id=1, source_target_pairs={{4,0},{8,12},{5,1},{9,13},{6,2},{10,14},{7,3},{11,15},{20,16},{24,... | collective-permute-start | bytes 884744 | tf_op jit(solution)/shard_map/ppermute | solution.py:345
  56.1 0.0 collective-permute-done.7.rest_1_.forward
  56.1 2.9 %shard_map.85.a0 = bf16[384,384]{1,0:T(8,128)(2,1)S(1)} custom-call(bf16[384,384]{1,0:T(8,128)(2,1)S(1)} %copy-done.2, bf16[2,384,384]{2,1,0:T(8,128)(2,1)S(1)} %collective-permute-done.refs_1_, bf16[2,384,384]{2,1,0:T(8,128)(2,1)S(1)} %collective-permute-done.1.refs_2_, bf16[2,384,384]{2,1,0:T(8,128)(2,1)S(1)} %collective-permute-done.2.refs_3_, ...), custom_call_target="tpu_custom_call" | custom-call | flops 1358954496 | bytes 8388608 | tf_op jit(solution)/shard_map/pallas_call | solution.py:241
  59.0 0.6 collective-permute-start.9
  59.6 0.0 collective-permute-start.14
  59.6 1.1 %collective-permute-done.15.a2 = bf16[384,384]{1,0:T(8,128)(2,1)S(1)} collective-permute-done((bf16[384,384]{1,0:T(8,128)(2,1)S(1)}, bf16[384,384]{1,0:T(8,128)(2,1)S(1)}, u32[]{:S(2)}, u32[]{:S(2)}) %collective-permute-start.15) | collective-permute-done | bytes 294944 | tf_op jit(solution)/shard_map/ppermute | solution.py:331
  60.8 0.0 collective-permute-start.16
  60.8 0.7 collective-permute-done.11.inner
  61.4 1.5 %collective-permute-start.13 = (bf16[384,384]{1,0:T(8,128)(2,1)S(1)}, bf16[384,384]{1,0:T(8,128)(2,1)S(1)}, u32[]{:S(2)}, u32[]{:S(2)}) collective-permute-start(bf16[384,384]{1,0:T(8,128)(2,1)S(1)} %collective-permute-done.7.rest_1_.forward), channel_id=1, source_target_pairs={{4,0},{8,12},{5,1},{9,13},{6,2},{10,14},{7,3},{11,15},{20,16},{24,... | collective-permute-start | bytes 884744 | tf_op jit(solution)/shard_map/ppermute | solution.py:345
  62.9 4.5 %collective-permute-done.12.rest_2_.outer = bf16[384,384]{1,0:T(8,128)(2,1)S(1)} collective-permute-done((bf16[384,384]{1,0:T(8,128)(2,1)S(1)}, bf16[384,384]{1,0:T(8,128)(2,1)S(1)}, u32[]{:S(2)}, u32[]{:S(2)}) %collective-permute-start.12) | collective-permute-done | bytes 294944 | tf_op jit(solution)/shard_map/ppermute | solution.py:345
  67.4 0.0 collective-permute-start.8
  67.4 0.0 collective-permute-done.9.a2
  67.4 0.5 collective-permute-start.10
  67.9 0.0 collective-permute-done.14.a1
  67.9 1.0 %shard_map.87 = bf16[384,384]{1,0:T(8,128)(2,1)S(1)} custom-call(bf16[384,384]{1,0:T(8,128)(2,1)S(1)} %shard_map.84.a0, bf16[384,384]{1,0:T(8,128)(2,1)S(1)} %collective-permute-done.14.a1, bf16[384,384]{1,0:T(8,128)(2,1)S(1)} %collective-permute-done.15.a2, bf16[384,384]{1,0:T(8,128)(2,1)S(1)} %collective-permute-done.16.a3, ...), custom_call_target="tpu_custom_call" | custom-call | flops 452984832 | bytes 2097152 | tf_op jit(solution)/shard_map/pallas_call | solution.py:334
  68.9 0.0 copy-start.3
  69.0 0.0 copy-start.1
  69.0 1.6 %collective-permute-start.17 = (bf16[384,384]{1,0:T(8,128)(2,1)S(1)}, bf16[384,384]{1,0:T(8,128)(2,1)S(1)}, u32[]{:S(2)}, u32[]{:S(2)}) collective-permute-start(bf16[384,384]{1,0:T(8,128)(2,1)S(1)} %shard_map.87), channel_id=1, source_target_pairs={{0,16},{16,0},{1,17},{17,1},{2,18},{18,2},{3,19},{19,3},{4,20},{20... | collective-permute-start | bytes 884744 | tf_op jit(solution)/shard_map/ppermute | solution.py:322
  70.6 7.8 %collective-permute-done.13.rest_3_.outer = bf16[384,384]{1,0:T(8,128)(2,1)S(1)} collective-permute-done((bf16[384,384]{1,0:T(8,128)(2,1)S(1)}, bf16[384,384]{1,0:T(8,128)(2,1)S(1)}, u32[]{:S(2)}, u32[]{:S(2)}) %collective-permute-start.13) | collective-permute-done | bytes 294944 | tf_op jit(solution)/shard_map/ppermute | solution.py:345
  78.4 1.0 %shard_map.88 = bf16[384,384]{1,0:T(8,128)(2,1)S(1)} custom-call(bf16[384,384]{1,0:T(8,128)(2,1)S(1)} %shard_map.84.a0, bf16[384,384]{1,0:T(8,128)(2,1)S(1)} %collective-permute-done.14.a1, bf16[384,384]{1,0:T(8,128)(2,1)S(1)} %collective-permute-done.15.a2, bf16[384,384]{1,0:T(8,128)(2,1)S(1)} %collective-permute-done.16.a3, ...), custom_call_target="tpu_custom_call" | custom-call | flops 452984832 | bytes 2097152 | tf_op jit(solution)/shard_map/pallas_call | solution.py:334
  79.4 1.6 %collective-permute-start.18 = (bf16[384,384]{1,0:T(8,128)(2,1)S(1)}, bf16[384,384]{1,0:T(8,128)(2,1)S(1)}, u32[]{:S(2)}, u32[]{:S(2)}) collective-permute-start(bf16[384,384]{1,0:T(8,128)(2,1)S(1)} %shard_map.88), channel_id=1, source_target_pairs={{0,16},{16,0},{1,17},{17,1},{2,18},{18,2},{3,19},{19,3},{4,20},{20... | collective-permute-start | bytes 884744 | tf_op jit(solution)/shard_map/ppermute | solution.py:322
  81.0 0.0 collective-permute-done.8.a1
  81.0 0.0 collective-permute-done.10.a3
  81.0 1.9 %shard_map.86.base = f32[384,768]{1,0:T(8,128)S(1)} custom-call(bf16[384,384]{1,0:T(8,128)(2,1)S(1)} %shard_map.85.a0, bf16[384,384]{1,0:T(8,128)(2,1)S(1)} %collective-permute-done.8.a1, bf16[384,384]{1,0:T(8,128)(2,1)S(1)} %collective-permute-done.9.a2, bf16[384,384]{1,0:T(8,128)(2,1)S(1)} %collective-permute-done.10.a3, bf16[4,384,384]{2,1,0:T(8,128)(2,1)S(1)} %copy-done, ...), custom_call_target="tpu_custom_call" | custom-call | flops 905969664 | bytes 2097152 | tf_op jit(solution)/shard_map/pallas_call | solution.py:334
  82.9 4.9 %collective-permute-done.18.rest_1_ = bf16[384,384]{1,0:T(8,128)(2,1)S(1)} collective-permute-done((bf16[384,384]{1,0:T(8,128)(2,1)S(1)}, bf16[384,384]{1,0:T(8,128)(2,1)S(1)}, u32[]{:S(2)}, u32[]{:S(2)}) %collective-permute-start.18) | collective-permute-done | bytes 294944 | tf_op jit(solution)/shard_map/ppermute | solution.py:322
  87.8 0.9 %shard_map.89 = bf16[384,768]{1,0:T(8,128)(2,1)} custom-call(f32[384,768]{1,0:T(8,128)S(1)} %shard_map.86.base, f32[1,768]{1,0:T(1,128)S(1)} %reshape.3.gate, bf16[384,384]{1,0:T(8,128)(2,1)S(1)} %collective-permute-done.17.rest_0_, bf16[384,384]{1,0:T(8,128)(2,1)S(1)} %collective-permute-done.18.rest_1_), custom_call_target="tpu_custom_call" | custom-call | flops 1179648 | bytes 2097152 | tf_op jit(solution)/shard_map/pallas_call | solution.py:334
  (9 shorter events, 0.0 us)
Async XLA Ops:
  3.3 23.8 %collective-permute-start.4 = (bf16[4,384,384]{2,1,0:T(8,128)(2,1)}, bf16[4,384,384]{2,1,0:T(8,128)(2,1)S(1)}, u32[]{:S(2)}, u32[]{:S(2)}) collective-permute-start(bf16[4,384,384]{2,1,0:T(8,128)(2,1)} %get-tuple-element.25.refs_2_.kvw), channel_id=1, source_target_pairs={{4,8},{8,4},{5,9},{9,5},{6,10},{10,6},{7,11},{11,7},{20,24},{24,20... | collective-permute-start | bytes 3538952 | tf_op jit(solution)/shard_map/ppermute | solution.py:328
  4.1 32.9 %collective-permute-start.3 = (bf16[4,384,384]{2,1,0:T(8,128)(2,1)}, bf16[4,384,384]{2,1,0:T(8,128)(2,1)S(1)}, u32[]{:S(2)}, u32[]{:S(2)}) collective-permute-start(bf16[4,384,384]{2,1,0:T(8,128)(2,1)} %get-tuple-element.25.refs_2_.kvw), channel_id=1, source_target_pairs={{0,4},{4,0},{8,12},{12,8},{1,5},{5,1},{9,13},{13,9},{2,6},{6,2},{1... | collective-permute-start | bytes 3538952 | tf_op jit(solution)/shard_map/ppermute | solution.py:325
  9.9 16.5 %collective-permute-start = (bf16[2,384,384]{2,1,0:T(8,128)(2,1)}, bf16[2,384,384]{2,1,0:T(8,128)(2,1)S(1)}, u32[]{:S(2)}, u32[]{:S(2)}) collective-permute-start(bf16[2,384,384]{2,1,0:T(8,128)(2,1)} %get-tuple-element.24), channel_id=1, source_target_pairs={{0,16},{16,0},{1,17},{17,1},{2,18},{18,2},{3,19},{19,3},{4,20},{20... | collective-permute-start | bytes 1769480 | tf_op jit(solution)/shard_map/ppermute | solution.py:322
  11.4 25.6 %copy-start = (bf16[4,384,384]{2,1,0:T(8,128)(2,1)S(1)}, bf16[4,384,384]{2,1,0:T(8,128)(2,1)}, u32[]{:S(2)}) copy-start(bf16[4,384,384]{2,1,0:T(8,128)(2,1)} %get-tuple-element.25.refs_2_.kvw) | copy-start | bytes 3538948
  11.4 25.6 %copy-start.2 = (bf16[384,384]{1,0:T(8,128)(2,1)S(1)}, bf16[384,384]{1,0:T(8,128)(2,1)}, u32[]{:S(2)}) copy-start(bf16[384,384]{1,0:T(8,128)(2,1)} %get-tuple-element.23.refs_0_) | copy-start | bytes 884740
  11.4 25.6 %collective-permute-start.5 = (bf16[384,384]{1,0:T(8,128)(2,1)}, bf16[384,384]{1,0:T(8,128)(2,1)S(1)}, u32[]{:S(2)}, u32[]{:S(2)}) collective-permute-start(bf16[384,384]{1,0:T(8,128)(2,1)} %get-tuple-element.26), channel_id=1, source_target_pairs={{0,16},{16,0},{1,17},{17,1},{2,18},{18,2},{3,19},{19,3},{4,20},{20... | collective-permute-start | bytes 884744 | tf_op jit(solution)/shard_map/ppermute | solution.py:322
  26.4 23.2 %collective-permute-start.1 = (bf16[2,384,384]{2,1,0:T(8,128)(2,1)S(1)}, bf16[2,384,384]{2,1,0:T(8,128)(2,1)S(1)}, u32[]{:S(2)}, u32[]{:S(2)}) collective-permute-start(bf16[2,384,384]{2,1,0:T(8,128)(2,1)S(1)} %collective-permute-done.refs_1_), channel_id=1, source_target_pairs={{0,4},{4,0},{8,12},{12,8},{1,5},{5,1},{9,13},{13,9},{2,6},{6,2},{1... | collective-permute-start | bytes 1769480 | tf_op jit(solution)/shard_map/ppermute | solution.py:325
  26.5 23.1 %collective-permute-start.2 = (bf16[2,384,384]{2,1,0:T(8,128)(2,1)S(1)}, bf16[2,384,384]{2,1,0:T(8,128)(2,1)S(1)}, u32[]{:S(2)}, u32[]{:S(2)}) collective-permute-start(bf16[2,384,384]{2,1,0:T(8,128)(2,1)S(1)} %collective-permute-done.refs_1_), channel_id=1, source_target_pairs={{4,8},{8,4},{5,9},{9,5},{6,10},{10,6},{7,11},{11,7},{20,24},{24,20... | collective-permute-start | bytes 1769480 | tf_op jit(solution)/shard_map/ppermute | solution.py:328
  41.6 11.0 %collective-permute-start.6 = (bf16[384,384]{1,0:T(8,128)(2,1)S(1)}, bf16[384,384]{1,0:T(8,128)(2,1)S(1)}, u32[]{:S(2)}, u32[]{:S(2)}) collective-permute-start(bf16[384,384]{1,0:T(8,128)(2,1)S(1)} %get-tuple-element.31), channel_id=1, source_target_pairs={{4,8},{8,4},{5,9},{9,5},{6,10},{10,6},{7,11},{11,7},{20,24},{24,20... | collective-permute-start | bytes 884744 | tf_op jit(solution)/shard_map/ppermute | solution.py:328
  42.2 19.2 %collective-permute-start.11 = (bf16[2,384,384]{2,1,0:T(8,128)(2,1)S(1)}, bf16[2,384,384]{2,1,0:T(8,128)(2,1)S(1)}, u32[]{:S(2)}, u32[]{:S(2)}) collective-permute-start(bf16[2,384,384]{2,1,0:T(8,128)(2,1)S(1)} %slice.13), channel_id=1, source_target_pairs={{4,0},{8,12},{5,1},{9,13},{6,2},{10,14},{7,3},{11,15},{20,16},{24,... | collective-permute-start | bytes 1769480 | tf_op jit(solution)/shard_map/ppermute | solution.py:345
  52.6 3.5 %collective-permute-start.7 = (bf16[384,384]{1,0:T(8,128)(2,1)S(1)}, bf16[384,384]{1,0:T(8,128)(2,1)S(1)}, u32[]{:S(2)}, u32[]{:S(2)}) collective-permute-start(bf16[384,384]{1,0:T(8,128)(2,1)S(1)} %get-tuple-element.33), channel_id=1, source_target_pairs={{4,8},{8,4},{5,9},{9,5},{6,10},{10,6},{7,11},{11,7},{20,24},{24,20... | collective-permute-start | bytes 884744 | tf_op jit(solution)/shard_map/ppermute | solution.py:328
  53.2 7.5 %collective-permute-start.15 = (bf16[384,384]{1,0:T(8,128)(2,1)S(1)}, bf16[384,384]{1,0:T(8,128)(2,1)S(1)}, u32[]{:S(2)}, u32[]{:S(2)}) collective-permute-start(bf16[384,384]{1,0:T(8,128)(2,1)S(1)} %shard_map.84.a0), channel_id=1, source_target_pairs={{0,2},{1,3},{2,0},{3,1},{4,6},{5,7},{6,4},{7,5},{8,10},{9,11},{10,... | collective-permute-start | bytes 884744 | tf_op jit(solution)/shard_map/ppermute | solution.py:331
  54.8 12.6 %collective-permute-start.12 = (bf16[384,384]{1,0:T(8,128)(2,1)S(1)}, bf16[384,384]{1,0:T(8,128)(2,1)S(1)}, u32[]{:S(2)}, u32[]{:S(2)}) collective-permute-start(bf16[384,384]{1,0:T(8,128)(2,1)S(1)} %collective-permute-done.6.rest_0_.forward), channel_id=1, source_target_pairs={{4,0},{8,12},{5,1},{9,13},{6,2},{10,14},{7,3},{11,15},{20,16},{24,... | collective-permute-start | bytes 884744 | tf_op jit(solution)/shard_map/ppermute | solution.py:345
  59.0 8.4 %collective-permute-start.9 = (bf16[384,384]{1,0:T(8,128)(2,1)S(1)}, bf16[384,384]{1,0:T(8,128)(2,1)S(1)}, u32[]{:S(2)}, u32[]{:S(2)}) collective-permute-start(bf16[384,384]{1,0:T(8,128)(2,1)S(1)} %shard_map.85.a0), channel_id=1, source_target_pairs={{0,2},{1,3},{2,0},{3,1},{4,6},{5,7},{6,4},{7,5},{8,10},{9,11},{10,... | collective-permute-start | bytes 884744 | tf_op jit(solution)/shard_map/ppermute | solution.py:331
  59.6 8.3 %collective-permute-start.14 = (bf16[384,384]{1,0:T(8,128)(2,1)S(1)}, bf16[384,384]{1,0:T(8,128)(2,1)S(1)}, u32[]{:S(2)}, u32[]{:S(2)}) collective-permute-start(bf16[384,384]{1,0:T(8,128)(2,1)S(1)} %shard_map.84.a0), channel_id=1, source_target_pairs={{0,1},{1,0},{2,3},{3,2},{4,5},{5,4},{6,7},{7,6},{8,9},{9,8},{10,11... | collective-permute-start | bytes 884744 | tf_op jit(solution)/shard_map/ppermute | solution.py:331
  60.8 7.2 %collective-permute-start.16 = (bf16[384,384]{1,0:T(8,128)(2,1)S(1)}, bf16[384,384]{1,0:T(8,128)(2,1)S(1)}, u32[]{:S(2)}, u32[]{:S(2)}) collective-permute-start(bf16[384,384]{1,0:T(8,128)(2,1)S(1)} %collective-permute-done.15.a2), channel_id=1, source_target_pairs={{0,1},{1,0},{2,3},{3,2},{4,5},{5,4},{6,7},{7,6},{8,9},{9,8},{10,11... | collective-permute-start | bytes 884744 | tf_op jit(solution)/shard_map/ppermute | solution.py:331
  61.4 16.9 %collective-permute-start.13 = (bf16[384,384]{1,0:T(8,128)(2,1)S(1)}, bf16[384,384]{1,0:T(8,128)(2,1)S(1)}, u32[]{:S(2)}, u32[]{:S(2)}) collective-permute-start(bf16[384,384]{1,0:T(8,128)(2,1)S(1)} %collective-permute-done.7.rest_1_.forward), channel_id=1, source_target_pairs={{4,0},{8,12},{5,1},{9,13},{6,2},{10,14},{7,3},{11,15},{20,16},{24,... | collective-permute-start | bytes 884744 | tf_op jit(solution)/shard_map/ppermute | solution.py:345
  67.4 13.5 %collective-permute-start.8 = (bf16[384,384]{1,0:T(8,128)(2,1)S(1)}, bf16[384,384]{1,0:T(8,128)(2,1)S(1)}, u32[]{:S(2)}, u32[]{:S(2)}) collective-permute-start(bf16[384,384]{1,0:T(8,128)(2,1)S(1)} %shard_map.85.a0), channel_id=1, source_target_pairs={{0,1},{1,0},{2,3},{3,2},{4,5},{5,4},{6,7},{7,6},{8,9},{9,8},{10,11... | collective-permute-start | bytes 884744 | tf_op jit(solution)/shard_map/ppermute | solution.py:331
  67.4 13.5 %collective-permute-start.10 = (bf16[384,384]{1,0:T(8,128)(2,1)S(1)}, bf16[384,384]{1,0:T(8,128)(2,1)S(1)}, u32[]{:S(2)}, u32[]{:S(2)}) collective-permute-start(bf16[384,384]{1,0:T(8,128)(2,1)S(1)} %collective-permute-done.9.a2), channel_id=1, source_target_pairs={{0,1},{1,0},{2,3},{3,2},{4,5},{5,4},{6,7},{7,6},{8,9},{9,8},{10,11... | collective-permute-start | bytes 884744 | tf_op jit(solution)/shard_map/ppermute | solution.py:331
  68.9 12.0 %copy-start.3 = (f32[768]{0:T(1024)S(1)}, f32[768]{0:T(1024)}, u32[]{:S(2)}) copy-start(f32[768]{0:T(1024)} %param.15) | copy-start | bytes 9220
  69.0 12.0 %copy-start.1 = (bf16[384,768]{1,0:T(8,128)(2,1)S(1)}, bf16[384,768]{1,0:T(8,128)(2,1)}, u32[]{:S(2)}) copy-start(bf16[384,768]{1,0:T(8,128)(2,1)} %stream_hbm.1) | copy-start | bytes 1769476
  69.0 13.9 %collective-permute-start.17 = (bf16[384,384]{1,0:T(8,128)(2,1)S(1)}, bf16[384,384]{1,0:T(8,128)(2,1)S(1)}, u32[]{:S(2)}, u32[]{:S(2)}) collective-permute-start(bf16[384,384]{1,0:T(8,128)(2,1)S(1)} %shard_map.87), channel_id=1, source_target_pairs={{0,16},{16,0},{1,17},{17,1},{2,18},{18,2},{3,19},{19,3},{4,20},{20... | collective-permute-start | bytes 884744 | tf_op jit(solution)/shard_map/ppermute | solution.py:322
  79.4 8.5 %collective-permute-start.18 = (bf16[384,384]{1,0:T(8,128)(2,1)S(1)}, bf16[384,384]{1,0:T(8,128)(2,1)S(1)}, u32[]{:S(2)}, u32[]{:S(2)}) collective-permute-start(bf16[384,384]{1,0:T(8,128)(2,1)S(1)} %shard_map.88), channel_id=1, source_target_pairs={{0,16},{16,0},{1,17},{17,1},{2,18},{18,2},{3,19},{19,3},{4,20},{20... | collective-permute-start | bytes 884744 | tf_op jit(solution)/shard_map/ppermute | solution.py:322

commit v4 on v3

--- a/solution.py
+++ b/solution.py
@@ -356,7 +356,6 @@
     inner, forwards = inward(early_mid), [middle(first_pair)]
     layers = [kv_peer, peer_pair, peer_mid]
     theirs = attend((1,), [q_peer], layers, head_size, carry)
-    theirs, forwards[0] = barrier((theirs, forwards[0]))
     across_theirs, beside_theirs = along(theirs, "col", 2), along(theirs, "col", 1)
     next_pair = barrier((kvw_pair[3], theirs))[0]
     forwards.append(middle(next_pair))
@@ -374,7 +373,7 @@
             jax.ShapeDtypeStruct((tokens, high - low), jnp.bfloat16),
             vmem,
             [],
-            tokens * width * (high - low) * 4,
+            tokens * width * (high - low) * 40,
         )
         if part == 0:
             sent, groups[0] = barrier((sent, groups[0]))

time: 90 us -> 87 us (0.967)
  waiting for transfers between devices: 49.3 us -> 44.9 us
  starting transfers between devices: 20.6 us -> 23 us
    ppermute x3, waiting for transfers between devices: 13 us -> 5.8 us  [inward(): return lax.ppermute(x, 'row', [(1, 0), (2, 3)])]
    ppermute x6, waiting for transfers between devices: 1.13 us -> 5.02 us  [along(): return lax.ppermute(x, axis, [(i, i ^ mask) for i in range(4)])]
    ppermute x4, starting transfers between devices: 5.2 us -> 6.29 us  [swap(): return lax.ppermute(x, 'seq', [(0, 1), (1, 0)])]
    ppermute x4, waiting for transfers between devices: 19.4 us -> 18.3 us  [swap(): return lax.ppermute(x, 'seq', [(0, 1), (1, 0)])]
    ppermute x6, starting transfers between devices: 2.67 us -> 3.71 us  [along(): return lax.ppermute(x, axis, [(i, i ^ mask) for i in range(4)])]
where the time goes in v4:
time: 87 us; the launch traced here: 86.8 us
  waiting for transfers between devices  44.9 us (52%)
  starting transfers between devices  23 us (26%)
  Pallas kernels  18.4 us (21%)
    ppermute x4, waiting for transfers between devices, swap(): return lax.ppermute(x, 'seq', [(0, 1), (1, 0)])  18.3 us
    ppermute x2, waiting for transfers between devices, pair(): return lax.ppermute(x, 'row', [(i, i ^ 1) for i in range(4)])  15.7 us
    pallas_call x3, Pallas kernels, attend(): pl.pallas_call(functools.partial(attend_kernel, 1.0 / math.sqrt(head_size...  10.3 us
    ppermute x4, starting transfers between devices, swap(): return lax.ppermute(x, 'seq', [(0, 1), (1, 0)])  6.29 us
    ppermute x2, starting transfers between devices, pair(): return lax.ppermute(x, 'row', [(i, i ^ 1) for i in range(4)])  6.19 us
    ppermute x3, waiting for transfers between devices, inward(): return lax.ppermute(x, 'row', [(1, 0), (2, 3)])  5.8 us
    ppermute x6, waiting for transfers between devices, along(): return lax.ppermute(x, axis, [(i, i ^ mask) for i in range(4)])  5.02 us
    pallas_call x4, Pallas kernels, call(): pl.pallas_call(kernel, out_shape=out_shape, in_specs=specs, out_specs=out...  4.72 us
  transfers between devices with their start and end apart: 19, of which 8 were waited for; matrix products, arithmetic and copies ran while one was open for 0% of the time, Pallas kernels for 16%

profile of v4, /device:TPU:0, one launch (start us, length us, event | category | flops | bytes accessed | tf_op | source)
XLA Modules:
  0.0 86.8 jit_solution(5332670877796899830)
XLA Ops:
  0.0 3.3 %shard_map.82 = (bf16[2,384,384]{2,1,0:T(8,128)(2,1)}, bf16[4,384,384]{2,1,0:T(8,128)(2,1)}, bf16[384,384]{1,0:T(8,128)(2,1)}, bf16[384,384]{1,0:T(8,128)(2,1)}) custom-call(bf16[384,768]{1,0:T(8,128)(2,1)} %q_hbm.1, bf16[384,768]{1,0:T(8,128)(2,1)} %k_hbm.1, bf16[384,768]{1,0:T(8,128)(2,1)} %v_hbm.1, f32[6,128]{1,0:T(8,128)} %qg_hbm.1, f32[6,128]{1,0:T(8,128)} %kg_hbm.1, ...), custom_call_target="tpu_custom_call" | custom-call | flops 4718592 | bytes 3538944 | tf_op jit(solution)/shard_map/pallas_call | solution.py:166
  3.3 0.7 collective-permute-start.4
  4.1 5.8 %collective-permute-start.3 = (bf16[4,384,384]{2,1,0:T(8,128)(2,1)}, bf16[4,384,384]{2,1,0:T(8,128)(2,1)S(1)}, u32[]{:S(2)}, u32[]{:S(2)}) collective-permute-start(bf16[4,384,384]{2,1,0:T(8,128)(2,1)} %get-tuple-element.23.refs_2_.kvw), channel_id=1, source_target_pairs={{0,4},{4,0},{8,12},{12,8},{1,5},{5,1},{9,13},{13,9},{2,6},{6,2},{1... | collective-permute-start | bytes 3538952 | tf_op jit(solution)/shard_map/ppermute | solution.py:325
  9.9 1.5 %collective-permute-start = (bf16[2,384,384]{2,1,0:T(8,128)(2,1)}, bf16[2,384,384]{2,1,0:T(8,128)(2,1)S(1)}, u32[]{:S(2)}, u32[]{:S(2)}) collective-permute-start(bf16[2,384,384]{2,1,0:T(8,128)(2,1)} %get-tuple-element.22), channel_id=1, source_target_pairs={{0,16},{16,0},{1,17},{17,1},{2,18},{18,2},{3,19},{19,3},{4,20},{20... | collective-permute-start | bytes 1769480 | tf_op jit(solution)/shard_map/ppermute | solution.py:322
  11.4 13.2 %collective-permute-done.refs_1_ = bf16[2,384,384]{2,1,0:T(8,128)(2,1)S(1)} collective-permute-done((bf16[2,384,384]{2,1,0:T(8,128)(2,1)}, bf16[2,384,384]{2,1,0:T(8,128)(2,1)S(1)}, u32[]{:S(2)}, u32[]{:S(2)}) %collective-permute-start) | collective-permute-done | bytes 589856 | tf_op jit(solution)/shard_map/ppermute | solution.py:322
  24.6 0.4 collective-permute-start.1
  25.0 0.7 collective-permute-start.2
  25.7 1.6 %collective-permute-start.5 = (bf16[384,384]{1,0:T(8,128)(2,1)}, bf16[384,384]{1,0:T(8,128)(2,1)S(1)}, u32[]{:S(2)}, u32[]{:S(2)}) collective-permute-start(bf16[384,384]{1,0:T(8,128)(2,1)} %get-tuple-element.24), channel_id=1, source_target_pairs={{0,16},{16,0},{1,17},{17,1},{2,18},{18,2},{3,19},{19,3},{4,20},{20... | collective-permute-start | bytes 884744 | tf_op jit(solution)/shard_map/ppermute | solution.py:322
  27.3 0.0 collective-permute-done.4.refs_4_.kvw_mid
  27.3 0.1 slice.13
  27.4 9.6 %collective-permute-done.3.refs_3_.kvw_pair = bf16[4,384,384]{2,1,0:T(8,128)(2,1)S(1)} collective-permute-done((bf16[4,384,384]{2,1,0:T(8,128)(2,1)}, bf16[4,384,384]{2,1,0:T(8,128)(2,1)S(1)}, u32[]{:S(2)}, u32[]{:S(2)}) %collective-permute-start.3) | collective-permute-done | bytes 1179680 | tf_op jit(solution)/shard_map/ppermute | solution.py:325
  37.0 0.1 slice_bitcast_fusion
  37.0 0.0 collective-permute-done.5.refs_1_.refs_0_
  37.1 4.5 %shard_map.83 = (f32[3,2,384,128]{3,2,1,0:T(8,128)S(1)}, f32[3,2,384,256]{3,2,1,0:T(8,128)S(1)}) custom-call(bf16[384,384]{1,0:T(8,128)(2,1)S(1)} %copy-done.2, bf16[384,384]{1,0:T(8,128)(2,1)S(1)} %collective-permute-done.5.refs_1_.refs_0_, bf16[4,384,384]{2,1,0:T(8,128)(2,1)S(1)} %copy-done, ...), custom_call_target="tpu_custom_call" | custom-call | flops 2717908992 | bytes 8388608 | tf_op jit(solution)/shard_map/pallas_call | solution.py:241
  41.5 1.3 %collective-permute-start.10 = (bf16[2,384,384]{2,1,0:T(8,128)(2,1)S(1)}, bf16[2,384,384]{2,1,0:T(8,128)(2,1)S(1)}, u32[]{:S(2)}, u32[]{:S(2)}) collective-permute-start(bf16[2,384,384]{2,1,0:T(8,128)(2,1)S(1)} %slice.13), channel_id=1, source_target_pairs={{4,0},{8,12},{5,1},{9,13},{6,2},{10,14},{7,3},{11,15},{20,16},{24,... | collective-permute-start | bytes 1769480 | tf_op jit(solution)/shard_map/ppermute | solution.py:345
  42.8 0.7 collective-permute-start.11
  43.5 6.1 %collective-permute-done.1.refs_2_ = bf16[2,384,384]{2,1,0:T(8,128)(2,1)S(1)} collective-permute-done((bf16[2,384,384]{2,1,0:T(8,128)(2,1)S(1)}, bf16[2,384,384]{2,1,0:T(8,128)(2,1)S(1)}, u32[]{:S(2)}, u32[]{:S(2)}) %collective-permute-start.1) | collective-permute-done | bytes 589856 | tf_op jit(solution)/shard_map/ppermute | solution.py:325
  49.6 0.0 collective-permute-done.2.refs_3_
  49.6 2.9 %shard_map.84.a0 = bf16[384,384]{1,0:T(8,128)(2,1)S(1)} custom-call(bf16[384,384]{1,0:T(8,128)(2,1)S(1)} %collective-permute-done.5.refs_1_.refs_0_, bf16[2,384,384]{2,1,0:T(8,128)(2,1)S(1)} %collective-permute-done.refs_1_, bf16[2,384,384]{2,1,0:T(8,128)(2,1)S(1)} %collective-permute-done.1.refs_2_, ...), custom_call_target="tpu_custom_call" | custom-call | flops 1358954496 | bytes 8388608 | tf_op jit(solution)/shard_map/pallas_call | solution.py:241
  52.5 1.6 %collective-permute-start.15 = (bf16[384,384]{1,0:T(8,128)(2,1)S(1)}, bf16[384,384]{1,0:T(8,128)(2,1)S(1)}, u32[]{:S(2)}, u32[]{:S(2)}) collective-permute-start(bf16[384,384]{1,0:T(8,128)(2,1)S(1)} %shard_map.84.a0), channel_id=1, source_target_pairs={{0,2},{1,3},{2,0},{3,1},{4,6},{5,7},{6,4},{7,5},{8,10},{9,11},{10,... | collective-permute-start | bytes 884744 | tf_op jit(solution)/shard_map/ppermute | solution.py:331
  54.1 0.7 collective-permute-start.6
  54.8 0.1 collective-permute-start.14
  54.9 0.0 collective-permute-done.11.rest_0_.forward
  54.9 1.3 %collective-permute-start.12 = (bf16[384,384]{1,0:T(8,128)(2,1)S(1)}, bf16[384,384]{1,0:T(8,128)(2,1)S(1)}, u32[]{:S(2)}, u32[]{:S(2)}) collective-permute-start(bf16[384,384]{1,0:T(8,128)(2,1)S(1)} %collective-permute-done.11.rest_0_.forward), channel_id=1, source_target_pairs={{4,0},{8,12},{5,1},{9,13},{6,2},{10,14},{7,3},{11,15},{20,16},{24,... | collective-permute-start | bytes 884744 | tf_op jit(solution)/shard_map/ppermute | solution.py:345
  56.2 3.2 %collective-permute-done.15.a2 = bf16[384,384]{1,0:T(8,128)(2,1)S(1)} collective-permute-done((bf16[384,384]{1,0:T(8,128)(2,1)S(1)}, bf16[384,384]{1,0:T(8,128)(2,1)S(1)}, u32[]{:S(2)}, u32[]{:S(2)}) %collective-permute-start.15) | collective-permute-done | bytes 294944 | tf_op jit(solution)/shard_map/ppermute | solution.py:331
  59.3 0.0 collective-permute-start.16
  59.3 0.0 collective-permute-done.6.rest_1_.forward
  59.3 2.9 %shard_map.85.a0 = bf16[384,384]{1,0:T(8,128)(2,1)S(1)} custom-call(bf16[384,384]{1,0:T(8,128)(2,1)S(1)} %copy-done.2, bf16[2,384,384]{2,1,0:T(8,128)(2,1)S(1)} %collective-permute-done.refs_1_, bf16[2,384,384]{2,1,0:T(8,128)(2,1)S(1)} %collective-permute-done.1.refs_2_, bf16[2,384,384]{2,1,0:T(8,128)(2,1)S(1)} %collective-permute-done.2.refs_3_, ...), custom_call_target="tpu_custom_call" | custom-call | flops 1358954496 | bytes 8388608 | tf_op jit(solution)/shard_map/pallas_call | solution.py:241
  62.3 0.6 collective-permute-start.7
  62.9 0.0 collective-permute-done.14.a1
  62.9 1.5 %collective-permute-start.8 = (bf16[384,384]{1,0:T(8,128)(2,1)S(1)}, bf16[384,384]{1,0:T(8,128)(2,1)S(1)}, u32[]{:S(2)}, u32[]{:S(2)}) collective-permute-start(bf16[384,384]{1,0:T(8,128)(2,1)S(1)} %shard_map.85.a0), channel_id=1, source_target_pairs={{0,2},{1,3},{2,0},{3,1},{4,6},{5,7},{6,4},{7,5},{8,10},{9,11},{10,... | collective-permute-start | bytes 884744 | tf_op jit(solution)/shard_map/ppermute | solution.py:331
  64.4 0.0 collective-permute-done.10.inner
  64.4 1.5 %collective-permute-start.13 = (bf16[384,384]{1,0:T(8,128)(2,1)S(1)}, bf16[384,384]{1,0:T(8,128)(2,1)S(1)}, u32[]{:S(2)}, u32[]{:S(2)}) collective-permute-start(bf16[384,384]{1,0:T(8,128)(2,1)S(1)} %collective-permute-done.6.rest_1_.forward), channel_id=1, source_target_pairs={{4,0},{8,12},{5,1},{9,13},{6,2},{10,14},{7,3},{11,15},{20,16},{24,... | collective-permute-start | bytes 884744 | tf_op jit(solution)/shard_map/ppermute | solution.py:345
  65.8 1.6 %collective-permute-done.12.rest_2_.outer = bf16[384,384]{1,0:T(8,128)(2,1)S(1)} collective-permute-done((bf16[384,384]{1,0:T(8,128)(2,1)S(1)}, bf16[384,384]{1,0:T(8,128)(2,1)S(1)}, u32[]{:S(2)}, u32[]{:S(2)}) %collective-permute-start.12) | collective-permute-done | bytes 294944 | tf_op jit(solution)/shard_map/ppermute | solution.py:345
  67.4 0.0 collective-permute-done.16.a3
  67.4 1.0 %shard_map.87 = bf16[384,384]{1,0:T(8,128)(2,1)S(1)} custom-call(bf16[384,384]{1,0:T(8,128)(2,1)S(1)} %shard_map.84.a0, bf16[384,384]{1,0:T(8,128)(2,1)S(1)} %collective-permute-done.14.a1, bf16[384,384]{1,0:T(8,128)(2,1)S(1)} %collective-permute-done.15.a2, bf16[384,384]{1,0:T(8,128)(2,1)S(1)} %collective-permute-done.16.a3, ...), custom_call_target="tpu_custom_call" | custom-call | flops 4529848320 | bytes 2097152 | tf_op jit(solution)/shard_map/pallas_call | solution.py:334
  68.4 0.0 copy-start.3
  68.4 0.0 copy-start.1
  68.4 1.6 %collective-permute-start.17 = (bf16[384,384]{1,0:T(8,128)(2,1)S(1)}, bf16[384,384]{1,0:T(8,128)(2,1)S(1)}, u32[]{:S(2)}, u32[]{:S(2)}) collective-permute-start(bf16[384,384]{1,0:T(8,128)(2,1)S(1)} %shard_map.87), channel_id=1, source_target_pairs={{0,16},{16,0},{1,17},{17,1},{2,18},{18,2},{3,19},{19,3},{4,20},{20... | collective-permute-start | bytes 884744 | tf_op jit(solution)/shard_map/ppermute | solution.py:322
  70.0 1.8 %collective-permute-done.8.a2 = bf16[384,384]{1,0:T(8,128)(2,1)S(1)} collective-permute-done((bf16[384,384]{1,0:T(8,128)(2,1)S(1)}, bf16[384,384]{1,0:T(8,128)(2,1)S(1)}, u32[]{:S(2)}, u32[]{:S(2)}) %collective-permute-start.8) | collective-permute-done | bytes 294944 | tf_op jit(solution)/shard_map/ppermute | solution.py:331
  71.9 0.0 collective-permute-start.9
  71.9 4.2 %collective-permute-done.13.rest_3_.outer = bf16[384,384]{1,0:T(8,128)(2,1)S(1)} collective-permute-done((bf16[384,384]{1,0:T(8,128)(2,1)S(1)}, bf16[384,384]{1,0:T(8,128)(2,1)S(1)}, u32[]{:S(2)}, u32[]{:S(2)}) %collective-permute-start.13) | collective-permute-done | bytes 294944 | tf_op jit(solution)/shard_map/ppermute | solution.py:345
  76.1 1.0 %shard_map.88 = bf16[384,384]{1,0:T(8,128)(2,1)S(1)} custom-call(bf16[384,384]{1,0:T(8,128)(2,1)S(1)} %shard_map.84.a0, bf16[384,384]{1,0:T(8,128)(2,1)S(1)} %collective-permute-done.14.a1, bf16[384,384]{1,0:T(8,128)(2,1)S(1)} %collective-permute-done.15.a2, bf16[384,384]{1,0:T(8,128)(2,1)S(1)} %collective-permute-done.16.a3, ...), custom_call_target="tpu_custom_call" | custom-call | flops 4529848320 | bytes 2097152 | tf_op jit(solution)/shard_map/pallas_call | solution.py:334
  77.1 1.6 %collective-permute-start.18 = (bf16[384,384]{1,0:T(8,128)(2,1)S(1)}, bf16[384,384]{1,0:T(8,128)(2,1)S(1)}, u32[]{:S(2)}, u32[]{:S(2)}) collective-permute-start(bf16[384,384]{1,0:T(8,128)(2,1)S(1)} %shard_map.88), channel_id=1, source_target_pairs={{0,16},{16,0},{1,17},{17,1},{2,18},{18,2},{3,19},{19,3},{4,20},{20... | collective-permute-start | bytes 884744 | tf_op jit(solution)/shard_map/ppermute | solution.py:322
  78.7 0.0 collective-permute-done.7.a1
  78.7 1.8 %shard_map.86.base = f32[384,768]{1,0:T(8,128)S(1)} custom-call(bf16[384,384]{1,0:T(8,128)(2,1)S(1)} %shard_map.85.a0, bf16[384,384]{1,0:T(8,128)(2,1)S(1)} %collective-permute-done.7.a1, bf16[384,384]{1,0:T(8,128)(2,1)S(1)} %collective-permute-done.8.a2, bf16[384,384]{1,0:T(8,128)(2,1)S(1)} %collective-permute-done.9.a3, bf16[4,384,384]{2,1,0:T(8,128)(2,1)S(1)} %copy-done, ...), custom_call_target="tpu_custom_call" | custom-call | flops 905969664 | bytes 2097152 | tf_op jit(solution)/shard_map/pallas_call | solution.py:334
  80.6 5.1 %collective-permute-done.18.rest_1_ = bf16[384,384]{1,0:T(8,128)(2,1)S(1)} collective-permute-done((bf16[384,384]{1,0:T(8,128)(2,1)S(1)}, bf16[384,384]{1,0:T(8,128)(2,1)S(1)}, u32[]{:S(2)}, u32[]{:S(2)}) %collective-permute-start.18) | collective-permute-done | bytes 294944 | tf_op jit(solution)/shard_map/ppermute | solution.py:322
  85.7 0.9 %shard_map.89 = bf16[384,768]{1,0:T(8,128)(2,1)} custom-call(f32[384,768]{1,0:T(8,128)S(1)} %shard_map.86.base, f32[1,768]{1,0:T(1,128)S(1)} %reshape.3.gate, bf16[384,384]{1,0:T(8,128)(2,1)S(1)} %collective-permute-done.17.rest_0_, bf16[384,384]{1,0:T(8,128)(2,1)S(1)} %collective-permute-done.18.rest_1_), custom_call_target="tpu_custom_call" | custom-call | flops 1179648 | bytes 2097152 | tf_op jit(solution)/shard_map/pallas_call | solution.py:334
  (9 shorter events, 0.0 us)
Async XLA Ops:
  3.3 24.0 %collective-permute-start.4 = (bf16[4,384,384]{2,1,0:T(8,128)(2,1)}, bf16[4,384,384]{2,1,0:T(8,128)(2,1)S(1)}, u32[]{:S(2)}, u32[]{:S(2)}) collective-permute-start(bf16[4,384,384]{2,1,0:T(8,128)(2,1)} %get-tuple-element.23.refs_2_.kvw), channel_id=1, source_target_pairs={{4,8},{8,4},{5,9},{9,5},{6,10},{10,6},{7,11},{11,7},{20,24},{24,20... | collective-permute-start | bytes 3538952 | tf_op jit(solution)/shard_map/ppermute | solution.py:328
  4.1 32.9 %collective-permute-start.3 = (bf16[4,384,384]{2,1,0:T(8,128)(2,1)}, bf16[4,384,384]{2,1,0:T(8,128)(2,1)S(1)}, u32[]{:S(2)}, u32[]{:S(2)}) collective-permute-start(bf16[4,384,384]{2,1,0:T(8,128)(2,1)} %get-tuple-element.23.refs_2_.kvw), channel_id=1, source_target_pairs={{0,4},{4,0},{8,12},{12,8},{1,5},{5,1},{9,13},{13,9},{2,6},{6,2},{1... | collective-permute-start | bytes 3538952 | tf_op jit(solution)/shard_map/ppermute | solution.py:325
  9.9 14.7 %collective-permute-start = (bf16[2,384,384]{2,1,0:T(8,128)(2,1)}, bf16[2,384,384]{2,1,0:T(8,128)(2,1)S(1)}, u32[]{:S(2)}, u32[]{:S(2)}) collective-permute-start(bf16[2,384,384]{2,1,0:T(8,128)(2,1)} %get-tuple-element.22), channel_id=1, source_target_pairs={{0,16},{16,0},{1,17},{17,1},{2,18},{18,2},{3,19},{19,3},{4,20},{20... | collective-permute-start | bytes 1769480 | tf_op jit(solution)/shard_map/ppermute | solution.py:322
  24.6 25.0 %collective-permute-start.1 = (bf16[2,384,384]{2,1,0:T(8,128)(2,1)S(1)}, bf16[2,384,384]{2,1,0:T(8,128)(2,1)S(1)}, u32[]{:S(2)}, u32[]{:S(2)}) collective-permute-start(bf16[2,384,384]{2,1,0:T(8,128)(2,1)S(1)} %collective-permute-done.refs_1_), channel_id=1, source_target_pairs={{0,4},{4,0},{8,12},{12,8},{1,5},{5,1},{9,13},{13,9},{2,6},{6,2},{1... | collective-permute-start | bytes 1769480 | tf_op jit(solution)/shard_map/ppermute | solution.py:325
  25.0 24.6 %collective-permute-start.2 = (bf16[2,384,384]{2,1,0:T(8,128)(2,1)S(1)}, bf16[2,384,384]{2,1,0:T(8,128)(2,1)S(1)}, u32[]{:S(2)}, u32[]{:S(2)}) collective-permute-start(bf16[2,384,384]{2,1,0:T(8,128)(2,1)S(1)} %collective-permute-done.refs_1_), channel_id=1, source_target_pairs={{4,8},{8,4},{5,9},{9,5},{6,10},{10,6},{7,11},{11,7},{20,24},{24,20... | collective-permute-start | bytes 1769480 | tf_op jit(solution)/shard_map/ppermute | solution.py:328
  25.7 11.3 %copy-start = (bf16[4,384,384]{2,1,0:T(8,128)(2,1)S(1)}, bf16[4,384,384]{2,1,0:T(8,128)(2,1)}, u32[]{:S(2)}) copy-start(bf16[4,384,384]{2,1,0:T(8,128)(2,1)} %get-tuple-element.23.refs_2_.kvw) | copy-start | bytes 3538948
  25.7 11.3 %copy-start.2 = (bf16[384,384]{1,0:T(8,128)(2,1)S(1)}, bf16[384,384]{1,0:T(8,128)(2,1)}, u32[]{:S(2)}) copy-start(bf16[384,384]{1,0:T(8,128)(2,1)} %get-tuple-element.21.refs_0_) | copy-start | bytes 884740
  25.7 11.3 %collective-permute-start.5 = (bf16[384,384]{1,0:T(8,128)(2,1)}, bf16[384,384]{1,0:T(8,128)(2,1)S(1)}, u32[]{:S(2)}, u32[]{:S(2)}) collective-permute-start(bf16[384,384]{1,0:T(8,128)(2,1)} %get-tuple-element.24), channel_id=1, source_target_pairs={{0,16},{16,0},{1,17},{17,1},{2,18},{18,2},{3,19},{19,3},{4,20},{20... | collective-permute-start | bytes 884744 | tf_op jit(solution)/shard_map/ppermute | solution.py:322
  41.5 22.9 %collective-permute-start.10 = (bf16[2,384,384]{2,1,0:T(8,128)(2,1)S(1)}, bf16[2,384,384]{2,1,0:T(8,128)(2,1)S(1)}, u32[]{:S(2)}, u32[]{:S(2)}) collective-permute-start(bf16[2,384,384]{2,1,0:T(8,128)(2,1)S(1)} %slice.13), channel_id=1, source_target_pairs={{4,0},{8,12},{5,1},{9,13},{6,2},{10,14},{7,3},{11,15},{20,16},{24,... | collective-permute-start | bytes 1769480 | tf_op jit(solution)/shard_map/ppermute | solution.py:345
  42.8 12.0 %collective-permute-start.11 = (bf16[384,384]{1,0:T(8,128)(2,1)S(1)}, bf16[384,384]{1,0:T(8,128)(2,1)S(1)}, u32[]{:S(2)}, u32[]{:S(2)}) collective-permute-start(bf16[384,384]{1,0:T(8,128)(2,1)S(1)} %get-tuple-element.33), channel_id=1, source_target_pairs={{4,8},{8,4},{5,9},{9,5},{6,10},{10,6},{7,11},{11,7},{20,24},{24,20... | collective-permute-start | bytes 884744 | tf_op jit(solution)/shard_map/ppermute | solution.py:328
  52.5 6.8 %collective-permute-start.15 = (bf16[384,384]{1,0:T(8,128)(2,1)S(1)}, bf16[384,384]{1,0:T(8,128)(2,1)S(1)}, u32[]{:S(2)}, u32[]{:S(2)}) collective-permute-start(bf16[384,384]{1,0:T(8,128)(2,1)S(1)} %shard_map.84.a0), channel_id=1, source_target_pairs={{0,2},{1,3},{2,0},{3,1},{4,6},{5,7},{6,4},{7,5},{8,10},{9,11},{10,... | collective-permute-start | bytes 884744 | tf_op jit(solution)/shard_map/ppermute | solution.py:331
  54.1 5.2 %collective-permute-start.6 = (bf16[384,384]{1,0:T(8,128)(2,1)S(1)}, bf16[384,384]{1,0:T(8,128)(2,1)S(1)}, u32[]{:S(2)}, u32[]{:S(2)}) collective-permute-start(bf16[384,384]{1,0:T(8,128)(2,1)S(1)} %get-tuple-element.29), channel_id=1, source_target_pairs={{4,8},{8,4},{5,9},{9,5},{6,10},{10,6},{7,11},{11,7},{20,24},{24,20... | collective-permute-start | bytes 884744 | tf_op jit(solution)/shard_map/ppermute | solution.py:328
  54.8 8.1 %collective-permute-start.14 = (bf16[384,384]{1,0:T(8,128)(2,1)S(1)}, bf16[384,384]{1,0:T(8,128)(2,1)S(1)}, u32[]{:S(2)}, u32[]{:S(2)}) collective-permute-start(bf16[384,384]{1,0:T(8,128)(2,1)S(1)} %shard_map.84.a0), channel_id=1, source_target_pairs={{0,1},{1,0},{2,3},{3,2},{4,5},{5,4},{6,7},{7,6},{8,9},{9,8},{10,11... | collective-permute-start | bytes 884744 | tf_op jit(solution)/shard_map/ppermute | solution.py:331
  54.9 12.5 %collective-permute-start.12 = (bf16[384,384]{1,0:T(8,128)(2,1)S(1)}, bf16[384,384]{1,0:T(8,128)(2,1)S(1)}, u32[]{:S(2)}, u32[]{:S(2)}) collective-permute-start(bf16[384,384]{1,0:T(8,128)(2,1)S(1)} %collective-permute-done.11.rest_0_.forward), channel_id=1, source_target_pairs={{4,0},{8,12},{5,1},{9,13},{6,2},{10,14},{7,3},{11,15},{20,16},{24,... | collective-permute-start | bytes 884744 | tf_op jit(solution)/shard_map/ppermute | solution.py:345
  59.3 8.1 %collective-permute-start.16 = (bf16[384,384]{1,0:T(8,128)(2,1)S(1)}, bf16[384,384]{1,0:T(8,128)(2,1)S(1)}, u32[]{:S(2)}, u32[]{:S(2)}) collective-permute-start(bf16[384,384]{1,0:T(8,128)(2,1)S(1)} %collective-permute-done.15.a2), channel_id=1, source_target_pairs={{0,1},{1,0},{2,3},{3,2},{4,5},{5,4},{6,7},{7,6},{8,9},{9,8},{10,11... | collective-permute-start | bytes 884744 | tf_op jit(solution)/shard_map/ppermute | solution.py:331
  62.3 16.4 %collective-permute-start.7 = (bf16[384,384]{1,0:T(8,128)(2,1)S(1)}, bf16[384,384]{1,0:T(8,128)(2,1)S(1)}, u32[]{:S(2)}, u32[]{:S(2)}) collective-permute-start(bf16[384,384]{1,0:T(8,128)(2,1)S(1)} %shard_map.85.a0), channel_id=1, source_target_pairs={{0,1},{1,0},{2,3},{3,2},{4,5},{5,4},{6,7},{7,6},{8,9},{9,8},{10,11... | collective-permute-start | bytes 884744 | tf_op jit(solution)/shard_map/ppermute | solution.py:331
  62.9 9.0 %collective-permute-start.8 = (bf16[384,384]{1,0:T(8,128)(2,1)S(1)}, bf16[384,384]{1,0:T(8,128)(2,1)S(1)}, u32[]{:S(2)}, u32[]{:S(2)}) collective-permute-start(bf16[384,384]{1,0:T(8,128)(2,1)S(1)} %shard_map.85.a0), channel_id=1, source_target_pairs={{0,2},{1,3},{2,0},{3,1},{4,6},{5,7},{6,4},{7,5},{8,10},{9,11},{10,... | collective-permute-start | bytes 884744 | tf_op jit(solution)/shard_map/ppermute | solution.py:331
  64.4 11.7 %collective-permute-start.13 = (bf16[384,384]{1,0:T(8,128)(2,1)S(1)}, bf16[384,384]{1,0:T(8,128)(2,1)S(1)}, u32[]{:S(2)}, u32[]{:S(2)}) collective-permute-start(bf16[384,384]{1,0:T(8,128)(2,1)S(1)} %collective-permute-done.6.rest_1_.forward), channel_id=1, source_target_pairs={{4,0},{8,12},{5,1},{9,13},{6,2},{10,14},{7,3},{11,15},{20,16},{24,... | collective-permute-start | bytes 884744 | tf_op jit(solution)/shard_map/ppermute | solution.py:345
  68.4 10.3 %copy-start.3 = (f32[768]{0:T(1024)S(1)}, f32[768]{0:T(1024)}, u32[]{:S(2)}) copy-start(f32[768]{0:T(1024)} %param.15) | copy-start | bytes 9220
  68.4 10.3 %copy-start.1 = (bf16[384,768]{1,0:T(8,128)(2,1)S(1)}, bf16[384,768]{1,0:T(8,128)(2,1)}, u32[]{:S(2)}) copy-start(bf16[384,768]{1,0:T(8,128)(2,1)} %stream_hbm.1) | copy-start | bytes 1769476
  68.4 12.1 %collective-permute-start.17 = (bf16[384,384]{1,0:T(8,128)(2,1)S(1)}, bf16[384,384]{1,0:T(8,128)(2,1)S(1)}, u32[]{:S(2)}, u32[]{:S(2)}) collective-permute-start(bf16[384,384]{1,0:T(8,128)(2,1)S(1)} %shard_map.87), channel_id=1, source_target_pairs={{0,16},{16,0},{1,17},{17,1},{2,18},{18,2},{3,19},{19,3},{4,20},{20... | collective-permute-start | bytes 884744 | tf_op jit(solution)/shard_map/ppermute | solution.py:322
  71.9 6.8 %collective-permute-start.9 = (bf16[384,384]{1,0:T(8,128)(2,1)S(1)}, bf16[384,384]{1,0:T(8,128)(2,1)S(1)}, u32[]{:S(2)}, u32[]{:S(2)}) collective-permute-start(bf16[384,384]{1,0:T(8,128)(2,1)S(1)} %collective-permute-done.8.a2), channel_id=1, source_target_pairs={{0,1},{1,0},{2,3},{3,2},{4,5},{5,4},{6,7},{7,6},{8,9},{9,8},{10,11... | collective-permute-start | bytes 884744 | tf_op jit(solution)/shard_map/ppermute | solution.py:331
  77.1 8.6 %collective-permute-start.18 = (bf16[384,384]{1,0:T(8,128)(2,1)S(1)}, bf16[384,384]{1,0:T(8,128)(2,1)S(1)}, u32[]{:S(2)}, u32[]{:S(2)}) collective-permute-start(bf16[384,384]{1,0:T(8,128)(2,1)S(1)} %shard_map.88), channel_id=1, source_target_pairs={{0,16},{16,0},{1,17},{17,1},{2,18},{18,2},{3,19},{19,3},{4,20},{20... | collective-permute-start | bytes 884744 | tf_op jit(solution)/shard_map/ppermute | solution.py:322

commit v5 on v4

--- a/solution.py
+++ b/solution.py
@@ -100,7 +100,7 @@
 ABSENT = 1e30
 LOG2_E = 1.4426950408889634
 MIB = 1 << 20
-CHUNKS = 2
+CUT = 3
 FIRST_VMEM = 60 * MIB
 LAST_VMEM = 16 * MIB
 
@@ -113,65 +113,87 @@
     return pl.BlockSpec(memory_space=pltpu.HBM)
 
 
+def normed(ref, gain_ref, part, out):
+    head_size = gain_ref.shape[1]
+    half = out.shape[1]
+    count = half // head_size
+    for index in range(count):
+        start = pl.multiple_of(part * half + index * head_size, head_size)
+        x = ref[:, pl.ds(start, head_size)].astype(jnp.float32)
+        mean_square = jnp.mean(x * x, axis=-1, keepdims=True)
+        gain = gain_ref[pl.ds(part * count + index, 1), :]
+        scaled = x * lax.rsqrt(mean_square + EPSILON) * gain
+        out[:, index * head_size : (index + 1) * head_size] = scaled.astype(jnp.bfloat16)
+
+
 def prep_kernel(
-    q_hbm, k_hbm, v_hbm, qg_hbm, kg_hbm, w_hbm, kv_send, kvw_keep, q_send, q_keep, *rest
+    k_hbm, v_hbm, kg_hbm, w_hbm, kv_send, kvw_keep, k_ref, kg_ref, sems
 ):
-    q_ref, k_ref, qg_ref, kg_ref, sems = rest
     mine = lax.axis_index("seq")
-    half = q_keep.shape[1]
-    head_size = qg_ref.shape[1]
-    count = half // head_size
+    half = kv_send.shape[1] // 2
     rows = pl.ds(pl.multiple_of(mine * half, half), half)
-    moved = [(kg_hbm, kg_ref), (k_hbm, k_ref), (qg_hbm, qg_ref), (q_hbm, q_ref)]
+    moved = [(kg_hbm, kg_ref), (k_hbm, k_ref)]
     for part, out in ((1 - mine, kv_send), (mine, kvw_keep)):
-        moved.append((v_hbm.at[:, pl.ds(pl.multiple_of(part * half, half), half)], out.at[1]))
-    for index in range(2):
-        moved.append((w_hbm.at[rows, index * half : (index + 1) * half], kvw_keep.at[2 + index]))
+        moved.append((v_hbm.at[:, pl.ds(pl.multiple_of(part * half, half), half)], out.at[:, half : 2 * half]))
+    moved.append((w_hbm.at[rows, :], kvw_keep.at[:, 2 * half :]))
     copies = [
         pltpu.make_async_copy(source, target, sems.at[index]) for index, (source, target) in enumerate(moved)
     ]
     for copy in copies:
         copy.start()
 
-    def normed(ref, gain_ref, part, out):
-        for index in range(count):
-            start = pl.multiple_of(part * half + index * head_size, head_size)
-            x = ref[:, pl.ds(start, head_size)].astype(jnp.float32)
-            mean_square = jnp.mean(x * x, axis=-1, keepdims=True)
-            gain = gain_ref[pl.ds(part * count + index, 1), :]
-            scaled = x * lax.rsqrt(mean_square + EPSILON) * gain
-            out[:, index * head_size : (index + 1) * head_size] = scaled.astype(jnp.bfloat16)
-
-    halves = ((1 - mine, kv_send, q_send), (mine, kvw_keep, q_keep))
     copies[0].wait()
     copies[1].wait()
-    for part, kv_out, _ in halves:
-        normed(k_ref, kg_ref, part, kv_out.at[0])
-    copies[2].wait()
-    copies[3].wait()
-    for part, _, q_out in halves:
+    for part, kv_out in ((1 - mine, kv_send), (mine, kvw_keep)):
+        normed(k_ref, kg_ref, part, kv_out.at[:, :half])
+    for copy in copies[2:]:
+        copy.wait()
+
+
+def query_kernel(q_hbm, qg_hbm, q_send, q_keep, q_ref, qg_ref, sems):
+    mine = lax.axis_index("seq")
+    copies = [
+        pltpu.make_async_copy(qg_hbm, qg_ref, sems.at[0]),
+        pltpu.make_async_copy(q_hbm, q_ref, sems.at[1]),
+    ]
+    for copy in copies:
+        copy.start()
+    for copy in copies:
+        copy.wait()
+    for part, q_out in ((1 - mine, q_send), (mine, q_keep)):
         normed(q_ref, qg_ref, part, q_out)
-    for copy in copies[4:]:
-        copy.wait()
 
 
 def prep(q, k, v, q_gain, k_gain, out_weight):
     rows, width = q.shape
     half = width // 2
     one = jax.ShapeDtypeStruct((rows, half), jnp.bfloat16)
-    two = jax.ShapeDtypeStruct((2, rows, half), jnp.bfloat16)
-    four = jax.ShapeDtypeStruct((4, rows, half), jnp.bfloat16)
+    two = jax.ShapeDtypeStruct((rows, width), jnp.bfloat16)
+    four = jax.ShapeDtypeStruct((rows, width + out_weight.shape[1]), jnp.bfloat16)
     block = pltpu.VMEM((rows, width), jnp.bfloat16)
     gain = pltpu.VMEM(q_gain.shape, jnp.float32)
-    return pl.pallas_call(
+    params = pltpu.CompilerParams(vmem_limit_bytes=FIRST_VMEM)
+    cost = pl.CostEstimate(flops=rows * width * 8, bytes_accessed=rows * width * 6, transcendentals=0)
+    kv_send, kvw = pl.pallas_call(
         prep_kernel,
-        out_shape=[two, four, one, one],
-        in_specs=[hbm_spec()] * 6,
-        out_specs=[vmem_spec()] * 4,
-        scratch_shapes=[block, block, gain, gain, pltpu.SemaphoreType.DMA((8,))],
-        compiler_params=pltpu.CompilerParams(vmem_limit_bytes=FIRST_VMEM),
-        cost_estimate=pl.CostEstimate(flops=rows * width * 16, bytes_accessed=rows * width * 12, transcendentals=0),
-    )(q, k, v, q_gain, k_gain, out_weight)
+        out_shape=[two, four],
+        in_specs=[hbm_spec()] * 4,
+        out_specs=[vmem_spec()] * 2,
+        scratch_shapes=[block, gain, pltpu.SemaphoreType.DMA((5,))],
+        compiler_params=params,
+        cost_estimate=cost,
+    )(k, v, k_gain, out_weight)
+    kvw, q = lax.optimization_barrier((kvw, q))
+    q_send, q_keep = pl.pallas_call(
+        query_kernel,
+        out_shape=[one, one],
+        in_specs=[hbm_spec()] * 2,
+        out_specs=[vmem_spec()] * 2,
+        scratch_shapes=[block, gain, pltpu.SemaphoreType.DMA((2,))],
+        compiler_params=pltpu.CompilerParams(vmem_limit_bytes=LAST_VMEM),
+        cost_estimate=cost,
+    )(q, q_gain)
+    return kv_send, kvw, q_send, q_keep
 
 
 def attend_kernel(scale, first, head_size, times, *refs):
@@ -180,14 +202,15 @@
     refs = refs[3:]
     height = lax.axis_index("row")
     flags = [None, None, (height > 0) & (height < lax.axis_size("row") - 1)]
-    rows = kv0.shape[1]
+    rows, half = queries[0].shape
     factor = scale * LOG2_E
     ones = jnp.ones((rows, head_size), jnp.bfloat16)
 
     for index in range(queries[0].shape[1] // head_size):
         columns = slice(index * head_size, (index + 1) * head_size)
-        keys = [kv[0, :, columns] for kv in (kv0, kv1, kv2)]
-        values = [jnp.concatenate([kv[1, :, columns], ones], axis=1) for kv in (kv0, kv1, kv2)]
+        beside = slice(half + index * head_size, half + (index + 1) * head_size)
+        keys = [kv[:, columns] for kv in (kv0, kv1, kv2)]
+        values = [jnp.concatenate([kv[:, beside], ones], axis=1) for kv in (kv0, kv1, kv2)]
         for which, q_ref in zip(times, queries):
             q = q_ref[:, columns]
             scores = [
@@ -266,27 +289,30 @@
                 write(part, low, high, total)
 
 
-def weight_of(kvw, kvw_pair, kvw_mid, inner, forward, outer, which, part):
+def weight_of(kvw, kvw_pair, kvw_mid, inner, forward, outer, which, low, high):
+    start = kvw.shape[1] - kvw.shape[0] * 2
+    columns = slice(start + low, start + high)
     if which == 2:
-        return inner[part] + forward(part)
+        return inner + forward
     if which == 3:
-        return kvw_mid[2 + part] + outer[part][...]
-    return (kvw, kvw_pair)[which][2 + part]
-
-
-def peer_kernel(part, a0, a1, a2, a3, kvw, kvw_pair, kvw_mid, inner, forward, outer, out):
-    def write(unused, low, high, total):
+        return kvw_mid[:, columns] + outer
+    return (kvw, kvw_pair)[which][:, columns]
+
+
+def peer_kernel(span, a0, a1, a2, a3, kvw, kvw_pair, kvw_mid, inner, forward, outer, out):
+    def write(part, low, high, total):
         out[...] = total.astype(out.dtype)
 
-    def weights(which, unused, low, high):
-        return weight_of(kvw, kvw_pair, kvw_mid, inner, lambda p: forward[...], {part: outer}, which, part)
-
-    plane_sum([a[...] for a in (a0, a1, a2, a3)], weights, [(0, out.shape[1])], write)
-
-
-def own_kernel(spans, a0, a1, a2, a3, kvw, kvw_pair, kvw_mid, inner, gate, stream_hbm, *rest):
-    forward, outer = rest[:2], rest[2 : 4]
-    out, stream, sem = rest[4 :]
+    def weights(which, part, low, high):
+        held = inner[:, slice(*span)], forward[...], outer[...]
+        return weight_of(kvw, kvw_pair, kvw_mid, *held, which, low, high)
+
+    plane_sum([a[...] for a in (a0, a1, a2, a3)], weights, [span], write)
+
+
+def own_kernel(spans, a0, a1, a2, a3, kvw, kvw_pair, kvw_mid, gate, stream_hbm, *rest):
+    forward, outer, inner = rest[:2], rest[2:4], rest[4:-3]
+    out, stream, sem = rest[-3:]
     copy = pltpu.make_async_copy(stream_hbm, stream, sem)
     copy.start()
     copy.wait()
@@ -295,7 +321,8 @@
         out[:, low:high] = stream[:, low:high].astype(jnp.float32) + gate[:, low:high] * total
 
     def weights(which, part, low, high):
-        return weight_of(kvw, kvw_pair, kvw_mid, inner, lambda p: forward[p][...], outer, which, part)
+        held = inner[0][:, low:high], forward[part][...], outer[part][...]
+        return weight_of(kvw, kvw_pair, kvw_mid, *held, which, low, high)
 
     plane_sum([a[...] for a in (a0, a1, a2, a3)], weights, spans, write)
 
@@ -316,7 +343,8 @@
     head_size = q_gain.shape[1]
     tokens, width = stream.shape
     rows = lax.axis_size("row")
-    spans = [(width * i // CHUNKS, width * (i + 1) // CHUNKS) for i in range(CHUNKS)]
+    cut = width // 6 * CUT
+    spans = [(0, cut), (cut, width)]
 
     def swap(x):
         return lax.ppermute(x, "seq", [(0, 1), (1, 0)])
@@ -352,12 +380,14 @@
     peer_pair, peer_mid = pair(kv_peer), middle(kv_peer)
 
     carry = attend((0, 1), [q_keep, q_peer], [kvw, kvw_pair, kvw_mid], head_size)
-    first_pair, early_mid, carry = barrier((kvw_pair[2], kvw_mid[2:], carry))
-    inner, forwards = inward(early_mid), [middle(first_pair)]
+    starts = [width + low for low, high in spans] + [2 * width]
+    halves = [slice(starts[part], starts[part + 1]) for part in range(2)]
+    first_pair, early_mid, carry = barrier((kvw_pair[:, halves[0]], kvw_mid[:, width:], carry))
+    inner, forwards = [inward(early_mid)], [middle(first_pair)]
     layers = [kv_peer, peer_pair, peer_mid]
     theirs = attend((1,), [q_peer], layers, head_size, carry)
     across_theirs, beside_theirs = along(theirs, "col", 2), along(theirs, "col", 1)
-    next_pair = barrier((kvw_pair[3], theirs))[0]
+    next_pair, _ = barrier((kvw_pair[:, halves[1]], theirs))
     forwards.append(middle(next_pair))
     outer = [inward(forwards[part]) for part in range(2)]
 
@@ -367,8 +397,8 @@
     sents = []
     for part, (low, high) in enumerate(spans):
         sent = call(
-            functools.partial(peer_kernel, part),
-            [*groups, kvw, kvw_pair, kvw_mid, inner, forwards[part], outer[part]],
+            functools.partial(peer_kernel, (low, high)),
+            [*groups, kvw, kvw_pair, kvw_mid, inner[0], forwards[part], outer[part]],
             [vmem] * 10,
             jax.ShapeDtypeStruct((tokens, high - low), jnp.bfloat16),
             vmem,
@@ -379,14 +409,14 @@
             sent, groups[0] = barrier((sent, groups[0]))
         sents.append(sent)
     received = [swap(sent) for sent in sents]
-    carry, forwards[1] = barrier((carry, forwards[1]))
+    carry, forwards[1], inner[0] = barrier((carry, forwards[1], inner[0]))
     mine = attend((0,), [q_keep], layers, head_size, carry)
     across_mine, beside_mine = along(mine, "col", 2), along(mine, "col", 1)
     groups = [mine, beside_mine, across_mine, along(across_mine, "col", 1)]
     base = call(
         functools.partial(own_kernel, spans),
-        [*groups, kvw, kvw_pair, kvw_mid, inner, gate, stream, *forwards, *outer],
-        [vmem] * 9 + [hbm] + [vmem] * 4,
+        [*groups, kvw, kvw_pair, kvw_mid, gate, stream, *forwards, *outer, *inner],
+        [vmem] * 8 + [hbm] + [vmem] * (4 + len(inner)),
         jax.ShapeDtypeStruct((tokens, width), jnp.float32),
         vmem,
         [pltpu.VMEM((tokens, width), stream.dtype), pltpu.SemaphoreType.DMA(())],
@@ -395,10 +425,10 @@
     return call(
         functools.partial(final_kernel, spans),
         [base, gate, *received],
-        [vmem] * (2 + CHUNKS),
+        [vmem] * (2 + len(received)),
         jax.ShapeDtypeStruct((tokens, width), jnp.bfloat16),
         hbm,
-        [pltpu.VMEM((tokens, width), jnp.bfloat16), pltpu.SemaphoreType.DMA((CHUNKS,))],
+        [pltpu.VMEM((tokens, width), jnp.bfloat16), pltpu.SemaphoreType.DMA((len(spans),))],
         tokens * width * 4,
     )
 

time: 87 us -> 86.1 us (0.990)
  waiting for transfers between devices: 44.9 us -> 43 us
    ppermute x3, waiting for transfers between devices: 5.8 us -> 1.67 us  [inward(): return lax.ppermute(x, 'row', [(1, 0), (2, 3)])]
    ppermute x6, waiting for transfers between devices: 5.02 us -> 7.18 us  [along(): return lax.ppermute(x, axis, [(i, i ^ mask) for i in range(4)])]
    pallas_call x1 -> x2, Pallas kernels: 3.33 us -> 3.37 us  [the longest x1 2.82 us: prep(): pl.pallas_call(prep_kernel, out_shape=[two, four], in_specs=[hbm_spec()]...]
  transfers between devices with their start and end apart: 19 -> 19, of which waited for: 8 -> 8; matrix products, arithmetic and copies ran while one was open for 0% -> 0% of each run, Pallas kernels for 16% -> 17%
where the time goes in v5:
time: 86.1 us; the launch traced here: 85.5 us
  waiting for transfers between devices  43 us (50%)
  starting transfers between devices  23.3 us (27%)
  Pallas kernels  18.6 us (22%)
    ppermute x4, waiting for transfers between devices, swap(): return lax.ppermute(x, 'seq', [(0, 1), (1, 0)])  19 us
    ppermute x2, waiting for transfers between devices, pair(): return lax.ppermute(x, 'row', [(i, i ^ 1) for i in range(4)])  15.2 us
    pallas_call x3, Pallas kernels, attend(): pl.pallas_call(functools.partial(attend_kernel, 1.0 / math.sqrt(head_size...  10.3 us
    ppermute x6, waiting for transfers between devices, along(): return lax.ppermute(x, axis, [(i, i ^ mask) for i in range(4)])  7.18 us
    ppermute x4, starting transfers between devices, swap(): return lax.ppermute(x, 'seq', [(0, 1), (1, 0)])  6.28 us
    ppermute x2, starting transfers between devices, pair(): return lax.ppermute(x, 'row', [(i, i ^ 1) for i in range(4)])  6.19 us
    pallas_call x4, Pallas kernels, call(): pl.pallas_call(kernel, out_shape=out_shape, in_specs=specs, out_specs=out...  4.95 us
    ppermute x3, starting transfers between devices, inward(): return lax.ppermute(x, 'row', [(1, 0), (2, 3)])  4.05 us
  transfers between devices with their start and end apart: 19, of which 8 were waited for; matrix products, arithmetic and copies ran while one was open for 0% of the time, Pallas kernels for 17%

profile of v5, /device:TPU:0, one launch (start us, length us, event | category | flops | bytes accessed | tf_op | source)
XLA Modules:
  0.0 85.5 jit_solution(505361728296571050)
XLA Ops:
  0.0 2.8 %shard_map.82 = (bf16[384,768]{1,0:T(8,128)(2,1)}, bf16[384,1536]{1,0:T(8,128)(2,1)}) custom-call(bf16[384,768]{1,0:T(8,128)(2,1)} %k_hbm.1, bf16[384,768]{1,0:T(8,128)(2,1)} %v_hbm.1, f32[6,128]{1,0:T(8,128)} %kg_hbm.1, bf16[768,768]{1,0:T(8,128)(2,1)} %w_hbm.1), custom_call_target="tpu_custom_call" | custom-call | flops 2359296 | bytes 1769472 | tf_op jit(solution)/shard_map/pallas_call | solution.py:177
  2.8 0.7 collective-permute-start.4
  3.6 5.8 %collective-permute-start.3 = (bf16[384,1536]{1,0:T(8,128)(2,1)}, bf16[384,1536]{1,0:T(8,128)(2,1)S(1)}, u32[]{:S(2)}, u32[]{:S(2)}) collective-permute-start(bf16[384,1536]{1,0:T(8,128)(2,1)} %get-tuple-element.28.refs_2_.kvw), channel_id=1, source_target_pairs={{0,4},{4,0},{8,12},{12,8},{1,5},{5,1},{9,13},{13,9},{2,6},{6,2},{1... | collective-permute-start | bytes 3538952 | tf_op jit(solution)/shard_map/ppermute | solution.py:353
  9.4 1.5 %collective-permute-start = (bf16[384,768]{1,0:T(8,128)(2,1)}, bf16[384,768]{1,0:T(8,128)(2,1)S(1)}, u32[]{:S(2)}, u32[]{:S(2)}) collective-permute-start(bf16[384,768]{1,0:T(8,128)(2,1)} %get-tuple-element.27), channel_id=1, source_target_pairs={{0,16},{16,0},{1,17},{17,1},{2,18},{18,2},{3,19},{19,3},{4,20},{20... | collective-permute-start | bytes 1769480 | tf_op jit(solution)/shard_map/ppermute | solution.py:350
  10.9 13.2 %collective-permute-done.refs_1_ = bf16[384,768]{1,0:T(8,128)(2,1)S(1)} collective-permute-done((bf16[384,768]{1,0:T(8,128)(2,1)}, bf16[384,768]{1,0:T(8,128)(2,1)S(1)}, u32[]{:S(2)}, u32[]{:S(2)}) %collective-permute-start) | collective-permute-done | bytes 589856 | tf_op jit(solution)/shard_map/ppermute | solution.py:350
  24.1 0.4 collective-permute-start.1
  24.5 0.7 collective-permute-start.2
  25.2 0.5 shard_map.83
  25.8 1.6 %collective-permute-start.5 = (bf16[384,384]{1,0:T(8,128)(2,1)S(1)}, bf16[384,384]{1,0:T(8,128)(2,1)S(1)}, u32[]{:S(2)}, u32[]{:S(2)}) collective-permute-start(bf16[384,384]{1,0:T(8,128)(2,1)S(1)} %get-tuple-element.29), channel_id=1, source_target_pairs={{0,16},{16,0},{1,17},{17,1},{2,18},{18,2},{3,19},{19,3},{4,20},{20... | collective-permute-start | bytes 884744 | tf_op jit(solution)/shard_map/ppermute | solution.py:350
  27.4 0.0 collective-permute-done.4.refs_4_.kvw_mid
  27.4 9.1 %collective-permute-done.3.refs_3_.kvw_pair = bf16[384,1536]{1,0:T(8,128)(2,1)S(1)} collective-permute-done((bf16[384,1536]{1,0:T(8,128)(2,1)}, bf16[384,1536]{1,0:T(8,128)(2,1)S(1)}, u32[]{:S(2)}, u32[]{:S(2)}) %collective-permute-start.3) | collective-permute-done | bytes 1179680 | tf_op jit(solution)/shard_map/ppermute | solution.py:353
  36.5 0.1 fusion
  36.5 0.0 collective-permute-done.5.refs_1_.refs_0_
  36.5 4.5 %shard_map.84 = (f32[3,2,384,128]{3,2,1,0:T(8,128)S(1)}, f32[3,2,384,256]{3,2,1,0:T(8,128)S(1)}) custom-call(bf16[384,384]{1,0:T(8,128)(2,1)S(1)} %get-tuple-element.26.refs_0_, bf16[384,384]{1,0:T(8,128)(2,1)S(1)} %collective-permute-done.5.refs_1_.refs_0_, bf16[384,1536]{1,0:T(8,128)(2,1)S(1)} %copy-done, ...), custom_call_target="tpu_custom_call" | custom-call | flops 2717908992 | bytes 8388608 | tf_op jit(solution)/shard_map/pallas_call | solution.py:264
  41.0 1.3 %collective-permute-start.7 = (bf16[384,768]{1,0:T(8,128)(2,1)S(1)}, bf16[384,768]{1,0:T(8,128)(2,1)S(1)}, u32[]{:S(2)}, u32[]{:S(2)}) collective-permute-start(bf16[384,768]{1,0:T(8,128)(2,1)S(1)} %slice.13), channel_id=1, source_target_pairs={{4,0},{8,12},{5,1},{9,13},{6,2},{10,14},{7,3},{11,15},{20,16},{24,... | collective-permute-start | bytes 1769480 | tf_op jit(solution)/shard_map/ppermute | solution.py:373
  42.3 0.7 collective-permute-start.11
  43.0 6.1 %collective-permute-done.1.refs_2_ = bf16[384,768]{1,0:T(8,128)(2,1)S(1)} collective-permute-done((bf16[384,768]{1,0:T(8,128)(2,1)S(1)}, bf16[384,768]{1,0:T(8,128)(2,1)S(1)}, u32[]{:S(2)}, u32[]{:S(2)}) %collective-permute-start.1) | collective-permute-done | bytes 589856 | tf_op jit(solution)/shard_map/ppermute | solution.py:353
  49.1 0.0 collective-permute-done.2.refs_3_
  49.1 2.9 %shard_map.85.a0 = bf16[384,384]{1,0:T(8,128)(2,1)S(1)} custom-call(bf16[384,384]{1,0:T(8,128)(2,1)S(1)} %collective-permute-done.5.refs_1_.refs_0_, bf16[384,768]{1,0:T(8,128)(2,1)S(1)} %collective-permute-done.refs_1_, bf16[384,768]{1,0:T(8,128)(2,1)S(1)} %collective-permute-done.1.refs_2_, bf16[384,768]{1,0:T(8,128)(2,1)S(1)} %collective-permute-done.2.refs_3_, ...), custom_call_target="tpu_custom_call" | custom-call | flops 1358954496 | bytes 8388608 | tf_op jit(solution)/shard_map/pallas_call | solution.py:264
  52.0 1.6 %collective-permute-start.15 = (bf16[384,384]{1,0:T(8,128)(2,1)S(1)}, bf16[384,384]{1,0:T(8,128)(2,1)S(1)}, u32[]{:S(2)}, u32[]{:S(2)}) collective-permute-start(bf16[384,384]{1,0:T(8,128)(2,1)S(1)} %shard_map.85.a0), channel_id=1, source_target_pairs={{0,2},{1,3},{2,0},{3,1},{4,6},{5,7},{6,4},{7,5},{8,10},{9,11},{10,... | collective-permute-start | bytes 884744 | tf_op jit(solution)/shard_map/ppermute | solution.py:359
  53.6 0.7 collective-permute-start.6
  54.3 0.1 collective-permute-start.14
  54.4 0.0 collective-permute-done.11.rest_0_.forward
  54.4 1.3 %collective-permute-start.12 = (bf16[384,384]{1,0:T(8,128)(2,1)S(1)}, bf16[384,384]{1,0:T(8,128)(2,1)S(1)}, u32[]{:S(2)}, u32[]{:S(2)}) collective-permute-start(bf16[384,384]{1,0:T(8,128)(2,1)S(1)} %collective-permute-done.11.rest_0_.forward), channel_id=1, source_target_pairs={{4,0},{8,12},{5,1},{9,13},{6,2},{10,14},{7,3},{11,15},{20,16},{24,... | collective-permute-start | bytes 884744 | tf_op jit(solution)/shard_map/ppermute | solution.py:373
  55.7 3.2 %collective-permute-done.15.a2 = bf16[384,384]{1,0:T(8,128)(2,1)S(1)} collective-permute-done((bf16[384,384]{1,0:T(8,128)(2,1)S(1)}, bf16[384,384]{1,0:T(8,128)(2,1)S(1)}, u32[]{:S(2)}, u32[]{:S(2)}) %collective-permute-start.15) | collective-permute-done | bytes 294944 | tf_op jit(solution)/shard_map/ppermute | solution.py:359
  58.8 0.0 collective-permute-done.6.rest_1_.forward
  58.8 1.5 %collective-permute-start.13 = (bf16[384,384]{1,0:T(8,128)(2,1)S(1)}, bf16[384,384]{1,0:T(8,128)(2,1)S(1)}, u32[]{:S(2)}, u32[]{:S(2)}) collective-permute-start(bf16[384,384]{1,0:T(8,128)(2,1)S(1)} %collective-permute-done.6.rest_1_.forward), channel_id=1, source_target_pairs={{4,0},{8,12},{5,1},{9,13},{6,2},{10,14},{7,3},{11,15},{20,16},{24,... | collective-permute-start | bytes 884744 | tf_op jit(solution)/shard_map/ppermute | solution.py:373
  60.3 0.7 collective-permute-done.7.rest_4_.inner
  61.0 2.9 %shard_map.86.a0 = bf16[384,384]{1,0:T(8,128)(2,1)S(1)} custom-call(bf16[384,384]{1,0:T(8,128)(2,1)S(1)} %get-tuple-element.26.refs_0_, bf16[384,768]{1,0:T(8,128)(2,1)S(1)} %collective-permute-done.refs_1_, bf16[384,768]{1,0:T(8,128)(2,1)S(1)} %collective-permute-done.1.refs_2_, bf16[384,768]{1,0:T(8,128)(2,1)S(1)} %collective-permute-done.2.refs_3_, ...), custom_call_target="tpu_custom_call" | custom-call | flops 1358954496 | bytes 8388608 | tf_op jit(solution)/shard_map/pallas_call | solution.py:264
  63.9 0.1 collective-permute-start.8
  64.0 0.0 collective-permute-done.14.a1
  64.0 2.3 %collective-permute-start.9 = (bf16[384,384]{1,0:T(8,128)(2,1)S(1)}, bf16[384,384]{1,0:T(8,128)(2,1)S(1)}, u32[]{:S(2)}, u32[]{:S(2)}) collective-permute-start(bf16[384,384]{1,0:T(8,128)(2,1)S(1)} %shard_map.86.a0), channel_id=1, source_target_pairs={{0,2},{1,3},{2,0},{3,1},{4,6},{5,7},{6,4},{7,5},{8,10},{9,11},{10,... | collective-permute-start | bytes 884744 | tf_op jit(solution)/shard_map/ppermute | solution.py:359
  66.3 1.0 %collective-permute-done.12.rest_2_.outer = bf16[384,384]{1,0:T(8,128)(2,1)S(1)} collective-permute-done((bf16[384,384]{1,0:T(8,128)(2,1)S(1)}, bf16[384,384]{1,0:T(8,128)(2,1)S(1)}, u32[]{:S(2)}, u32[]{:S(2)}) %collective-permute-start.12) | collective-permute-done | bytes 294944 | tf_op jit(solution)/shard_map/ppermute | solution.py:373
  67.3 0.0 collective-permute-done.16.a3
  67.3 1.0 %shard_map.88 = bf16[384,384]{1,0:T(8,128)(2,1)S(1)} custom-call(bf16[384,384]{1,0:T(8,128)(2,1)S(1)} %shard_map.85.a0, bf16[384,384]{1,0:T(8,128)(2,1)S(1)} %collective-permute-done.14.a1, bf16[384,384]{1,0:T(8,128)(2,1)S(1)} %collective-permute-done.15.a2, bf16[384,384]{1,0:T(8,128)(2,1)S(1)} %collective-permute-done.16.a3, bf16[384,1536]{1,0:T(8,128)(2,1)S(1)} %copy-done, ...), custom_call_target="tpu_custom_call" | custom-call | flops 4529848320 | bytes 2097152 | tf_op jit(solution)/shard_map/pallas_call | solution.py:362
  68.3 0.0 copy-start.4
  68.3 0.0 copy-start.1
  68.3 1.6 %collective-permute-start.17 = (bf16[384,384]{1,0:T(8,128)(2,1)S(1)}, bf16[384,384]{1,0:T(8,128)(2,1)S(1)}, u32[]{:S(2)}, u32[]{:S(2)}) collective-permute-start(bf16[384,384]{1,0:T(8,128)(2,1)S(1)} %shard_map.88), channel_id=1, source_target_pairs={{0,16},{16,0},{1,17},{17,1},{2,18},{18,2},{3,19},{19,3},{4,20},{20... | collective-permute-start | bytes 884744 | tf_op jit(solution)/shard_map/ppermute | solution.py:350
  69.9 4.0 %collective-permute-done.9.a2 = bf16[384,384]{1,0:T(8,128)(2,1)S(1)} collective-permute-done((bf16[384,384]{1,0:T(8,128)(2,1)S(1)}, bf16[384,384]{1,0:T(8,128)(2,1)S(1)}, u32[]{:S(2)}, u32[]{:S(2)}) %collective-permute-start.9) | collective-permute-done | bytes 294944 | tf_op jit(solution)/shard_map/ppermute | solution.py:359
  73.9 0.0 collective-permute-start.10
  73.9 0.0 collective-permute-done.13.rest_3_.outer
  73.9 1.0 %shard_map.89 = bf16[384,384]{1,0:T(8,128)(2,1)S(1)} custom-call(bf16[384,384]{1,0:T(8,128)(2,1)S(1)} %shard_map.85.a0, bf16[384,384]{1,0:T(8,128)(2,1)S(1)} %collective-permute-done.14.a1, bf16[384,384]{1,0:T(8,128)(2,1)S(1)} %collective-permute-done.15.a2, bf16[384,384]{1,0:T(8,128)(2,1)S(1)} %collective-permute-done.16.a3, bf16[384,1536]{1,0:T(8,128)(2,1)S(1)} %copy-done, ...), custom_call_target="tpu_custom_call" | custom-call | flops 4529848320 | bytes 2097152 | tf_op jit(solution)/shard_map/pallas_call | solution.py:362
  74.9 1.6 %collective-permute-start.18 = (bf16[384,384]{1,0:T(8,128)(2,1)S(1)}, bf16[384,384]{1,0:T(8,128)(2,1)S(1)}, u32[]{:S(2)}, u32[]{:S(2)}) collective-permute-start(bf16[384,384]{1,0:T(8,128)(2,1)S(1)} %shard_map.89), channel_id=1, source_target_pairs={{0,16},{16,0},{1,17},{17,1},{2,18},{18,2},{3,19},{19,3},{4,20},{20... | collective-permute-start | bytes 884744 | tf_op jit(solution)/shard_map/ppermute | solution.py:350
  76.5 0.0 collective-permute-done.8.a1
  76.5 2.1 %shard_map.87.base = f32[384,768]{1,0:T(8,128)S(1)} custom-call(bf16[384,384]{1,0:T(8,128)(2,1)S(1)} %shard_map.86.a0, bf16[384,384]{1,0:T(8,128)(2,1)S(1)} %collective-permute-done.8.a1, bf16[384,384]{1,0:T(8,128)(2,1)S(1)} %collective-permute-done.9.a2, bf16[384,384]{1,0:T(8,128)(2,1)S(1)} %collective-permute-done.10.a3, bf16[384,1536]{1,0:T(8,128)(2,1)S(1)} %copy-done, ...), custom_call_target="tpu_custom_call" | custom-call | flops 905969664 | bytes 2097152 | tf_op jit(solution)/shard_map/pallas_call | solution.py:362
  78.6 0.0 collective-permute-done.17.rest_0_
  78.6 5.8 %collective-permute-done.18.rest_1_ = bf16[384,384]{1,0:T(8,128)(2,1)S(1)} collective-permute-done((bf16[384,384]{1,0:T(8,128)(2,1)S(1)}, bf16[384,384]{1,0:T(8,128)(2,1)S(1)}, u32[]{:S(2)}, u32[]{:S(2)}) %collective-permute-start.18) | collective-permute-done | bytes 294944 | tf_op jit(solution)/shard_map/ppermute | solution.py:350
  84.4 0.9 %shard_map.90 = bf16[384,768]{1,0:T(8,128)(2,1)} custom-call(f32[384,768]{1,0:T(8,128)S(1)} %shard_map.87.base, f32[1,768]{1,0:T(1,128)S(1)} %reshape.3.gate, bf16[384,384]{1,0:T(8,128)(2,1)S(1)} %collective-permute-done.17.rest_0_, bf16[384,384]{1,0:T(8,128)(2,1)S(1)} %collective-permute-done.18.rest_1_), custom_call_target="tpu_custom_call" | custom-call | flops 1179648 | bytes 2097152 | tf_op jit(solution)/shard_map/pallas_call | solution.py:362
  (12 shorter events, 0.1 us)
Async XLA Ops:
  0.0 25.2 %copy-start.2 = (bf16[384,768]{1,0:T(8,128)(2,1)S(1)}, bf16[384,768]{1,0:T(8,128)(2,1)}, u32[]{:S(2)}) copy-start(bf16[384,768]{1,0:T(8,128)(2,1)} %q_hbm) | copy-start | bytes 1769476
  0.0 25.2 %copy-start.3 = (f32[6,128]{1,0:T(8,128)S(1)}, f32[6,128]{1,0:T(8,128)}, u32[]{:S(2)}) copy-start(f32[6,128]{1,0:T(8,128)} %qg_hbm.1) | copy-start | bytes 9220
  2.8 24.5 %collective-permute-start.4 = (bf16[384,1536]{1,0:T(8,128)(2,1)}, bf16[384,1536]{1,0:T(8,128)(2,1)S(1)}, u32[]{:S(2)}, u32[]{:S(2)}) collective-permute-start(bf16[384,1536]{1,0:T(8,128)(2,1)} %get-tuple-element.28.refs_2_.kvw), channel_id=1, source_target_pairs={{4,8},{8,4},{5,9},{9,5},{6,10},{10,6},{7,11},{11,7},{20,24},{24,20... | collective-permute-start | bytes 3538952 | tf_op jit(solution)/shard_map/ppermute | solution.py:356
  3.6 32.9 %collective-permute-start.3 = (bf16[384,1536]{1,0:T(8,128)(2,1)}, bf16[384,1536]{1,0:T(8,128)(2,1)S(1)}, u32[]{:S(2)}, u32[]{:S(2)}) collective-permute-start(bf16[384,1536]{1,0:T(8,128)(2,1)} %get-tuple-element.28.refs_2_.kvw), channel_id=1, source_target_pairs={{0,4},{4,0},{8,12},{12,8},{1,5},{5,1},{9,13},{13,9},{2,6},{6,2},{1... | collective-permute-start | bytes 3538952 | tf_op jit(solution)/shard_map/ppermute | solution.py:353
  9.4 14.7 %collective-permute-start = (bf16[384,768]{1,0:T(8,128)(2,1)}, bf16[384,768]{1,0:T(8,128)(2,1)S(1)}, u32[]{:S(2)}, u32[]{:S(2)}) collective-permute-start(bf16[384,768]{1,0:T(8,128)(2,1)} %get-tuple-element.27), channel_id=1, source_target_pairs={{0,16},{16,0},{1,17},{17,1},{2,18},{18,2},{3,19},{19,3},{4,20},{20... | collective-permute-start | bytes 1769480 | tf_op jit(solution)/shard_map/ppermute | solution.py:350
  24.1 25.0 %collective-permute-start.1 = (bf16[384,768]{1,0:T(8,128)(2,1)S(1)}, bf16[384,768]{1,0:T(8,128)(2,1)S(1)}, u32[]{:S(2)}, u32[]{:S(2)}) collective-permute-start(bf16[384,768]{1,0:T(8,128)(2,1)S(1)} %collective-permute-done.refs_1_), channel_id=1, source_target_pairs={{0,4},{4,0},{8,12},{12,8},{1,5},{5,1},{9,13},{13,9},{2,6},{6,2},{1... | collective-permute-start | bytes 1769480 | tf_op jit(solution)/shard_map/ppermute | solution.py:353
  24.5 24.6 %collective-permute-start.2 = (bf16[384,768]{1,0:T(8,128)(2,1)S(1)}, bf16[384,768]{1,0:T(8,128)(2,1)S(1)}, u32[]{:S(2)}, u32[]{:S(2)}) collective-permute-start(bf16[384,768]{1,0:T(8,128)(2,1)S(1)} %collective-permute-done.refs_1_), channel_id=1, source_target_pairs={{4,8},{8,4},{5,9},{9,5},{6,10},{10,6},{7,11},{11,7},{20,24},{24,20... | collective-permute-start | bytes 1769480 | tf_op jit(solution)/shard_map/ppermute | solution.py:356
  25.8 10.8 %copy-start = (bf16[384,1536]{1,0:T(8,128)(2,1)S(1)}, bf16[384,1536]{1,0:T(8,128)(2,1)}, u32[]{:S(2)}) copy-start(bf16[384,1536]{1,0:T(8,128)(2,1)} %get-tuple-element.28.refs_2_.kvw) | copy-start | bytes 3538948
  25.8 10.8 %collective-permute-start.5 = (bf16[384,384]{1,0:T(8,128)(2,1)S(1)}, bf16[384,384]{1,0:T(8,128)(2,1)S(1)}, u32[]{:S(2)}, u32[]{:S(2)}) collective-permute-start(bf16[384,384]{1,0:T(8,128)(2,1)S(1)} %get-tuple-element.29), channel_id=1, source_target_pairs={{0,16},{16,0},{1,17},{17,1},{2,18},{18,2},{3,19},{19,3},{4,20},{20... | collective-permute-start | bytes 884744 | tf_op jit(solution)/shard_map/ppermute | solution.py:350
  41.0 20.0 %collective-permute-start.7 = (bf16[384,768]{1,0:T(8,128)(2,1)S(1)}, bf16[384,768]{1,0:T(8,128)(2,1)S(1)}, u32[]{:S(2)}, u32[]{:S(2)}) collective-permute-start(bf16[384,768]{1,0:T(8,128)(2,1)S(1)} %slice.13), channel_id=1, source_target_pairs={{4,0},{8,12},{5,1},{9,13},{6,2},{10,14},{7,3},{11,15},{20,16},{24,... | collective-permute-start | bytes 1769480 | tf_op jit(solution)/shard_map/ppermute | solution.py:373
  42.3 12.0 %collective-permute-start.11 = (bf16[384,384]{1,0:T(8,128)(2,1)S(1)}, bf16[384,384]{1,0:T(8,128)(2,1)S(1)}, u32[]{:S(2)}, u32[]{:S(2)}) collective-permute-start(bf16[384,384]{1,0:T(8,128)(2,1)S(1)} %get-tuple-element.38), channel_id=1, source_target_pairs={{4,8},{8,4},{5,9},{9,5},{6,10},{10,6},{7,11},{11,7},{20,24},{24,20... | collective-permute-start | bytes 884744 | tf_op jit(solution)/shard_map/ppermute | solution.py:356
  52.0 6.8 %collective-permute-start.15 = (bf16[384,384]{1,0:T(8,128)(2,1)S(1)}, bf16[384,384]{1,0:T(8,128)(2,1)S(1)}, u32[]{:S(2)}, u32[]{:S(2)}) collective-permute-start(bf16[384,384]{1,0:T(8,128)(2,1)S(1)} %shard_map.85.a0), channel_id=1, source_target_pairs={{0,2},{1,3},{2,0},{3,1},{4,6},{5,7},{6,4},{7,5},{8,10},{9,11},{10,... | collective-permute-start | bytes 884744 | tf_op jit(solution)/shard_map/ppermute | solution.py:359
  53.6 5.2 %collective-permute-start.6 = (bf16[384,384]{1,0:T(8,128)(2,1)S(1)}, bf16[384,384]{1,0:T(8,128)(2,1)S(1)}, u32[]{:S(2)}, u32[]{:S(2)}) collective-permute-start(bf16[384,384]{1,0:T(8,128)(2,1)S(1)} %get-tuple-element.34), channel_id=1, source_target_pairs={{4,8},{8,4},{5,9},{9,5},{6,10},{10,6},{7,11},{11,7},{20,24},{24,20... | collective-permute-start | bytes 884744 | tf_op jit(solution)/shard_map/ppermute | solution.py:356
  54.3 9.7 %collective-permute-start.14 = (bf16[384,384]{1,0:T(8,128)(2,1)S(1)}, bf16[384,384]{1,0:T(8,128)(2,1)S(1)}, u32[]{:S(2)}, u32[]{:S(2)}) collective-permute-start(bf16[384,384]{1,0:T(8,128)(2,1)S(1)} %shard_map.85.a0), channel_id=1, source_target_pairs={{0,1},{1,0},{2,3},{3,2},{4,5},{5,4},{6,7},{7,6},{8,9},{9,8},{10,11... | collective-permute-start | bytes 884744 | tf_op jit(solution)/shard_map/ppermute | solution.py:359
  54.4 12.9 %collective-permute-start.12 = (bf16[384,384]{1,0:T(8,128)(2,1)S(1)}, bf16[384,384]{1,0:T(8,128)(2,1)S(1)}, u32[]{:S(2)}, u32[]{:S(2)}) collective-permute-start(bf16[384,384]{1,0:T(8,128)(2,1)S(1)} %collective-permute-done.11.rest_0_.forward), channel_id=1, source_target_pairs={{4,0},{8,12},{5,1},{9,13},{6,2},{10,14},{7,3},{11,15},{20,16},{24,... | collective-permute-start | bytes 884744 | tf_op jit(solution)/shard_map/ppermute | solution.py:373
  58.8 8.5 %collective-permute-start.16 = (bf16[384,384]{1,0:T(8,128)(2,1)S(1)}, bf16[384,384]{1,0:T(8,128)(2,1)S(1)}, u32[]{:S(2)}, u32[]{:S(2)}) collective-permute-start(bf16[384,384]{1,0:T(8,128)(2,1)S(1)} %collective-permute-done.15.a2), channel_id=1, source_target_pairs={{0,1},{1,0},{2,3},{3,2},{4,5},{5,4},{6,7},{7,6},{8,9},{9,8},{10,11... | collective-permute-start | bytes 884744 | tf_op jit(solution)/shard_map/ppermute | solution.py:359
  58.8 15.1 %collective-permute-start.13 = (bf16[384,384]{1,0:T(8,128)(2,1)S(1)}, bf16[384,384]{1,0:T(8,128)(2,1)S(1)}, u32[]{:S(2)}, u32[]{:S(2)}) collective-permute-start(bf16[384,384]{1,0:T(8,128)(2,1)S(1)} %collective-permute-done.6.rest_1_.forward), channel_id=1, source_target_pairs={{4,0},{8,12},{5,1},{9,13},{6,2},{10,14},{7,3},{11,15},{20,16},{24,... | collective-permute-start | bytes 884744 | tf_op jit(solution)/shard_map/ppermute | solution.py:373
  63.9 12.6 %collective-permute-start.8 = (bf16[384,384]{1,0:T(8,128)(2,1)S(1)}, bf16[384,384]{1,0:T(8,128)(2,1)S(1)}, u32[]{:S(2)}, u32[]{:S(2)}) collective-permute-start(bf16[384,384]{1,0:T(8,128)(2,1)S(1)} %shard_map.86.a0), channel_id=1, source_target_pairs={{0,1},{1,0},{2,3},{3,2},{4,5},{5,4},{6,7},{7,6},{8,9},{9,8},{10,11... | collective-permute-start | bytes 884744 | tf_op jit(solution)/shard_map/ppermute | solution.py:359
  64.0 9.9 %collective-permute-start.9 = (bf16[384,384]{1,0:T(8,128)(2,1)S(1)}, bf16[384,384]{1,0:T(8,128)(2,1)S(1)}, u32[]{:S(2)}, u32[]{:S(2)}) collective-permute-start(bf16[384,384]{1,0:T(8,128)(2,1)S(1)} %shard_map.86.a0), channel_id=1, source_target_pairs={{0,2},{1,3},{2,0},{3,1},{4,6},{5,7},{6,4},{7,5},{8,10},{9,11},{10,... | collective-permute-start | bytes 884744 | tf_op jit(solution)/shard_map/ppermute | solution.py:359
  68.3 8.2 %copy-start.4 = (f32[768]{0:T(1024)S(1)}, f32[768]{0:T(1024)}, u32[]{:S(2)}) copy-start(f32[768]{0:T(1024)} %param.15) | copy-start | bytes 9220
  68.3 8.2 %copy-start.1 = (bf16[384,768]{1,0:T(8,128)(2,1)S(1)}, bf16[384,768]{1,0:T(8,128)(2,1)}, u32[]{:S(2)}) copy-start(bf16[384,768]{1,0:T(8,128)(2,1)} %stream_hbm.1) | copy-start | bytes 1769476
  68.3 10.3 %collective-permute-start.17 = (bf16[384,384]{1,0:T(8,128)(2,1)S(1)}, bf16[384,384]{1,0:T(8,128)(2,1)S(1)}, u32[]{:S(2)}, u32[]{:S(2)}) collective-permute-start(bf16[384,384]{1,0:T(8,128)(2,1)S(1)} %shard_map.88), channel_id=1, source_target_pairs={{0,16},{16,0},{1,17},{17,1},{2,18},{18,2},{3,19},{19,3},{4,20},{20... | collective-permute-start | bytes 884744 | tf_op jit(solution)/shard_map/ppermute | solution.py:350
  73.9 2.6 %collective-permute-start.10 = (bf16[384,384]{1,0:T(8,128)(2,1)S(1)}, bf16[384,384]{1,0:T(8,128)(2,1)S(1)}, u32[]{:S(2)}, u32[]{:S(2)}) collective-permute-start(bf16[384,384]{1,0:T(8,128)(2,1)S(1)} %collective-permute-done.9.a2), channel_id=1, source_target_pairs={{0,1},{1,0},{2,3},{3,2},{4,5},{5,4},{6,7},{7,6},{8,9},{9,8},{10,11... | collective-permute-start | bytes 884744 | tf_op jit(solution)/shard_map/ppermute | solution.py:359
  74.9 9.5 %collective-permute-start.18 = (bf16[384,384]{1,0:T(8,128)(2,1)S(1)}, bf16[384,384]{1,0:T(8,128)(2,1)S(1)}, u32[]{:S(2)}, u32[]{:S(2)}) collective-permute-start(bf16[384,384]{1,0:T(8,128)(2,1)S(1)} %shard_map.89), channel_id=1, source_target_pairs={{0,16},{16,0},{1,17},{17,1},{2,18},{18,2},{3,19},{19,3},{4,20},{20... | collective-permute-start | bytes 884744 | tf_op jit(solution)/shard_map/ppermute | solution.py:350

commit v6 on v5

--- a/solution.py
+++ b/solution.py
@@ -411,8 +411,9 @@
     received = [swap(sent) for sent in sents]
     carry, forwards[1], inner[0] = barrier((carry, forwards[1], inner[0]))
     mine = attend((0,), [q_keep], layers, head_size, carry)
-    across_mine, beside_mine = along(mine, "col", 2), along(mine, "col", 1)
-    groups = [mine, beside_mine, across_mine, along(across_mine, "col", 1)]
+    beside_mine = along(mine, "col", 1)
+    across_mine = along(mine, "col", 2)
+    groups = [mine, beside_mine, across_mine, along(beside_mine, "col", 2)]
     base = call(
         functools.partial(own_kernel, spans),
         [*groups, kvw, kvw_pair, kvw_mid, gate, stream, *forwards, *outer, *inner],

time: 86.1 us -> 84.3 us (0.979)
  waiting for transfers between devices: 43 us -> 39.3 us
  starting transfers between devices: 23.3 us -> 25.5 us
    ppermute x4, waiting for transfers between devices: 19 us -> 13.8 us  [swap(): return lax.ppermute(x, 'seq', [(0, 1), (1, 0)])]
    ppermute x6, starting transfers between devices: 4.01 us -> 6.25 us  [along(): return lax.ppermute(x, axis, [(i, i ^ mask) for i in range(4)])]
    ppermute x3, waiting for transfers between devices: 1.67 us -> 2.74 us  [inward(): return lax.ppermute(x, 'row', [(1, 0), (2, 3)])]
  transfers between devices with their start and end apart: 19 -> 19, of which waited for: 8 -> 9; matrix products, arithmetic and copies ran while one was open for 0% -> 0% of each run, Pallas kernels for 17% -> 18%
where the time goes in v6:
time: 84.3 us; the launch traced here: 84 us
  waiting for transfers between devices  39.3 us (47%)
  starting transfers between devices  25.5 us (30%)
  Pallas kernels  18.6 us (22%)
    ppermute x2, waiting for transfers between devices, pair(): return lax.ppermute(x, 'row', [(i, i ^ 1) for i in range(4)])  15.2 us
    ppermute x4, waiting for transfers between devices, swap(): return lax.ppermute(x, 'seq', [(0, 1), (1, 0)])  13.8 us
    pallas_call x3, Pallas kernels, attend(): pl.pallas_call(functools.partial(attend_kernel, 1.0 / math.sqrt(head_size...  10.3 us
    ppermute x6, waiting for transfers between devices, along(): return lax.ppermute(x, axis, [(i, i ^ mask) for i in range(4)])  7.59 us
    ppermute x4, starting transfers between devices, swap(): return lax.ppermute(x, 'seq', [(0, 1), (1, 0)])  6.28 us
    ppermute x6, starting transfers between devices, along(): return lax.ppermute(x, axis, [(i, i ^ mask) for i in range(4)])  6.25 us
    ppermute x2, starting transfers between devices, pair(): return lax.ppermute(x, 'row', [(i, i ^ 1) for i in range(4)])  6.19 us
    pallas_call x4, Pallas kernels, call(): pl.pallas_call(kernel, out_shape=out_shape, in_specs=specs, out_specs=out...  4.94 us
  transfers between devices with their start and end apart: 19, of which 9 were waited for; matrix products, arithmetic and copies ran while one was open for 0% of the time, Pallas kernels for 18%

profile of v6, /device:TPU:0, one launch (start us, length us, event | category | flops | bytes accessed | tf_op | source)
XLA Modules:
  0.0 84.0 jit_solution(4009298008323761877)
XLA Ops:
  0.0 2.8 %shard_map.82 = (bf16[384,768]{1,0:T(8,128)(2,1)}, bf16[384,1536]{1,0:T(8,128)(2,1)}) custom-call(bf16[384,768]{1,0:T(8,128)(2,1)} %k_hbm.1, bf16[384,768]{1,0:T(8,128)(2,1)} %v_hbm.1, f32[6,128]{1,0:T(8,128)} %kg_hbm.1, bf16[768,768]{1,0:T(8,128)(2,1)} %w_hbm.1), custom_call_target="tpu_custom_call" | custom-call | flops 2359296 | bytes 1769472 | tf_op jit(solution)/shard_map/pallas_call | solution.py:177
  2.8 0.7 collective-permute-start.4
  3.6 5.8 %collective-permute-start.3 = (bf16[384,1536]{1,0:T(8,128)(2,1)}, bf16[384,1536]{1,0:T(8,128)(2,1)S(1)}, u32[]{:S(2)}, u32[]{:S(2)}) collective-permute-start(bf16[384,1536]{1,0:T(8,128)(2,1)} %get-tuple-element.28.refs_2_.kvw), channel_id=1, source_target_pairs={{0,4},{4,0},{8,12},{12,8},{1,5},{5,1},{9,13},{13,9},{2,6},{6,2},{1... | collective-permute-start | bytes 3538952 | tf_op jit(solution)/shard_map/ppermute | solution.py:353
  9.4 1.5 %collective-permute-start = (bf16[384,768]{1,0:T(8,128)(2,1)}, bf16[384,768]{1,0:T(8,128)(2,1)S(1)}, u32[]{:S(2)}, u32[]{:S(2)}) collective-permute-start(bf16[384,768]{1,0:T(8,128)(2,1)} %get-tuple-element.27), channel_id=1, source_target_pairs={{0,16},{16,0},{1,17},{17,1},{2,18},{18,2},{3,19},{19,3},{4,20},{20... | collective-permute-start | bytes 1769480 | tf_op jit(solution)/shard_map/ppermute | solution.py:350
  10.9 13.2 %collective-permute-done.refs_1_ = bf16[384,768]{1,0:T(8,128)(2,1)S(1)} collective-permute-done((bf16[384,768]{1,0:T(8,128)(2,1)}, bf16[384,768]{1,0:T(8,128)(2,1)S(1)}, u32[]{:S(2)}, u32[]{:S(2)}) %collective-permute-start) | collective-permute-done | bytes 589856 | tf_op jit(solution)/shard_map/ppermute | solution.py:350
  24.1 0.4 collective-permute-start.1
  24.5 0.7 collective-permute-start.2
  25.2 0.5 shard_map.83
  25.8 1.6 %collective-permute-start.5 = (bf16[384,384]{1,0:T(8,128)(2,1)S(1)}, bf16[384,384]{1,0:T(8,128)(2,1)S(1)}, u32[]{:S(2)}, u32[]{:S(2)}) collective-permute-start(bf16[384,384]{1,0:T(8,128)(2,1)S(1)} %get-tuple-element.29), channel_id=1, source_target_pairs={{0,16},{16,0},{1,17},{17,1},{2,18},{18,2},{3,19},{19,3},{4,20},{20... | collective-permute-start | bytes 884744 | tf_op jit(solution)/shard_map/ppermute | solution.py:350
  27.4 0.0 collective-permute-done.4.refs_4_.kvw_mid
  27.4 9.1 %collective-permute-done.3.refs_3_.kvw_pair = bf16[384,1536]{1,0:T(8,128)(2,1)S(1)} collective-permute-done((bf16[384,1536]{1,0:T(8,128)(2,1)}, bf16[384,1536]{1,0:T(8,128)(2,1)S(1)}, u32[]{:S(2)}, u32[]{:S(2)}) %collective-permute-start.3) | collective-permute-done | bytes 1179680 | tf_op jit(solution)/shard_map/ppermute | solution.py:353
  36.5 0.1 fusion
  36.5 0.0 collective-permute-done.5.refs_1_.refs_0_
  36.5 4.5 %shard_map.84 = (f32[3,2,384,128]{3,2,1,0:T(8,128)S(1)}, f32[3,2,384,256]{3,2,1,0:T(8,128)S(1)}) custom-call(bf16[384,384]{1,0:T(8,128)(2,1)S(1)} %get-tuple-element.26.refs_0_, bf16[384,384]{1,0:T(8,128)(2,1)S(1)} %collective-permute-done.5.refs_1_.refs_0_, bf16[384,1536]{1,0:T(8,128)(2,1)S(1)} %copy-done, ...), custom_call_target="tpu_custom_call" | custom-call | flops 2717908992 | bytes 8388608 | tf_op jit(solution)/shard_map/pallas_call | solution.py:264
  41.0 1.3 %collective-permute-start.7 = (bf16[384,768]{1,0:T(8,128)(2,1)S(1)}, bf16[384,768]{1,0:T(8,128)(2,1)S(1)}, u32[]{:S(2)}, u32[]{:S(2)}) collective-permute-start(bf16[384,768]{1,0:T(8,128)(2,1)S(1)} %slice.13), channel_id=1, source_target_pairs={{4,0},{8,12},{5,1},{9,13},{6,2},{10,14},{7,3},{11,15},{20,16},{24,... | collective-permute-start | bytes 1769480 | tf_op jit(solution)/shard_map/ppermute | solution.py:373
  42.3 0.7 collective-permute-start.11
  43.0 6.1 %collective-permute-done.1.refs_2_ = bf16[384,768]{1,0:T(8,128)(2,1)S(1)} collective-permute-done((bf16[384,768]{1,0:T(8,128)(2,1)S(1)}, bf16[384,768]{1,0:T(8,128)(2,1)S(1)}, u32[]{:S(2)}, u32[]{:S(2)}) %collective-permute-start.1) | collective-permute-done | bytes 589856 | tf_op jit(solution)/shard_map/ppermute | solution.py:353
  49.1 0.0 collective-permute-done.2.refs_3_
  49.1 2.9 %shard_map.85.a0 = bf16[384,384]{1,0:T(8,128)(2,1)S(1)} custom-call(bf16[384,384]{1,0:T(8,128)(2,1)S(1)} %collective-permute-done.5.refs_1_.refs_0_, bf16[384,768]{1,0:T(8,128)(2,1)S(1)} %collective-permute-done.refs_1_, bf16[384,768]{1,0:T(8,128)(2,1)S(1)} %collective-permute-done.1.refs_2_, bf16[384,768]{1,0:T(8,128)(2,1)S(1)} %collective-permute-done.2.refs_3_, ...), custom_call_target="tpu_custom_call" | custom-call | flops 1358954496 | bytes 8388608 | tf_op jit(solution)/shard_map/pallas_call | solution.py:264
  52.0 1.6 %collective-permute-start.15 = (bf16[384,384]{1,0:T(8,128)(2,1)S(1)}, bf16[384,384]{1,0:T(8,128)(2,1)S(1)}, u32[]{:S(2)}, u32[]{:S(2)}) collective-permute-start(bf16[384,384]{1,0:T(8,128)(2,1)S(1)} %shard_map.85.a0), channel_id=1, source_target_pairs={{0,2},{1,3},{2,0},{3,1},{4,6},{5,7},{6,4},{7,5},{8,10},{9,11},{10,... | collective-permute-start | bytes 884744 | tf_op jit(solution)/shard_map/ppermute | solution.py:359
  53.6 0.7 collective-permute-start.6
  54.3 0.1 collective-permute-start.14
  54.4 0.0 collective-permute-done.11.rest_0_.forward
  54.4 1.3 %collective-permute-start.12 = (bf16[384,384]{1,0:T(8,128)(2,1)S(1)}, bf16[384,384]{1,0:T(8,128)(2,1)S(1)}, u32[]{:S(2)}, u32[]{:S(2)}) collective-permute-start(bf16[384,384]{1,0:T(8,128)(2,1)S(1)} %collective-permute-done.11.rest_0_.forward), channel_id=1, source_target_pairs={{4,0},{8,12},{5,1},{9,13},{6,2},{10,14},{7,3},{11,15},{20,16},{24,... | collective-permute-start | bytes 884744 | tf_op jit(solution)/shard_map/ppermute | solution.py:373
  55.7 3.2 %collective-permute-done.15.a2 = bf16[384,384]{1,0:T(8,128)(2,1)S(1)} collective-permute-done((bf16[384,384]{1,0:T(8,128)(2,1)S(1)}, bf16[384,384]{1,0:T(8,128)(2,1)S(1)}, u32[]{:S(2)}, u32[]{:S(2)}) %collective-permute-start.15) | collective-permute-done | bytes 294944 | tf_op jit(solution)/shard_map/ppermute | solution.py:359
  58.8 0.0 collective-permute-start.16
  58.8 0.0 collective-permute-done.6.rest_1_.forward
  58.8 1.5 %collective-permute-start.13 = (bf16[384,384]{1,0:T(8,128)(2,1)S(1)}, bf16[384,384]{1,0:T(8,128)(2,1)S(1)}, u32[]{:S(2)}, u32[]{:S(2)}) collective-permute-start(bf16[384,384]{1,0:T(8,128)(2,1)S(1)} %collective-permute-done.6.rest_1_.forward), channel_id=1, source_target_pairs={{4,0},{8,12},{5,1},{9,13},{6,2},{10,14},{7,3},{11,15},{20,16},{24,... | collective-permute-start | bytes 884744 | tf_op jit(solution)/shard_map/ppermute | solution.py:373
  60.3 0.7 collective-permute-done.7.rest_4_.inner
  61.0 2.9 %shard_map.86.a0 = bf16[384,384]{1,0:T(8,128)(2,1)S(1)} custom-call(bf16[384,384]{1,0:T(8,128)(2,1)S(1)} %get-tuple-element.26.refs_0_, bf16[384,768]{1,0:T(8,128)(2,1)S(1)} %collective-permute-done.refs_1_, bf16[384,768]{1,0:T(8,128)(2,1)S(1)} %collective-permute-done.1.refs_2_, bf16[384,768]{1,0:T(8,128)(2,1)S(1)} %collective-permute-done.2.refs_3_, ...), custom_call_target="tpu_custom_call" | custom-call | flops 1358954496 | bytes 8388608 | tf_op jit(solution)/shard_map/pallas_call | solution.py:264
  63.9 0.1 collective-permute-start.8
  64.0 0.0 collective-permute-done.14.a1
  64.0 2.3 %collective-permute-start.9 = (bf16[384,384]{1,0:T(8,128)(2,1)S(1)}, bf16[384,384]{1,0:T(8,128)(2,1)S(1)}, u32[]{:S(2)}, u32[]{:S(2)}) collective-permute-start(bf16[384,384]{1,0:T(8,128)(2,1)S(1)} %shard_map.86.a0), channel_id=1, source_target_pairs={{0,2},{1,3},{2,0},{3,1},{4,6},{5,7},{6,4},{7,5},{8,10},{9,11},{10,... | collective-permute-start | bytes 884744 | tf_op jit(solution)/shard_map/ppermute | solution.py:359
  66.3 1.0 %collective-permute-done.12.rest_2_.outer = bf16[384,384]{1,0:T(8,128)(2,1)S(1)} collective-permute-done((bf16[384,384]{1,0:T(8,128)(2,1)S(1)}, bf16[384,384]{1,0:T(8,128)(2,1)S(1)}, u32[]{:S(2)}, u32[]{:S(2)}) %collective-permute-start.12) | collective-permute-done | bytes 294944 | tf_op jit(solution)/shard_map/ppermute | solution.py:373
  67.3 0.0 collective-permute-done.16.a3
  67.3 1.0 %shard_map.88 = bf16[384,384]{1,0:T(8,128)(2,1)S(1)} custom-call(bf16[384,384]{1,0:T(8,128)(2,1)S(1)} %shard_map.85.a0, bf16[384,384]{1,0:T(8,128)(2,1)S(1)} %collective-permute-done.14.a1, bf16[384,384]{1,0:T(8,128)(2,1)S(1)} %collective-permute-done.15.a2, bf16[384,384]{1,0:T(8,128)(2,1)S(1)} %collective-permute-done.16.a3, bf16[384,1536]{1,0:T(8,128)(2,1)S(1)} %copy-done, ...), custom_call_target="tpu_custom_call" | custom-call | flops 4529848320 | bytes 2097152 | tf_op jit(solution)/shard_map/pallas_call | solution.py:362
  68.3 0.0 copy-start.4
  68.3 0.0 copy-start.1
  68.3 1.6 %collective-permute-start.17 = (bf16[384,384]{1,0:T(8,128)(2,1)S(1)}, bf16[384,384]{1,0:T(8,128)(2,1)S(1)}, u32[]{:S(2)}, u32[]{:S(2)}) collective-permute-start(bf16[384,384]{1,0:T(8,128)(2,1)S(1)} %shard_map.88), channel_id=1, source_target_pairs={{0,16},{16,0},{1,17},{17,1},{2,18},{18,2},{3,19},{19,3},{4,20},{20... | collective-permute-start | bytes 884744 | tf_op jit(solution)/shard_map/ppermute | solution.py:350
  69.9 0.0 collective-permute-done.8.a1
  69.9 2.2 %collective-permute-start.10 = (bf16[384,384]{1,0:T(8,128)(2,1)S(1)}, bf16[384,384]{1,0:T(8,128)(2,1)S(1)}, u32[]{:S(2)}, u32[]{:S(2)}) collective-permute-start(bf16[384,384]{1,0:T(8,128)(2,1)S(1)} %collective-permute-done.8.a1), channel_id=1, source_target_pairs={{0,2},{1,3},{2,0},{3,1},{4,6},{5,7},{6,4},{7,5},{8,10},{9,11},{10,... | collective-permute-start | bytes 884744 | tf_op jit(solution)/shard_map/ppermute | solution.py:359
  72.2 1.1 %collective-permute-done.13.rest_3_.outer = bf16[384,384]{1,0:T(8,128)(2,1)S(1)} collective-permute-done((bf16[384,384]{1,0:T(8,128)(2,1)S(1)}, bf16[384,384]{1,0:T(8,128)(2,1)S(1)}, u32[]{:S(2)}, u32[]{:S(2)}) %collective-permute-start.13) | collective-permute-done | bytes 294944 | tf_op jit(solution)/shard_map/ppermute | solution.py:373
  73.2 1.0 %shard_map.89 = bf16[384,384]{1,0:T(8,128)(2,1)S(1)} custom-call(bf16[384,384]{1,0:T(8,128)(2,1)S(1)} %shard_map.85.a0, bf16[384,384]{1,0:T(8,128)(2,1)S(1)} %collective-permute-done.14.a1, bf16[384,384]{1,0:T(8,128)(2,1)S(1)} %collective-permute-done.15.a2, bf16[384,384]{1,0:T(8,128)(2,1)S(1)} %collective-permute-done.16.a3, bf16[384,1536]{1,0:T(8,128)(2,1)S(1)} %copy-done, ...), custom_call_target="tpu_custom_call" | custom-call | flops 4529848320 | bytes 2097152 | tf_op jit(solution)/shard_map/pallas_call | solution.py:362
  74.2 1.6 %collective-permute-start.18 = (bf16[384,384]{1,0:T(8,128)(2,1)S(1)}, bf16[384,384]{1,0:T(8,128)(2,1)S(1)}, u32[]{:S(2)}, u32[]{:S(2)}) collective-permute-start(bf16[384,384]{1,0:T(8,128)(2,1)S(1)} %shard_map.89), channel_id=1, source_target_pairs={{0,16},{16,0},{1,17},{17,1},{2,18},{18,2},{3,19},{19,3},{4,20},{20... | collective-permute-start | bytes 884744 | tf_op jit(solution)/shard_map/ppermute | solution.py:350
  75.8 4.4 %collective-permute-done.10.a3 = bf16[384,384]{1,0:T(8,128)(2,1)S(1)} collective-permute-done((bf16[384,384]{1,0:T(8,128)(2,1)S(1)}, bf16[384,384]{1,0:T(8,128)(2,1)S(1)}, u32[]{:S(2)}, u32[]{:S(2)}) %collective-permute-start.10) | collective-permute-done | bytes 294944 | tf_op jit(solution)/shard_map/ppermute | solution.py:359
  80.2 2.1 %shard_map.87.base = f32[384,768]{1,0:T(8,128)S(1)} custom-call(bf16[384,384]{1,0:T(8,128)(2,1)S(1)} %shard_map.86.a0, bf16[384,384]{1,0:T(8,128)(2,1)S(1)} %collective-permute-done.8.a1, bf16[384,384]{1,0:T(8,128)(2,1)S(1)} %collective-permute-done.9.a2, bf16[384,384]{1,0:T(8,128)(2,1)S(1)} %collective-permute-done.10.a3, bf16[384,1536]{1,0:T(8,128)(2,1)S(1)} %copy-done, ...), custom_call_target="tpu_custom_call" | custom-call | flops 905969664 | bytes 2097152 | tf_op jit(solution)/shard_map/pallas_call | solution.py:362
  82.3 0.6 collective-permute-done.18.rest_1_
  82.9 0.9 %shard_map.90 = bf16[384,768]{1,0:T(8,128)(2,1)} custom-call(f32[384,768]{1,0:T(8,128)S(1)} %shard_map.87.base, f32[1,768]{1,0:T(1,128)S(1)} %reshape.3.gate, bf16[384,384]{1,0:T(8,128)(2,1)S(1)} %collective-permute-done.17.rest_0_, bf16[384,384]{1,0:T(8,128)(2,1)S(1)} %collective-permute-done.18.rest_1_), custom_call_target="tpu_custom_call" | custom-call | flops 1179648 | bytes 2097152 | tf_op jit(solution)/shard_map/pallas_call | solution.py:362
  (12 shorter events, 0.1 us)
Async XLA Ops:
  0.0 25.2 %copy-start.2 = (bf16[384,768]{1,0:T(8,128)(2,1)S(1)}, bf16[384,768]{1,0:T(8,128)(2,1)}, u32[]{:S(2)}) copy-start(bf16[384,768]{1,0:T(8,128)(2,1)} %q_hbm) | copy-start | bytes 1769476
  0.0 25.2 %copy-start.3 = (f32[6,128]{1,0:T(8,128)S(1)}, f32[6,128]{1,0:T(8,128)}, u32[]{:S(2)}) copy-start(f32[6,128]{1,0:T(8,128)} %qg_hbm.1) | copy-start | bytes 9220
  2.8 24.5 %collective-permute-start.4 = (bf16[384,1536]{1,0:T(8,128)(2,1)}, bf16[384,1536]{1,0:T(8,128)(2,1)S(1)}, u32[]{:S(2)}, u32[]{:S(2)}) collective-permute-start(bf16[384,1536]{1,0:T(8,128)(2,1)} %get-tuple-element.28.refs_2_.kvw), channel_id=1, source_target_pairs={{4,8},{8,4},{5,9},{9,5},{6,10},{10,6},{7,11},{11,7},{20,24},{24,20... | collective-permute-start | bytes 3538952 | tf_op jit(solution)/shard_map/ppermute | solution.py:356
  3.6 32.9 %collective-permute-start.3 = (bf16[384,1536]{1,0:T(8,128)(2,1)}, bf16[384,1536]{1,0:T(8,128)(2,1)S(1)}, u32[]{:S(2)}, u32[]{:S(2)}) collective-permute-start(bf16[384,1536]{1,0:T(8,128)(2,1)} %get-tuple-element.28.refs_2_.kvw), channel_id=1, source_target_pairs={{0,4},{4,0},{8,12},{12,8},{1,5},{5,1},{9,13},{13,9},{2,6},{6,2},{1... | collective-permute-start | bytes 3538952 | tf_op jit(solution)/shard_map/ppermute | solution.py:353
  9.4 14.7 %collective-permute-start = (bf16[384,768]{1,0:T(8,128)(2,1)}, bf16[384,768]{1,0:T(8,128)(2,1)S(1)}, u32[]{:S(2)}, u32[]{:S(2)}) collective-permute-start(bf16[384,768]{1,0:T(8,128)(2,1)} %get-tuple-element.27), channel_id=1, source_target_pairs={{0,16},{16,0},{1,17},{17,1},{2,18},{18,2},{3,19},{19,3},{4,20},{20... | collective-permute-start | bytes 1769480 | tf_op jit(solution)/shard_map/ppermute | solution.py:350
  24.1 25.0 %collective-permute-start.1 = (bf16[384,768]{1,0:T(8,128)(2,1)S(1)}, bf16[384,768]{1,0:T(8,128)(2,1)S(1)}, u32[]{:S(2)}, u32[]{:S(2)}) collective-permute-start(bf16[384,768]{1,0:T(8,128)(2,1)S(1)} %collective-permute-done.refs_1_), channel_id=1, source_target_pairs={{0,4},{4,0},{8,12},{12,8},{1,5},{5,1},{9,13},{13,9},{2,6},{6,2},{1... | collective-permute-start | bytes 1769480 | tf_op jit(solution)/shard_map/ppermute | solution.py:353
  24.5 24.6 %collective-permute-start.2 = (bf16[384,768]{1,0:T(8,128)(2,1)S(1)}, bf16[384,768]{1,0:T(8,128)(2,1)S(1)}, u32[]{:S(2)}, u32[]{:S(2)}) collective-permute-start(bf16[384,768]{1,0:T(8,128)(2,1)S(1)} %collective-permute-done.refs_1_), channel_id=1, source_target_pairs={{4,8},{8,4},{5,9},{9,5},{6,10},{10,6},{7,11},{11,7},{20,24},{24,20... | collective-permute-start | bytes 1769480 | tf_op jit(solution)/shard_map/ppermute | solution.py:356
  25.8 10.8 %copy-start = (bf16[384,1536]{1,0:T(8,128)(2,1)S(1)}, bf16[384,1536]{1,0:T(8,128)(2,1)}, u32[]{:S(2)}) copy-start(bf16[384,1536]{1,0:T(8,128)(2,1)} %get-tuple-element.28.refs_2_.kvw) | copy-start | bytes 3538948
  25.8 10.8 %collective-permute-start.5 = (bf16[384,384]{1,0:T(8,128)(2,1)S(1)}, bf16[384,384]{1,0:T(8,128)(2,1)S(1)}, u32[]{:S(2)}, u32[]{:S(2)}) collective-permute-start(bf16[384,384]{1,0:T(8,128)(2,1)S(1)} %get-tuple-element.29), channel_id=1, source_target_pairs={{0,16},{16,0},{1,17},{17,1},{2,18},{18,2},{3,19},{19,3},{4,20},{20... | collective-permute-start | bytes 884744 | tf_op jit(solution)/shard_map/ppermute | solution.py:350
  41.0 20.0 %collective-permute-start.7 = (bf16[384,768]{1,0:T(8,128)(2,1)S(1)}, bf16[384,768]{1,0:T(8,128)(2,1)S(1)}, u32[]{:S(2)}, u32[]{:S(2)}) collective-permute-start(bf16[384,768]{1,0:T(8,128)(2,1)S(1)} %slice.13), channel_id=1, source_target_pairs={{4,0},{8,12},{5,1},{9,13},{6,2},{10,14},{7,3},{11,15},{20,16},{24,... | collective-permute-start | bytes 1769480 | tf_op jit(solution)/shard_map/ppermute | solution.py:373
  42.3 12.0 %collective-permute-start.11 = (bf16[384,384]{1,0:T(8,128)(2,1)S(1)}, bf16[384,384]{1,0:T(8,128)(2,1)S(1)}, u32[]{:S(2)}, u32[]{:S(2)}) collective-permute-start(bf16[384,384]{1,0:T(8,128)(2,1)S(1)} %get-tuple-element.38), channel_id=1, source_target_pairs={{4,8},{8,4},{5,9},{9,5},{6,10},{10,6},{7,11},{11,7},{20,24},{24,20... | collective-permute-start | bytes 884744 | tf_op jit(solution)/shard_map/ppermute | solution.py:356
  52.0 6.8 %collective-permute-start.15 = (bf16[384,384]{1,0:T(8,128)(2,1)S(1)}, bf16[384,384]{1,0:T(8,128)(2,1)S(1)}, u32[]{:S(2)}, u32[]{:S(2)}) collective-permute-start(bf16[384,384]{1,0:T(8,128)(2,1)S(1)} %shard_map.85.a0), channel_id=1, source_target_pairs={{0,2},{1,3},{2,0},{3,1},{4,6},{5,7},{6,4},{7,5},{8,10},{9,11},{10,... | collective-permute-start | bytes 884744 | tf_op jit(solution)/shard_map/ppermute | solution.py:359
  53.6 5.2 %collective-permute-start.6 = (bf16[384,384]{1,0:T(8,128)(2,1)S(1)}, bf16[384,384]{1,0:T(8,128)(2,1)S(1)}, u32[]{:S(2)}, u32[]{:S(2)}) collective-permute-start(bf16[384,384]{1,0:T(8,128)(2,1)S(1)} %get-tuple-element.34), channel_id=1, source_target_pairs={{4,8},{8,4},{5,9},{9,5},{6,10},{10,6},{7,11},{11,7},{20,24},{24,20... | collective-permute-start | bytes 884744 | tf_op jit(solution)/shard_map/ppermute | solution.py:356
  54.3 9.7 %collective-permute-start.14 = (bf16[384,384]{1,0:T(8,128)(2,1)S(1)}, bf16[384,384]{1,0:T(8,128)(2,1)S(1)}, u32[]{:S(2)}, u32[]{:S(2)}) collective-permute-start(bf16[384,384]{1,0:T(8,128)(2,1)S(1)} %shard_map.85.a0), channel_id=1, source_target_pairs={{0,1},{1,0},{2,3},{3,2},{4,5},{5,4},{6,7},{7,6},{8,9},{9,8},{10,11... | collective-permute-start | bytes 884744 | tf_op jit(solution)/shard_map/ppermute | solution.py:359
  54.4 12.9 %collective-permute-start.12 = (bf16[384,384]{1,0:T(8,128)(2,1)S(1)}, bf16[384,384]{1,0:T(8,128)(2,1)S(1)}, u32[]{:S(2)}, u32[]{:S(2)}) collective-permute-start(bf16[384,384]{1,0:T(8,128)(2,1)S(1)} %collective-permute-done.11.rest_0_.forward), channel_id=1, source_target_pairs={{4,0},{8,12},{5,1},{9,13},{6,2},{10,14},{7,3},{11,15},{20,16},{24,... | collective-permute-start | bytes 884744 | tf_op jit(solution)/shard_map/ppermute | solution.py:373
  58.8 8.5 %collective-permute-start.16 = (bf16[384,384]{1,0:T(8,128)(2,1)S(1)}, bf16[384,384]{1,0:T(8,128)(2,1)S(1)}, u32[]{:S(2)}, u32[]{:S(2)}) collective-permute-start(bf16[384,384]{1,0:T(8,128)(2,1)S(1)} %collective-permute-done.15.a2), channel_id=1, source_target_pairs={{0,1},{1,0},{2,3},{3,2},{4,5},{5,4},{6,7},{7,6},{8,9},{9,8},{10,11... | collective-permute-start | bytes 884744 | tf_op jit(solution)/shard_map/ppermute | solution.py:359
  58.8 14.4 %collective-permute-start.13 = (bf16[384,384]{1,0:T(8,128)(2,1)S(1)}, bf16[384,384]{1,0:T(8,128)(2,1)S(1)}, u32[]{:S(2)}, u32[]{:S(2)}) collective-permute-start(bf16[384,384]{1,0:T(8,128)(2,1)S(1)} %collective-permute-done.6.rest_1_.forward), channel_id=1, source_target_pairs={{4,0},{8,12},{5,1},{9,13},{6,2},{10,14},{7,3},{11,15},{20,16},{24,... | collective-permute-start | bytes 884744 | tf_op jit(solution)/shard_map/ppermute | solution.py:373
  63.9 6.0 %collective-permute-start.8 = (bf16[384,384]{1,0:T(8,128)(2,1)S(1)}, bf16[384,384]{1,0:T(8,128)(2,1)S(1)}, u32[]{:S(2)}, u32[]{:S(2)}) collective-permute-start(bf16[384,384]{1,0:T(8,128)(2,1)S(1)} %shard_map.86.a0), channel_id=1, source_target_pairs={{0,1},{1,0},{2,3},{3,2},{4,5},{5,4},{6,7},{7,6},{8,9},{9,8},{10,11... | collective-permute-start | bytes 884744 | tf_op jit(solution)/shard_map/ppermute | solution.py:359
  64.0 11.8 %collective-permute-start.9 = (bf16[384,384]{1,0:T(8,128)(2,1)S(1)}, bf16[384,384]{1,0:T(8,128)(2,1)S(1)}, u32[]{:S(2)}, u32[]{:S(2)}) collective-permute-start(bf16[384,384]{1,0:T(8,128)(2,1)S(1)} %shard_map.86.a0), channel_id=1, source_target_pairs={{0,2},{1,3},{2,0},{3,1},{4,6},{5,7},{6,4},{7,5},{8,10},{9,11},{10,... | collective-permute-start | bytes 884744 | tf_op jit(solution)/shard_map/ppermute | solution.py:359
  68.3 7.5 %copy-start.4 = (f32[768]{0:T(1024)S(1)}, f32[768]{0:T(1024)}, u32[]{:S(2)}) copy-start(f32[768]{0:T(1024)} %param.15) | copy-start | bytes 9220
  68.3 11.9 %copy-start.1 = (bf16[384,768]{1,0:T(8,128)(2,1)S(1)}, bf16[384,768]{1,0:T(8,128)(2,1)}, u32[]{:S(2)}) copy-start(bf16[384,768]{1,0:T(8,128)(2,1)} %stream_hbm.1) | copy-start | bytes 1769476
  68.3 14.0 %collective-permute-start.17 = (bf16[384,384]{1,0:T(8,128)(2,1)S(1)}, bf16[384,384]{1,0:T(8,128)(2,1)S(1)}, u32[]{:S(2)}, u32[]{:S(2)}) collective-permute-start(bf16[384,384]{1,0:T(8,128)(2,1)S(1)} %shard_map.88), channel_id=1, source_target_pairs={{0,16},{16,0},{1,17},{17,1},{2,18},{18,2},{3,19},{19,3},{4,20},{20... | collective-permute-start | bytes 884744 | tf_op jit(solution)/shard_map/ppermute | solution.py:350
  69.9 10.3 %collective-permute-start.10 = (bf16[384,384]{1,0:T(8,128)(2,1)S(1)}, bf16[384,384]{1,0:T(8,128)(2,1)S(1)}, u32[]{:S(2)}, u32[]{:S(2)}) collective-permute-start(bf16[384,384]{1,0:T(8,128)(2,1)S(1)} %collective-permute-done.8.a1), channel_id=1, source_target_pairs={{0,2},{1,3},{2,0},{3,1},{4,6},{5,7},{6,4},{7,5},{8,10},{9,11},{10,... | collective-permute-start | bytes 884744 | tf_op jit(solution)/shard_map/ppermute | solution.py:359
  74.2 8.7 %collective-permute-start.18 = (bf16[384,384]{1,0:T(8,128)(2,1)S(1)}, bf16[384,384]{1,0:T(8,128)(2,1)S(1)}, u32[]{:S(2)}, u32[]{:S(2)}) collective-permute-start(bf16[384,384]{1,0:T(8,128)(2,1)S(1)} %shard_map.89), channel_id=1, source_target_pairs={{0,16},{16,0},{1,17},{17,1},{2,18},{18,2},{3,19},{19,3},{4,20},{20... | collective-permute-start | bytes 884744 | tf_op jit(solution)/shard_map/ppermute | solution.py:350

commit v7 on v6

--- a/solution.py
+++ b/solution.py
@@ -304,7 +304,7 @@
         out[...] = total.astype(out.dtype)
 
     def weights(which, part, low, high):
-        held = inner[:, slice(*span)], forward[...], outer[...]
+        held = inner[...], forward[...], outer[...]
         return weight_of(kvw, kvw_pair, kvw_mid, *held, which, low, high)
 
     plane_sum([a[...] for a in (a0, a1, a2, a3)], weights, [span], write)
@@ -321,7 +321,7 @@
         out[:, low:high] = stream[:, low:high].astype(jnp.float32) + gate[:, low:high] * total
 
     def weights(which, part, low, high):
-        held = inner[0][:, low:high], forward[part][...], outer[part][...]
+        held = inner[part][...], forward[part][...], outer[part][...]
         return weight_of(kvw, kvw_pair, kvw_mid, *held, which, low, high)
 
     plane_sum([a[...] for a in (a0, a1, a2, a3)], weights, spans, write)
@@ -382,13 +382,14 @@
     carry = attend((0, 1), [q_keep, q_peer], [kvw, kvw_pair, kvw_mid], head_size)
     starts = [width + low for low, high in spans] + [2 * width]
     halves = [slice(starts[part], starts[part + 1]) for part in range(2)]
-    first_pair, early_mid, carry = barrier((kvw_pair[:, halves[0]], kvw_mid[:, width:], carry))
+    first_pair, early_mid, carry = barrier((kvw_pair[:, halves[0]], kvw_mid[:, halves[0]], carry))
     inner, forwards = [inward(early_mid)], [middle(first_pair)]
     layers = [kv_peer, peer_pair, peer_mid]
     theirs = attend((1,), [q_peer], layers, head_size, carry)
     across_theirs, beside_theirs = along(theirs, "col", 2), along(theirs, "col", 1)
-    next_pair, _ = barrier((kvw_pair[:, halves[1]], theirs))
+    next_pair, next_mid, _ = barrier((kvw_pair[:, halves[1]], kvw_mid[:, halves[1]], theirs))
     forwards.append(middle(next_pair))
+    inner.append(inward(next_mid))
     outer = [inward(forwards[part]) for part in range(2)]
 
     gate = gate.reshape(1, width)
@@ -398,7 +399,7 @@
     for part, (low, high) in enumerate(spans):
         sent = call(
             functools.partial(peer_kernel, (low, high)),
-            [*groups, kvw, kvw_pair, kvw_mid, inner[0], forwards[part], outer[part]],
+            [*groups, kvw, kvw_pair, kvw_mid, inner[part], forwards[part], outer[part]],
             [vmem] * 10,
             jax.ShapeDtypeStruct((tokens, high - low), jnp.bfloat16),
             vmem,

time: 84.3 us -> 93.5 us (1.11)
  waiting for transfers between devices: 39.3 us -> 50.2 us
  starting transfers between devices: 25.5 us -> 23.8 us
    ppermute x3 -> x4, waiting for transfers between devices: 2.74 us -> 18.5 us  [inward(): return lax.ppermute(x, 'row', [(1, 0), (2, 3)])]
    ppermute x6, waiting for transfers between devices: 7.59 us -> 3.19 us  [along(): return lax.ppermute(x, axis, [(i, i ^ mask) for i in range(4)])]
    ppermute x2, waiting for transfers between devices: 15.2 us -> 11.2 us  [pair(): return lax.ppermute(x, 'row', [(i, i ^ 1) for i in range(4)])]
    ppermute x4, waiting for transfers between devices: 13.8 us -> 17.3 us  [swap(): return lax.ppermute(x, 'seq', [(0, 1), (1, 0)])]
    ppermute x6, starting transfers between devices: 6.25 us -> 3 us  [along(): return lax.ppermute(x, axis, [(i, i ^ mask) for i in range(4)])]
    ppermute x3 -> x4, starting transfers between devices: 4.05 us -> 5.33 us  [inward(): return lax.ppermute(x, 'row', [(1, 0), (2, 3)])]
    ppermute x2, starting transfers between devices: 6.19 us -> 7.43 us  [pair(): return lax.ppermute(x, 'row', [(i, i ^ 1) for i in range(4)])]
    ppermute x4, starting transfers between devices: 6.28 us -> 5.33 us  [swap(): return lax.ppermute(x, 'seq', [(0, 1), (1, 0)])]
  transfers between devices with their start and end apart: 19 -> 20, of which waited for: 9 -> 9; matrix products, arithmetic and copies ran while one was open for 0% -> 0% of each run, Pallas kernels for 18% -> 16%
where the time goes in v7:
time: 93.5 us; the launch traced here: 93.3 us
  waiting for transfers between devices  50.2 us (54%)
  starting transfers between devices  23.8 us (25%)
  Pallas kernels  18.6 us (20%)
    ppermute x4, waiting for transfers between devices, inward(): return lax.ppermute(x, 'row', [(1, 0), (2, 3)])  18.5 us
    ppermute x4, waiting for transfers between devices, swap(): return lax.ppermute(x, 'seq', [(0, 1), (1, 0)])  17.3 us
    ppermute x2, waiting for transfers between devices, pair(): return lax.ppermute(x, 'row', [(i, i ^ 1) for i in range(4)])  11.2 us
    pallas_call x3, Pallas kernels, attend(): pl.pallas_call(functools.partial(attend_kernel, 1.0 / math.sqrt(head_size...  10.3 us
    ppermute x2, starting transfers between devices, pair(): return lax.ppermute(x, 'row', [(i, i ^ 1) for i in range(4)])  7.43 us
    ppermute x4, starting transfers between devices, swap(): return lax.ppermute(x, 'seq', [(0, 1), (1, 0)])  5.33 us
    ppermute x4, starting transfers between devices, inward(): return lax.ppermute(x, 'row', [(1, 0), (2, 3)])  5.33 us
    pallas_call x4, Pallas kernels, call(): pl.pallas_call(kernel, out_shape=out_shape, in_specs=specs, out_specs=out...  4.96 us
  transfers between devices with their start and end apart: 20, of which 9 were waited for; matrix products, arithmetic and copies ran while one was open for 0% of the time, Pallas kernels for 16%

profile of v7, /device:TPU:0, one launch (start us, length us, event | category | flops | bytes accessed | tf_op | source)
XLA Modules:
  0.0 93.3 jit_solution(11364937802808646692)
XLA Ops:
  0.0 2.8 %shard_map.82 = (bf16[384,768]{1,0:T(8,128)(2,1)}, bf16[384,1536]{1,0:T(8,128)(2,1)}) custom-call(bf16[384,768]{1,0:T(8,128)(2,1)} %k_hbm.1, bf16[384,768]{1,0:T(8,128)(2,1)} %v_hbm.1, f32[6,128]{1,0:T(8,128)} %kg_hbm.1, bf16[768,768]{1,0:T(8,128)(2,1)} %w_hbm.1), custom_call_target="tpu_custom_call" | custom-call | flops 2359296 | bytes 1769472 | tf_op jit(solution)/shard_map/pallas_call | solution.py:177
  2.8 3.1 %collective-permute-start.3 = (bf16[384,1536]{1,0:T(8,128)(2,1)}, bf16[384,1536]{1,0:T(8,128)(2,1)S(1)}, u32[]{:S(2)}, u32[]{:S(2)}) collective-permute-start(bf16[384,1536]{1,0:T(8,128)(2,1)} %get-tuple-element.29.refs_2_.kvw), channel_id=1, source_target_pairs={{0,4},{4,0},{8,12},{12,8},{1,5},{5,1},{9,13},{13,9},{2,6},{6,2},{1... | collective-permute-start | bytes 3538952 | tf_op jit(solution)/shard_map/ppermute | solution.py:353
  5.9 0.7 collective-permute-start.4
  6.6 1.6 %collective-permute-start = (bf16[384,768]{1,0:T(8,128)(2,1)}, bf16[384,768]{1,0:T(8,128)(2,1)S(1)}, u32[]{:S(2)}, u32[]{:S(2)}) collective-permute-start(bf16[384,768]{1,0:T(8,128)(2,1)} %get-tuple-element.28), channel_id=1, source_target_pairs={{0,16},{16,0},{1,17},{17,1},{2,18},{18,2},{3,19},{19,3},{4,20},{20... | collective-permute-start | bytes 1769480 | tf_op jit(solution)/shard_map/ppermute | solution.py:350
  8.2 0.5 shard_map.83
  8.8 0.6 collective-permute-start.5
  9.3 13.8 %collective-permute-done.refs_1_ = bf16[384,768]{1,0:T(8,128)(2,1)S(1)} collective-permute-done((bf16[384,768]{1,0:T(8,128)(2,1)}, bf16[384,768]{1,0:T(8,128)(2,1)S(1)}, u32[]{:S(2)}, u32[]{:S(2)}) %collective-permute-start) | collective-permute-done | bytes 589856 | tf_op jit(solution)/shard_map/ppermute | solution.py:350
  23.2 4.3 %collective-permute-start.1 = (bf16[384,768]{1,0:T(8,128)(2,1)S(1)}, bf16[384,768]{1,0:T(8,128)(2,1)S(1)}, u32[]{:S(2)}, u32[]{:S(2)}) collective-permute-start(bf16[384,768]{1,0:T(8,128)(2,1)S(1)} %collective-permute-done.refs_1_), channel_id=1, source_target_pairs={{0,4},{4,0},{8,12},{12,8},{1,5},{5,1},{9,13},{13,9},{2,6},{6,2},{1... | collective-permute-start | bytes 1769480 | tf_op jit(solution)/shard_map/ppermute | solution.py:353
  27.5 0.7 collective-permute-start.2
  28.2 4.7 %collective-permute-done.3.refs_3_.kvw_pair = bf16[384,1536]{1,0:T(8,128)(2,1)S(1)} collective-permute-done((bf16[384,1536]{1,0:T(8,128)(2,1)}, bf16[384,1536]{1,0:T(8,128)(2,1)S(1)}, u32[]{:S(2)}, u32[]{:S(2)}) %collective-permute-start.3) | collective-permute-done | bytes 1179680 | tf_op jit(solution)/shard_map/ppermute | solution.py:353
  32.9 0.1 fusion.1
  33.0 0.0 collective-permute-done.4.refs_4_.kvw_mid
  33.0 0.1 fusion
  33.1 0.0 collective-permute-done.5.refs_1_.refs_0_
  33.1 4.5 %shard_map.84 = (f32[3,2,384,128]{3,2,1,0:T(8,128)S(1)}, f32[3,2,384,256]{3,2,1,0:T(8,128)S(1)}) custom-call(bf16[384,384]{1,0:T(8,128)(2,1)S(1)} %get-tuple-element.27.refs_0_, bf16[384,384]{1,0:T(8,128)(2,1)S(1)} %collective-permute-done.5.refs_1_.refs_0_, bf16[384,1536]{1,0:T(8,128)(2,1)S(1)} %copy-done, ...), custom_call_target="tpu_custom_call" | custom-call | flops 2717908992 | bytes 8388608 | tf_op jit(solution)/shard_map/pallas_call | solution.py:264
  37.5 0.7 collective-permute-start.11
  38.2 6.5 %collective-permute-done.1.refs_2_ = bf16[384,768]{1,0:T(8,128)(2,1)S(1)} collective-permute-done((bf16[384,768]{1,0:T(8,128)(2,1)S(1)}, bf16[384,768]{1,0:T(8,128)(2,1)S(1)}, u32[]{:S(2)}, u32[]{:S(2)}) %collective-permute-start.1) | collective-permute-done | bytes 589856 | tf_op jit(solution)/shard_map/ppermute | solution.py:353
  44.7 0.0 collective-permute-done.2.refs_3_
  44.7 2.9 %shard_map.85.a0 = bf16[384,384]{1,0:T(8,128)(2,1)S(1)} custom-call(bf16[384,384]{1,0:T(8,128)(2,1)S(1)} %collective-permute-done.5.refs_1_.refs_0_, bf16[384,768]{1,0:T(8,128)(2,1)S(1)} %collective-permute-done.refs_1_, bf16[384,768]{1,0:T(8,128)(2,1)S(1)} %collective-permute-done.1.refs_2_, bf16[384,768]{1,0:T(8,128)(2,1)S(1)} %collective-permute-done.2.refs_3_, ...), custom_call_target="tpu_custom_call" | custom-call | flops 1358954496 | bytes 8388608 | tf_op jit(solution)/shard_map/pallas_call | solution.py:264
  47.7 1.7 %collective-permute-start.16 = (bf16[384,384]{1,0:T(8,128)(2,1)S(1)}, bf16[384,384]{1,0:T(8,128)(2,1)S(1)}, u32[]{:S(2)}, u32[]{:S(2)}) collective-permute-start(bf16[384,384]{1,0:T(8,128)(2,1)S(1)} %shard_map.85.a0), channel_id=1, source_target_pairs={{0,2},{1,3},{2,0},{3,1},{4,6},{5,7},{6,4},{7,5},{8,10},{9,11},{10,... | collective-permute-start | bytes 884744 | tf_op jit(solution)/shard_map/ppermute | solution.py:359
  49.4 0.7 collective-permute-start.6
  50.1 1.3 %collective-permute-start.7 = (bf16[384,384]{1,0:T(8,128)(2,1)S(1)}, bf16[384,384]{1,0:T(8,128)(2,1)S(1)}, u32[]{:S(2)}, u32[]{:S(2)}) collective-permute-start(bf16[384,384]{1,0:T(8,128)(2,1)S(1)} %get-tuple-element.36), channel_id=1, source_target_pairs={{4,0},{8,12},{5,1},{9,13},{6,2},{10,14},{7,3},{11,15},{20,16},{24,... | collective-permute-start | bytes 884744 | tf_op jit(solution)/shard_map/ppermute | solution.py:373
  51.4 0.1 collective-permute-start.15
  51.4 1.3 %collective-permute-start.12 = (bf16[384,384]{1,0:T(8,128)(2,1)S(1)}, bf16[384,384]{1,0:T(8,128)(2,1)S(1)}, u32[]{:S(2)}, u32[]{:S(2)}) collective-permute-start(bf16[384,384]{1,0:T(8,128)(2,1)S(1)} %collective-permute-done.11.rest_0_.forward), channel_id=1, source_target_pairs={{4,0},{8,12},{5,1},{9,13},{6,2},{10,14},{7,3},{11,15},{20,16},{24,... | collective-permute-start | bytes 884744 | tf_op jit(solution)/shard_map/ppermute | solution.py:373
  52.7 3.2 %collective-permute-done.16.a2 = bf16[384,384]{1,0:T(8,128)(2,1)S(1)} collective-permute-done((bf16[384,384]{1,0:T(8,128)(2,1)S(1)}, bf16[384,384]{1,0:T(8,128)(2,1)S(1)}, u32[]{:S(2)}, u32[]{:S(2)}) %collective-permute-start.16) | collective-permute-done | bytes 294944 | tf_op jit(solution)/shard_map/ppermute | solution.py:359
  55.9 0.0 collective-permute-start.17
  55.9 0.0 collective-permute-done.6.rest_1_.forward
  55.9 1.5 %collective-permute-start.14 = (bf16[384,384]{1,0:T(8,128)(2,1)S(1)}, bf16[384,384]{1,0:T(8,128)(2,1)S(1)}, u32[]{:S(2)}, u32[]{:S(2)}) collective-permute-start(bf16[384,384]{1,0:T(8,128)(2,1)S(1)} %get-tuple-element.42), channel_id=1, source_target_pairs={{4,0},{8,12},{5,1},{9,13},{6,2},{10,14},{7,3},{11,15},{20,16},{24,... | collective-permute-start | bytes 884744 | tf_op jit(solution)/shard_map/ppermute | solution.py:373
  57.4 9.6 %collective-permute-done.7.rest_4_.inner = bf16[384,384]{1,0:T(8,128)(2,1)S(1)} collective-permute-done((bf16[384,384]{1,0:T(8,128)(2,1)S(1)}, bf16[384,384]{1,0:T(8,128)(2,1)S(1)}, u32[]{:S(2)}, u32[]{:S(2)}) %collective-permute-start.7) | collective-permute-done | bytes 294944 | tf_op jit(solution)/shard_map/ppermute | solution.py:373
  67.0 2.9 %shard_map.86.a0 = bf16[384,384]{1,0:T(8,128)(2,1)S(1)} custom-call(bf16[384,384]{1,0:T(8,128)(2,1)S(1)} %get-tuple-element.27.refs_0_, bf16[384,768]{1,0:T(8,128)(2,1)S(1)} %collective-permute-done.refs_1_, bf16[384,768]{1,0:T(8,128)(2,1)S(1)} %collective-permute-done.1.refs_2_, bf16[384,768]{1,0:T(8,128)(2,1)S(1)} %collective-permute-done.2.refs_3_, ...), custom_call_target="tpu_custom_call" | custom-call | flops 1358954496 | bytes 8388608 | tf_op jit(solution)/shard_map/pallas_call | solution.py:264
  69.9 0.1 collective-permute-start.8
  70.0 0.6 collective-permute-start.9
  70.6 2.7 %collective-permute-done.12.rest_2_.outer = bf16[384,384]{1,0:T(8,128)(2,1)S(1)} collective-permute-done((bf16[384,384]{1,0:T(8,128)(2,1)S(1)}, bf16[384,384]{1,0:T(8,128)(2,1)S(1)}, u32[]{:S(2)}, u32[]{:S(2)}) %collective-permute-start.12) | collective-permute-done | bytes 294944 | tf_op jit(solution)/shard_map/ppermute | solution.py:373
  73.3 1.3 %collective-permute-start.13 = (bf16[384,384]{1,0:T(8,128)(2,1)S(1)}, bf16[384,384]{1,0:T(8,128)(2,1)S(1)}, u32[]{:S(2)}, u32[]{:S(2)}) collective-permute-start(bf16[384,384]{1,0:T(8,128)(2,1)S(1)} %collective-permute-done.6.rest_1_.forward), channel_id=1, source_target_pairs={{4,0},{8,12},{5,1},{9,13},{6,2},{10,14},{7,3},{11,15},{20,16},{24,... | collective-permute-start | bytes 884744 | tf_op jit(solution)/shard_map/ppermute | solution.py:373
  74.6 0.0 collective-permute-done.17.a3
  74.6 1.0 %shard_map.88 = bf16[384,384]{1,0:T(8,128)(2,1)S(1)} custom-call(bf16[384,384]{1,0:T(8,128)(2,1)S(1)} %shard_map.85.a0, bf16[384,384]{1,0:T(8,128)(2,1)S(1)} %collective-permute-done.15.a1, bf16[384,384]{1,0:T(8,128)(2,1)S(1)} %collective-permute-done.16.a2, bf16[384,384]{1,0:T(8,128)(2,1)S(1)} %collective-permute-done.17.a3, bf16[384,1536]{1,0:T(8,128)(2,1)S(1)} %copy-done, ...), custom_call_target="tpu_custom_call" | custom-call | flops 4529848320 | bytes 2097152 | tf_op jit(solution)/shard_map/pallas_call | solution.py:362
  75.6 0.0 copy-start.4
  75.6 0.0 copy-start.1
  75.6 1.6 %collective-permute-start.18 = (bf16[384,384]{1,0:T(8,128)(2,1)S(1)}, bf16[384,384]{1,0:T(8,128)(2,1)S(1)}, u32[]{:S(2)}, u32[]{:S(2)}) collective-permute-start(bf16[384,384]{1,0:T(8,128)(2,1)S(1)} %shard_map.88), channel_id=1, source_target_pairs={{0,16},{16,0},{1,17},{17,1},{2,18},{18,2},{3,19},{19,3},{4,20},{20... | collective-permute-start | bytes 884744 | tf_op jit(solution)/shard_map/ppermute | solution.py:350
  77.2 0.0 collective-permute-done.8.a1
  77.2 0.5 collective-permute-start.10
  77.8 1.9 %collective-permute-done.14.rest_5_.inner = bf16[384,384]{1,0:T(8,128)(2,1)S(1)} collective-permute-done((bf16[384,384]{1,0:T(8,128)(2,1)S(1)}, bf16[384,384]{1,0:T(8,128)(2,1)S(1)}, u32[]{:S(2)}, u32[]{:S(2)}) %collective-permute-start.14) | collective-permute-done | bytes 294944 | tf_op jit(solution)/shard_map/ppermute | solution.py:373
  79.6 4.4 %collective-permute-done.13.rest_3_.outer = bf16[384,384]{1,0:T(8,128)(2,1)S(1)} collective-permute-done((bf16[384,384]{1,0:T(8,128)(2,1)S(1)}, bf16[384,384]{1,0:T(8,128)(2,1)S(1)}, u32[]{:S(2)}, u32[]{:S(2)}) %collective-permute-start.13) | collective-permute-done | bytes 294944 | tf_op jit(solution)/shard_map/ppermute | solution.py:373
  84.0 1.0 %shard_map.89 = bf16[384,384]{1,0:T(8,128)(2,1)S(1)} custom-call(bf16[384,384]{1,0:T(8,128)(2,1)S(1)} %shard_map.85.a0, bf16[384,384]{1,0:T(8,128)(2,1)S(1)} %collective-permute-done.15.a1, bf16[384,384]{1,0:T(8,128)(2,1)S(1)} %collective-permute-done.16.a2, bf16[384,384]{1,0:T(8,128)(2,1)S(1)} %collective-permute-done.17.a3, bf16[384,1536]{1,0:T(8,128)(2,1)S(1)} %copy-done, ...), custom_call_target="tpu_custom_call" | custom-call | flops 4529848320 | bytes 2097152 | tf_op jit(solution)/shard_map/pallas_call | solution.py:362
  85.0 1.6 %collective-permute-start.19 = (bf16[384,384]{1,0:T(8,128)(2,1)S(1)}, bf16[384,384]{1,0:T(8,128)(2,1)S(1)}, u32[]{:S(2)}, u32[]{:S(2)}) collective-permute-start(bf16[384,384]{1,0:T(8,128)(2,1)S(1)} %shard_map.89), channel_id=1, source_target_pairs={{0,16},{16,0},{1,17},{17,1},{2,18},{18,2},{3,19},{19,3},{4,20},{20... | collective-permute-start | bytes 884744 | tf_op jit(solution)/shard_map/ppermute | solution.py:350
  86.6 2.1 %shard_map.87.base = f32[384,768]{1,0:T(8,128)S(1)} custom-call(bf16[384,384]{1,0:T(8,128)(2,1)S(1)} %shard_map.86.a0, bf16[384,384]{1,0:T(8,128)(2,1)S(1)} %collective-permute-done.8.a1, bf16[384,384]{1,0:T(8,128)(2,1)S(1)} %collective-permute-done.9.a2, bf16[384,384]{1,0:T(8,128)(2,1)S(1)} %collective-permute-done.10.a3, bf16[384,1536]{1,0:T(8,128)(2,1)S(1)} %copy-done, ...), custom_call_target="tpu_custom_call" | custom-call | flops 905969664 | bytes 2097152 | tf_op jit(solution)/shard_map/pallas_call | solution.py:362
  88.7 3.4 %collective-permute-done.19.rest_1_ = bf16[384,384]{1,0:T(8,128)(2,1)S(1)} collective-permute-done((bf16[384,384]{1,0:T(8,128)(2,1)S(1)}, bf16[384,384]{1,0:T(8,128)(2,1)S(1)}, u32[]{:S(2)}, u32[]{:S(2)}) %collective-permute-start.19) | collective-permute-done | bytes 294944 | tf_op jit(solution)/shard_map/ppermute | solution.py:350
  92.2 0.9 shard_map.90
  (14 shorter events, 0.0 us)
Async XLA Ops:
  0.0 8.2 %copy-start.2 = (bf16[384,768]{1,0:T(8,128)(2,1)S(1)}, bf16[384,768]{1,0:T(8,128)(2,1)}, u32[]{:S(2)}) copy-start(bf16[384,768]{1,0:T(8,128)(2,1)} %q_hbm) | copy-start | bytes 1769476
  0.0 8.2 %copy-start.3 = (f32[6,128]{1,0:T(8,128)S(1)}, f32[6,128]{1,0:T(8,128)}, u32[]{:S(2)}) copy-start(f32[6,128]{1,0:T(8,128)} %qg_hbm.1) | copy-start | bytes 9220
  2.8 30.1 %collective-permute-start.3 = (bf16[384,1536]{1,0:T(8,128)(2,1)}, bf16[384,1536]{1,0:T(8,128)(2,1)S(1)}, u32[]{:S(2)}, u32[]{:S(2)}) collective-permute-start(bf16[384,1536]{1,0:T(8,128)(2,1)} %get-tuple-element.29.refs_2_.kvw), channel_id=1, source_target_pairs={{0,4},{4,0},{8,12},{12,8},{1,5},{5,1},{9,13},{13,9},{2,6},{6,2},{1... | collective-permute-start | bytes 3538952 | tf_op jit(solution)/shard_map/ppermute | solution.py:353
  5.9 27.1 %collective-permute-start.4 = (bf16[384,1536]{1,0:T(8,128)(2,1)}, bf16[384,1536]{1,0:T(8,128)(2,1)S(1)}, u32[]{:S(2)}, u32[]{:S(2)}) collective-permute-start(bf16[384,1536]{1,0:T(8,128)(2,1)} %get-tuple-element.29.refs_2_.kvw), channel_id=1, source_target_pairs={{4,8},{8,4},{5,9},{9,5},{6,10},{10,6},{7,11},{11,7},{20,24},{24,20... | collective-permute-start | bytes 3538952 | tf_op jit(solution)/shard_map/ppermute | solution.py:356
  6.6 16.5 %collective-permute-start = (bf16[384,768]{1,0:T(8,128)(2,1)}, bf16[384,768]{1,0:T(8,128)(2,1)S(1)}, u32[]{:S(2)}, u32[]{:S(2)}) collective-permute-start(bf16[384,768]{1,0:T(8,128)(2,1)} %get-tuple-element.28), channel_id=1, source_target_pairs={{0,16},{16,0},{1,17},{17,1},{2,18},{18,2},{3,19},{19,3},{4,20},{20... | collective-permute-start | bytes 1769480 | tf_op jit(solution)/shard_map/ppermute | solution.py:350
  8.8 24.3 %copy-start = (bf16[384,1536]{1,0:T(8,128)(2,1)S(1)}, bf16[384,1536]{1,0:T(8,128)(2,1)}, u32[]{:S(2)}) copy-start(bf16[384,1536]{1,0:T(8,128)(2,1)} %get-tuple-element.29.refs_2_.kvw) | copy-start | bytes 3538948
  8.8 24.3 %collective-permute-start.5 = (bf16[384,384]{1,0:T(8,128)(2,1)S(1)}, bf16[384,384]{1,0:T(8,128)(2,1)S(1)}, u32[]{:S(2)}, u32[]{:S(2)}) collective-permute-start(bf16[384,384]{1,0:T(8,128)(2,1)S(1)} %get-tuple-element.30), channel_id=1, source_target_pairs={{0,16},{16,0},{1,17},{17,1},{2,18},{18,2},{3,19},{19,3},{4,20},{20... | collective-permute-start | bytes 884744 | tf_op jit(solution)/shard_map/ppermute | solution.py:350
  23.2 21.6 %collective-permute-start.1 = (bf16[384,768]{1,0:T(8,128)(2,1)S(1)}, bf16[384,768]{1,0:T(8,128)(2,1)S(1)}, u32[]{:S(2)}, u32[]{:S(2)}) collective-permute-start(bf16[384,768]{1,0:T(8,128)(2,1)S(1)} %collective-permute-done.refs_1_), channel_id=1, source_target_pairs={{0,4},{4,0},{8,12},{12,8},{1,5},{5,1},{9,13},{13,9},{2,6},{6,2},{1... | collective-permute-start | bytes 1769480 | tf_op jit(solution)/shard_map/ppermute | solution.py:353
  27.5 17.2 %collective-permute-start.2 = (bf16[384,768]{1,0:T(8,128)(2,1)S(1)}, bf16[384,768]{1,0:T(8,128)(2,1)S(1)}, u32[]{:S(2)}, u32[]{:S(2)}) collective-permute-start(bf16[384,768]{1,0:T(8,128)(2,1)S(1)} %collective-permute-done.refs_1_), channel_id=1, source_target_pairs={{4,8},{8,4},{5,9},{9,5},{6,10},{10,6},{7,11},{11,7},{20,24},{24,20... | collective-permute-start | bytes 1769480 | tf_op jit(solution)/shard_map/ppermute | solution.py:356
  37.5 13.9 %collective-permute-start.11 = (bf16[384,384]{1,0:T(8,128)(2,1)S(1)}, bf16[384,384]{1,0:T(8,128)(2,1)S(1)}, u32[]{:S(2)}, u32[]{:S(2)}) collective-permute-start(bf16[384,384]{1,0:T(8,128)(2,1)S(1)} %get-tuple-element.39), channel_id=1, source_target_pairs={{4,8},{8,4},{5,9},{9,5},{6,10},{10,6},{7,11},{11,7},{20,24},{24,20... | collective-permute-start | bytes 884744 | tf_op jit(solution)/shard_map/ppermute | solution.py:356
  47.7 8.3 %collective-permute-start.16 = (bf16[384,384]{1,0:T(8,128)(2,1)S(1)}, bf16[384,384]{1,0:T(8,128)(2,1)S(1)}, u32[]{:S(2)}, u32[]{:S(2)}) collective-permute-start(bf16[384,384]{1,0:T(8,128)(2,1)S(1)} %shard_map.85.a0), channel_id=1, source_target_pairs={{0,2},{1,3},{2,0},{3,1},{4,6},{5,7},{6,4},{7,5},{8,10},{9,11},{10,... | collective-permute-start | bytes 884744 | tf_op jit(solution)/shard_map/ppermute | solution.py:359
  49.4 6.5 %collective-permute-start.6 = (bf16[384,384]{1,0:T(8,128)(2,1)S(1)}, bf16[384,384]{1,0:T(8,128)(2,1)S(1)}, u32[]{:S(2)}, u32[]{:S(2)}) collective-permute-start(bf16[384,384]{1,0:T(8,128)(2,1)S(1)} %get-tuple-element.35), channel_id=1, source_target_pairs={{4,8},{8,4},{5,9},{9,5},{6,10},{10,6},{7,11},{11,7},{20,24},{24,20... | collective-permute-start | bytes 884744 | tf_op jit(solution)/shard_map/ppermute | solution.py:356
  50.1 16.9 %collective-permute-start.7 = (bf16[384,384]{1,0:T(8,128)(2,1)S(1)}, bf16[384,384]{1,0:T(8,128)(2,1)S(1)}, u32[]{:S(2)}, u32[]{:S(2)}) collective-permute-start(bf16[384,384]{1,0:T(8,128)(2,1)S(1)} %get-tuple-element.36), channel_id=1, source_target_pairs={{4,0},{8,12},{5,1},{9,13},{6,2},{10,14},{7,3},{11,15},{20,16},{24,... | collective-permute-start | bytes 884744 | tf_op jit(solution)/shard_map/ppermute | solution.py:373
  51.4 18.7 %collective-permute-start.15 = (bf16[384,384]{1,0:T(8,128)(2,1)S(1)}, bf16[384,384]{1,0:T(8,128)(2,1)S(1)}, u32[]{:S(2)}, u32[]{:S(2)}) collective-permute-start(bf16[384,384]{1,0:T(8,128)(2,1)S(1)} %shard_map.85.a0), channel_id=1, source_target_pairs={{0,1},{1,0},{2,3},{3,2},{4,5},{5,4},{6,7},{7,6},{8,9},{9,8},{10,11... | collective-permute-start | bytes 884744 | tf_op jit(solution)/shard_map/ppermute | solution.py:359
  51.4 21.9 %collective-permute-start.12 = (bf16[384,384]{1,0:T(8,128)(2,1)S(1)}, bf16[384,384]{1,0:T(8,128)(2,1)S(1)}, u32[]{:S(2)}, u32[]{:S(2)}) collective-permute-start(bf16[384,384]{1,0:T(8,128)(2,1)S(1)} %collective-permute-done.11.rest_0_.forward), channel_id=1, source_target_pairs={{4,0},{8,12},{5,1},{9,13},{6,2},{10,14},{7,3},{11,15},{20,16},{24,... | collective-permute-start | bytes 884744 | tf_op jit(solution)/shard_map/ppermute | solution.py:373
  55.9 18.7 %collective-permute-start.17 = (bf16[384,384]{1,0:T(8,128)(2,1)S(1)}, bf16[384,384]{1,0:T(8,128)(2,1)S(1)}, u32[]{:S(2)}, u32[]{:S(2)}) collective-permute-start(bf16[384,384]{1,0:T(8,128)(2,1)S(1)} %collective-permute-done.16.a2), channel_id=1, source_target_pairs={{0,1},{1,0},{2,3},{3,2},{4,5},{5,4},{6,7},{7,6},{8,9},{9,8},{10,11... | collective-permute-start | bytes 884744 | tf_op jit(solution)/shard_map/ppermute | solution.py:359
  55.9 23.7 %collective-permute-start.14 = (bf16[384,384]{1,0:T(8,128)(2,1)S(1)}, bf16[384,384]{1,0:T(8,128)(2,1)S(1)}, u32[]{:S(2)}, u32[]{:S(2)}) collective-permute-start(bf16[384,384]{1,0:T(8,128)(2,1)S(1)} %get-tuple-element.42), channel_id=1, source_target_pairs={{4,0},{8,12},{5,1},{9,13},{6,2},{10,14},{7,3},{11,15},{20,16},{24,... | collective-permute-start | bytes 884744 | tf_op jit(solution)/shard_map/ppermute | solution.py:373
  69.9 7.3 %collective-permute-start.8 = (bf16[384,384]{1,0:T(8,128)(2,1)S(1)}, bf16[384,384]{1,0:T(8,128)(2,1)S(1)}, u32[]{:S(2)}, u32[]{:S(2)}) collective-permute-start(bf16[384,384]{1,0:T(8,128)(2,1)S(1)} %shard_map.86.a0), channel_id=1, source_target_pairs={{0,1},{1,0},{2,3},{3,2},{4,5},{5,4},{6,7},{7,6},{8,9},{9,8},{10,11... | collective-permute-start | bytes 884744 | tf_op jit(solution)/shard_map/ppermute | solution.py:359
  70.0 16.6 %collective-permute-start.9 = (bf16[384,384]{1,0:T(8,128)(2,1)S(1)}, bf16[384,384]{1,0:T(8,128)(2,1)S(1)}, u32[]{:S(2)}, u32[]{:S(2)}) collective-permute-start(bf16[384,384]{1,0:T(8,128)(2,1)S(1)} %shard_map.86.a0), channel_id=1, source_target_pairs={{0,2},{1,3},{2,0},{3,1},{4,6},{5,7},{6,4},{7,5},{8,10},{9,11},{10,... | collective-permute-start | bytes 884744 | tf_op jit(solution)/shard_map/ppermute | solution.py:359
  73.3 10.7 %collective-permute-start.13 = (bf16[384,384]{1,0:T(8,128)(2,1)S(1)}, bf16[384,384]{1,0:T(8,128)(2,1)S(1)}, u32[]{:S(2)}, u32[]{:S(2)}) collective-permute-start(bf16[384,384]{1,0:T(8,128)(2,1)S(1)} %collective-permute-done.6.rest_1_.forward), channel_id=1, source_target_pairs={{4,0},{8,12},{5,1},{9,13},{6,2},{10,14},{7,3},{11,15},{20,16},{24,... | collective-permute-start | bytes 884744 | tf_op jit(solution)/shard_map/ppermute | solution.py:373
  75.6 11.0 %copy-start.4 = (f32[768]{0:T(1024)S(1)}, f32[768]{0:T(1024)}, u32[]{:S(2)}) copy-start(f32[768]{0:T(1024)} %param.15) | copy-start | bytes 9220
  75.6 11.0 %copy-start.1 = (bf16[384,768]{1,0:T(8,128)(2,1)S(1)}, bf16[384,768]{1,0:T(8,128)(2,1)}, u32[]{:S(2)}) copy-start(bf16[384,768]{1,0:T(8,128)(2,1)} %stream_hbm.1) | copy-start | bytes 1769476
  75.6 13.1 %collective-permute-start.18 = (bf16[384,384]{1,0:T(8,128)(2,1)S(1)}, bf16[384,384]{1,0:T(8,128)(2,1)S(1)}, u32[]{:S(2)}, u32[]{:S(2)}) collective-permute-start(bf16[384,384]{1,0:T(8,128)(2,1)S(1)} %shard_map.88), channel_id=1, source_target_pairs={{0,16},{16,0},{1,17},{17,1},{2,18},{18,2},{3,19},{19,3},{4,20},{20... | collective-permute-start | bytes 884744 | tf_op jit(solution)/shard_map/ppermute | solution.py:350
  77.2 9.4 %collective-permute-start.10 = (bf16[384,384]{1,0:T(8,128)(2,1)S(1)}, bf16[384,384]{1,0:T(8,128)(2,1)S(1)}, u32[]{:S(2)}, u32[]{:S(2)}) collective-permute-start(bf16[384,384]{1,0:T(8,128)(2,1)S(1)} %collective-permute-done.8.a1), channel_id=1, source_target_pairs={{0,2},{1,3},{2,0},{3,1},{4,6},{5,7},{6,4},{7,5},{8,10},{9,11},{10,... | collective-permute-start | bytes 884744 | tf_op jit(solution)/shard_map/ppermute | solution.py:359
  85.0 7.1 %collective-permute-start.19 = (bf16[384,384]{1,0:T(8,128)(2,1)S(1)}, bf16[384,384]{1,0:T(8,128)(2,1)S(1)}, u32[]{:S(2)}, u32[]{:S(2)}) collective-permute-start(bf16[384,384]{1,0:T(8,128)(2,1)S(1)} %shard_map.89), channel_id=1, source_target_pairs={{0,16},{16,0},{1,17},{17,1},{2,18},{18,2},{3,19},{19,3},{4,20},{20... | collective-permute-start | bytes 884744 | tf_op jit(solution)/shard_map/ppermute | solution.py:350
